TPU v7x, 32 devices: a whole 2x2x4 slice. The times are simulated.
32 devices in a mesh: dp: 8 (over z, x), shard: 4 (over y, core).
Axes of the slice: x: 2, y: 2, z: 4, core: 2. Of those that a mesh axis runs over, the one named last changes fastest.
Arguments:
- layer_input: bfloat16 [16384, 960], P(('dp', 'shard')), may hold values from -6 to 6
- cotangent: bfloat16 [16384, 960], P(('dp', 'shard')), may hold values from -6 to 6
- master_attention: float32 [2457600], P(('dp', 'shard'))
- master_feedforward: float32 [7372800], P(('dp', 'shard'))
- master_gains: float32 [1920], P(('dp', 'shard')), may hold values from 0.5 to 1.5
- first_attention: float32 [2457600], P(('dp', 'shard')), may hold values from -20 to 20
- second_attention: float32 [2457600], P(('dp', 'shard')), may hold values from 0.16384 to 4.9152
- first_feedforward: float32 [7372800], P(('dp', 'shard')), may hold values from -20 to 20
- second_feedforward: float32 [7372800], P(('dp', 'shard')), may hold values from 0.16384 to 4.9152
- first_gains: float32 [1920], P(('dp', 'shard')), may hold values from -20 to 20
- second_gains: float32 [1920], P(('dp', 'shard')), may hold values from 0.16384 to 4.9152
- block_start: int32 [128], P('dp'), may hold values from 0 to 15, as said below
- block_fill: int32 [128], P('dp'), may hold values from 0 to 128
Outputs:
- layer_output: float32 [16384, 960], P(('dp', 'shard'))
- input_gradient: float32 [16384, 960], P(('dp', 'shard'))
- attention_gradient: float32 [2457600], P(('dp', 'shard'))
- feedforward_gradient: float32 [7372800], P(('dp', 'shard'))
- gains_gradient: float32 [1920], P(('dp', 'shard'))
- attention_first: float32 [2457600], P(('dp', 'shard'))
- attention_second: float32 [2457600], P(('dp', 'shard'))
- feedforward_first: float32 [7372800], P(('dp', 'shard'))
- feedforward_second: float32 [7372800], P(('dp', 'shard'))
- gains_first: float32 [1920], P(('dp', 'shard'))
- gains_second: float32 [1920], P(('dp', 'shard'))
- attention_update: float32 [2457600], P(('dp', 'shard'))
- feedforward_update: float32 [7372800], P(('dp', 'shard'))
- gains_update: float32 [1920], P(('dp', 'shard'))
Inputs may be any that keep to these rules, and one draw needn't show every extreme that they name: Within each group of 16 blocks, block_start of a block is never above the block's own index and at most 15 below it; a sequence takes consecutive blocks that share block_start, all full but its last; padding blocks (fill 0, their own start) come after all live blocks of a group, of which there are 4 or more; some sequence has exactly 2048 tokens.
All inputs are finite; a program needn't handle non-finite values.
Results may differ from a plain program's by a relative error of at most 0.033.
Values may be sent and summed in bfloat16 or wider, within the bound.
No kernel may reach another device: no remote copies, remote signals or barrier semaphores. Data moves between devices by JAX's collectives and lax.ppermute only.
A program may use at most 448 MiB of HBM per device.

v0:
```python
import math

import jax
import jax.numpy as jnp
from jax import lax
from jax.sharding import PartitionSpec as P

MODEL_WIDTH = 960
QUERY_HEADS = 15
KEY_VALUE_HEADS = 5
HEAD_SIZE = 64
FF = 2560
BLK = 128
ADAM_STEP = 10
TOK_DEV = 512


epsilon = 1e-05
masked_value = -1e30
learning_rate = 0.03
weight_decay = 0.1


def rope_tables(positions):
    steps = jnp.arange(HEAD_SIZE // 2, dtype=jnp.float32) * (2.0 / HEAD_SIZE)
    inverse = jnp.exp(-math.log(10000.0) * steps)
    angles = positions.astype(jnp.float32)[:, None] * inverse[None, :]
    return (jnp.cos(angles), jnp.sin(angles))


def apply_rotation(field, cosine_table, sine_table, heads):
    rows = field.shape[0]
    shaped = field.reshape(rows, heads, HEAD_SIZE)
    front = shaped[:, :, : HEAD_SIZE // 2]
    back = shaped[:, :, HEAD_SIZE // 2 :]
    cosine_wide = cosine_table[:, None, :]
    sine_wide = sine_table[:, None, :]
    turned = jnp.concatenate(
        [front * cosine_wide - back * sine_wide, back * cosine_wide + front * sine_wide], axis=2
    )
    return turned.reshape(rows, heads * HEAD_SIZE)


def reverse_rotation(field, cosine_table, sine_table, heads):
    rows = field.shape[0]
    shaped = field.reshape(rows, heads, HEAD_SIZE)
    front = shaped[:, :, : HEAD_SIZE // 2]
    back = shaped[:, :, HEAD_SIZE // 2 :]
    cosine_wide = cosine_table[:, None, :]
    sine_wide = sine_table[:, None, :]
    turned = jnp.concatenate(
        [front * cosine_wide + back * sine_wide, back * cosine_wide - front * sine_wide], axis=2
    )
    return turned.reshape(rows, heads * HEAD_SIZE)


def norm_scale(field):
    return lax.rsqrt(jnp.mean(field * field, axis=1, keepdims=True) + epsilon)


def norm_back(upstream, normed, scale, gain):
    scaled = upstream * gain[None, :]
    return scale * (scaled - normed * jnp.mean(scaled * normed, axis=1, keepdims=True))


def adam_step(grad, moment, second, master):
    moment_new = 0.9 * moment + 0.1 * grad
    second_new = 0.999 * second + 0.001 * grad * grad
    corrected = moment_new / (1.0 - 0.9**ADAM_STEP)
    scaled = second_new / (1.0 - 0.999**ADAM_STEP)
    update = -learning_rate * (corrected / (jnp.sqrt(scaled) + 1e-08) + weight_decay * master)
    return (moment_new, second_new, update)


def local(
    layer_input,
    cotangent,
    master_attention,
    master_feedforward,
    master_gains,
    first_attention,
    second_attention,
    first_feedforward,
    second_feedforward,
    first_gains,
    second_gains,
    block_start,
    block_fill,
):
    attention_flat, feedforward_flat, gains_flat = (
        lax.all_gather(master_attention.astype(jnp.bfloat16), ("dp", "shard"), axis=0, tiled=True),
        lax.all_gather(
            master_feedforward.astype(jnp.bfloat16), ("dp", "shard"), axis=0, tiled=True
        ),
        lax.all_gather(master_gains.astype(jnp.bfloat16), ("dp", "shard"), axis=0, tiled=True),
    )
    query_width = QUERY_HEADS * HEAD_SIZE
    key_head_width = KEY_VALUE_HEADS * HEAD_SIZE
    grouped_rows = QUERY_HEADS // KEY_VALUE_HEADS
    sequence_span = grouped_rows * HEAD_SIZE
    score_scale = 1.0 / math.sqrt(HEAD_SIZE)
    edge_one = MODEL_WIDTH * query_width
    edge_two = edge_one + MODEL_WIDTH * key_head_width
    edge_three = edge_two + MODEL_WIDTH * key_head_width
    query_weight = attention_flat[:edge_one].reshape(MODEL_WIDTH, query_width)
    key_matrix = attention_flat[edge_one:edge_two].reshape(MODEL_WIDTH, key_head_width)
    value_weight = attention_flat[edge_two:edge_three].reshape(MODEL_WIDTH, key_head_width)
    out_weight = attention_flat[edge_three:].reshape(query_width, MODEL_WIDTH)
    gate_weight = feedforward_flat[: MODEL_WIDTH * FF].reshape(MODEL_WIDTH, FF)
    up_weight = feedforward_flat[MODEL_WIDTH * FF : 2 * MODEL_WIDTH * FF].reshape(MODEL_WIDTH, FF)
    down_weight = feedforward_flat[2 * MODEL_WIDTH * FF :].reshape(FF, MODEL_WIDTH)
    gain_one = gains_flat[:MODEL_WIDTH].astype(jnp.float32)
    gain_two = gains_flat[MODEL_WIDTH:].astype(jnp.float32)
    shard_count = lax.axis_size("shard")
    group_rows = shard_count * TOK_DEV
    first_row = lax.axis_index("shard") * TOK_DEV
    slots = jnp.arange(group_rows, dtype=jnp.int32)
    tags = jnp.repeat(block_start, BLK)
    live_all = slots % BLK < jnp.repeat(block_fill, BLK)
    local_slots = first_row + jnp.arange(TOK_DEV, dtype=jnp.int32)
    local_tags = lax.dynamic_slice_in_dim(tags, first_row, TOK_DEV)
    live_rows = lax.dynamic_slice_in_dim(live_all, first_row, TOK_DEV)
    allowed = (
        (local_tags[:, None] == tags[None, :])
        & (slots[None, :] <= local_slots[:, None])
        & (live_all[None, :] | (slots[None, :] == local_slots[:, None]))
    )
    cosine_table, sine_table = rope_tables(local_slots - local_tags * BLK)
    inputs = layer_input.astype(jnp.float32)
    scale_one = norm_scale(inputs)
    normed_one = inputs * scale_one
    first_hidden = (normed_one * gain_one[None, :]).astype(jnp.bfloat16)
    query_rows = apply_rotation(
        jnp.dot(first_hidden, query_weight, preferred_element_type=jnp.float32),
        cosine_table,
        sine_table,
        QUERY_HEADS,
    ).astype(jnp.bfloat16)
    key_rows = apply_rotation(
        jnp.dot(first_hidden, key_matrix, preferred_element_type=jnp.float32),
        cosine_table,
        sine_table,
        KEY_VALUE_HEADS,
    ).astype(jnp.bfloat16)
    value_rows = jnp.dot(first_hidden, value_weight, preferred_element_type=jnp.float32).astype(
        jnp.bfloat16
    )
    key_all, value_all = (
        lax.all_gather(key_rows, "shard", axis=0, tiled=True),
        lax.all_gather(value_rows, "shard", axis=0, tiled=True),
    )
    outputs = []
    log_totals = []
    for head_number in range(KEY_VALUE_HEADS):
        query_head = query_rows[
            :, head_number * sequence_span : (head_number + 1) * sequence_span
        ].reshape(TOK_DEV, grouped_rows, HEAD_SIZE)
        key_head = key_all[:, head_number * HEAD_SIZE : (head_number + 1) * HEAD_SIZE]
        value_head = value_all[:, head_number * HEAD_SIZE : (head_number + 1) * HEAD_SIZE]
        scores = (
            jnp.einsum("tgd,sd->gts", query_head, key_head, preferred_element_type=jnp.float32)
            * score_scale
        )
        masked = jnp.where(allowed[None, :, :], scores, masked_value)
        top = jnp.max(masked, axis=2, keepdims=True)
        exponent = jnp.exp(masked - top)
        total = jnp.sum(exponent, axis=2, keepdims=True)
        probs = (exponent / total).astype(jnp.bfloat16)
        outputs.append(
            jnp.einsum(
                "gts,sd->tgd", probs, value_head, preferred_element_type=jnp.float32
            ).reshape(TOK_DEV, sequence_span)
        )
        log_totals.append(top + jnp.log(total))
    mixed = jnp.concatenate(outputs, axis=1).astype(jnp.bfloat16)
    middle = inputs + jnp.dot(mixed, out_weight, preferred_element_type=jnp.float32)
    scale_two = norm_scale(middle)
    normed_two = middle * scale_two
    hidden_two = (normed_two * gain_two[None, :]).astype(jnp.bfloat16)
    gate = jnp.dot(hidden_two, gate_weight, preferred_element_type=jnp.float32)
    upper = jnp.dot(hidden_two, up_weight, preferred_element_type=jnp.float32)
    sigmoid_gate = jax.nn.sigmoid(gate)
    activated = gate * sigmoid_gate
    inner = (activated * upper).astype(jnp.bfloat16)
    layer_output = middle + jnp.dot(inner, down_weight, preferred_element_type=jnp.float32)
    grad_out = cotangent.astype(jnp.float32) * live_rows[:, None].astype(jnp.float32)
    grad_low = grad_out.astype(jnp.bfloat16)
    d_down_weight = jnp.einsum("tf,td->fd", inner, grad_low, preferred_element_type=jnp.float32)
    d_inner = jnp.einsum("td,fd->tf", grad_low, down_weight, preferred_element_type=jnp.float32)
    d_gate = (d_inner * upper * sigmoid_gate * (1.0 + gate * (1.0 - sigmoid_gate))).astype(
        jnp.bfloat16
    )
    d_upper = (d_inner * activated).astype(jnp.bfloat16)
    d_gate_weight = jnp.einsum("td,tf->df", hidden_two, d_gate, preferred_element_type=jnp.float32)
    d_up_weight = jnp.einsum("td,tf->df", hidden_two, d_upper, preferred_element_type=jnp.float32)
    d_hidden_two = jnp.einsum(
        "tf,df->td", d_gate, gate_weight, preferred_element_type=jnp.float32
    ) + jnp.einsum("tf,df->td", d_upper, up_weight, preferred_element_type=jnp.float32)
    d_gain_two = jnp.sum(d_hidden_two * normed_two, axis=0)
    d_middle = grad_out + norm_back(d_hidden_two, normed_two, scale_two, gain_two)
    feedforward_terms = jnp.concatenate(
        [d_gate_weight.reshape(-1), d_up_weight.reshape(-1), d_down_weight.reshape(-1)]
    )
    d_branch = d_middle.astype(jnp.bfloat16)
    d_out_weight = jnp.einsum("tq,td->qd", mixed, d_branch, preferred_element_type=jnp.float32)
    d_mixed = jnp.einsum(
        "td,qd->tq", d_branch, out_weight, preferred_element_type=jnp.float32
    ).astype(jnp.bfloat16)
    query_grads = []
    key_grads = []
    value_grads = []
    for head_number in range(KEY_VALUE_HEADS):
        query_head = query_rows[
            :, head_number * sequence_span : (head_number + 1) * sequence_span
        ].reshape(TOK_DEV, grouped_rows, HEAD_SIZE)
        key_head = key_all[:, head_number * HEAD_SIZE : (head_number + 1) * HEAD_SIZE]
        value_head = value_all[:, head_number * HEAD_SIZE : (head_number + 1) * HEAD_SIZE]
        upstream = d_mixed[
            :, head_number * sequence_span : (head_number + 1) * sequence_span
        ].reshape(TOK_DEV, grouped_rows, HEAD_SIZE)
        scores = (
            jnp.einsum("tgd,sd->gts", query_head, key_head, preferred_element_type=jnp.float32)
            * score_scale
        )
        masked = jnp.where(allowed[None, :, :], scores, masked_value)
        probs = jnp.exp(masked - log_totals[head_number])
        d_probs = jnp.einsum(
            "tgd,sd->gts", upstream, value_head, preferred_element_type=jnp.float32
        )
        delta = jnp.sum(probs * d_probs, axis=2, keepdims=True)
        d_scores = (probs * (d_probs - delta)).astype(jnp.bfloat16)
        query_grads.append(
            (
                jnp.einsum("gts,sd->tgd", d_scores, key_head, preferred_element_type=jnp.float32)
                * score_scale
            ).reshape(TOK_DEV, sequence_span)
        )
        key_grads.append(
            jnp.einsum("gts,tgd->sd", d_scores, query_head, preferred_element_type=jnp.float32)
            * score_scale
        )
        value_grads.append(
            jnp.einsum(
                "gts,tgd->sd",
                probs.astype(jnp.bfloat16),
                upstream,
                preferred_element_type=jnp.float32,
            )
        )
    group_terms = jnp.concatenate(key_grads + value_grads, axis=1)
    shard_terms = lax.psum_scatter(
        group_terms.astype(jnp.bfloat16), "shard", scatter_dimension=0, tiled=True
    ).astype(jnp.float32)
    key_gradient = reverse_rotation(
        shard_terms[:, :key_head_width], cosine_table, sine_table, KEY_VALUE_HEADS
    ).astype(jnp.bfloat16)
    d_value = shard_terms[:, key_head_width:].astype(jnp.bfloat16)
    d_query = reverse_rotation(
        jnp.concatenate(query_grads, axis=1), cosine_table, sine_table, QUERY_HEADS
    ).astype(jnp.bfloat16)
    d_query_weight = jnp.einsum(
        "td,tq->dq", first_hidden, d_query, preferred_element_type=jnp.float32
    )
    d_key_weight = jnp.einsum(
        "td,tk->dk", first_hidden, key_gradient, preferred_element_type=jnp.float32
    )
    d_value_weight = jnp.einsum(
        "td,tk->dk", first_hidden, d_value, preferred_element_type=jnp.float32
    )
    d_hidden_one = jnp.einsum(
        "tq,dq->td", d_query, query_weight, preferred_element_type=jnp.float32
    )
    d_hidden_one = d_hidden_one + jnp.einsum(
        "tk,dk->td", key_gradient, key_matrix, preferred_element_type=jnp.float32
    )
    d_hidden_one = d_hidden_one + jnp.einsum(
        "tk,dk->td", d_value, value_weight, preferred_element_type=jnp.float32
    )
    d_gain_one = jnp.sum(d_hidden_one * normed_one, axis=0)
    input_gradient = d_middle + norm_back(d_hidden_one, normed_one, scale_one, gain_one)
    attention_terms = jnp.concatenate(
        [
            d_query_weight.reshape(-1),
            d_key_weight.reshape(-1),
            d_value_weight.reshape(-1),
            d_out_weight.reshape(-1),
        ]
    )
    gains_terms = jnp.concatenate([d_gain_one, d_gain_two])
    attention_gradient, feedforward_gradient, gains_gradient = (
        lax.psum_scatter(attention_terms, ("dp", "shard"), scatter_dimension=0, tiled=True),
        lax.psum_scatter(feedforward_terms, ("dp", "shard"), scatter_dimension=0, tiled=True),
        lax.psum_scatter(gains_terms, ("dp", "shard"), scatter_dimension=0, tiled=True),
    )
    attention_first, attention_second, attention_update = adam_step(
        attention_gradient, first_attention, second_attention, master_attention
    )
    feedforward_first, feedforward_second, feedforward_update = adam_step(
        feedforward_gradient, first_feedforward, second_feedforward, master_feedforward
    )
    gains_first, gains_second, gains_update = adam_step(
        gains_gradient, first_gains, second_gains, master_gains
    )
    return (
        layer_output,
        input_gradient,
        attention_gradient,
        feedforward_gradient,
        gains_gradient,
        attention_first,
        attention_second,
        feedforward_first,
        feedforward_second,
        gains_first,
        gains_second,
        attention_update,
        feedforward_update,
        gains_update,
    )


def solution(mesh):
    return jax.shard_map(
        local,
        mesh=mesh,
        in_specs=(
            P(("dp", "shard"), None),
            P(("dp", "shard"), None),
            P(("dp", "shard")),
            P(("dp", "shard")),
            P(("dp", "shard")),
            P(("dp", "shard")),
            P(("dp", "shard")),
            P(("dp", "shard")),
            P(("dp", "shard")),
            P(("dp", "shard")),
            P(("dp", "shard")),
            P("dp"),
            P("dp"),
        ),
        out_specs=(
            P(("dp", "shard"), None),
            P(("dp", "shard"), None),
            P(("dp", "shard")),
            P(("dp", "shard")),
            P(("dp", "shard")),
            P(("dp", "shard")),
            P(("dp", "shard")),
            P(("dp", "shard")),
            P(("dp", "shard")),
            P(("dp", "shard")),
            P(("dp", "shard")),
            P(("dp", "shard")),
            P(("dp", "shard")),
            P(("dp", "shard")),
        ),
        check_vma=False,
    )
```

profile of v0, /device:TPU:0, one launch (start us, length us, event | category | flops | bytes accessed | tf_op | source)
XLA Modules:
  0.0 1156.1 jit_solution(1588537911075840645)
XLA Ops:
  9.9 42.9 %all-reduce = bf16[1920]{0:T(1024)(128)(2,1)S(1)} all-reduce(bf16[1920]{0:T(1024)(128)(2,1)S(1)} %dynamic-update-slice), channel_id=1, replica_groups=mesh['dp'=8,'shard'=4] {'dp','shard'}, use_global_device_ids=true, to_apply=%add | all-reduce | flops 1920 | bytes 7680
  54.9 23.7 %all-gather.5.cloned.1.call-done = bf16[2457600]{0:T(1024)(128)(2,1)} async-done(((bf16[76800]{0:T(1024)(128)(2,1)}), bf16[2457600]{0:T(1024)(128)(2,1)}) %all-gather.5.cloned.1.call-update) | async-done | bytes 4915216 | tf_op jit(solution)/shard_map/all_gather | solution.py:91
  169.6 58.3 %all-gather.11.cloned.1.call-done = bf16[7372800]{0:T(1024)(128)(2,1)} async-done(((bf16[230400]{0:T(1024)(128)(2,1)}), bf16[7372800]{0:T(1024)(128)(2,1)}) %all-gather.11.cloned.1.call-update) | async-done | bytes 14745616 | tf_op jit(solution)/shard_map/all_gather | solution.py:92
  228.0 11.3 fusion.173
  239.2 10.0 slice.234
  249.2 10.0 slice.236
  271.0 9.6 slice.238
  280.6 10.7 multiply_convert_fusion
  317.6 10.4 fusion.14
  339.7 9.0 fusion.11
  353.5 8.7 fusion.6
  362.2 12.3 %fusion.8 = bf16[3,512,2048]{1,2,0:T(8,128)(2,1)} fusion(f32[2048,512,3]{1,0,2:T(8,128)} %get-tuple-element.84, f32[3,512,2048]{1,2,0:T(8,128)} %copy-done.4, f32[3,512]{1,0:T(4,128)S(1)} %get-tuple-element.83, f32[3,512]{1,0:T(4,128)S(1)} %log_add_fusion.2), kind=kLoop, calls=%fused_computation.15 | loop fusion | flops 12582912 | bytes 31469568 | tf_op jit(solution)/shard_map/convert_element_type | solution.py:231
  379.4 8.7 fusion.3
  388.1 12.3 %fusion.5 = bf16[3,512,2048]{1,2,0:T(8,128)(2,1)} fusion(f32[2048,512,3]{1,0,2:T(8,128)} %get-tuple-element.86, f32[3,512,2048]{1,2,0:T(8,128)} %copy-done.5, f32[3,512]{1,0:T(4,128)S(1)} %get-tuple-element.85, f32[3,512]{1,0:T(4,128)S(1)} %log_add_fusion.1), kind=kLoop, calls=%fused_computation.10 | loop fusion | flops 12582912 | bytes 31469568 | tf_op jit(solution)/shard_map/convert_element_type | solution.py:231
  405.3 8.6 fusion
  413.8 12.5 %fusion.2 = bf16[3,512,2048]{1,2,0:T(8,128)(2,1)} fusion(f32[2048,512,3]{1,0,2:T(8,128)} %get-tuple-element.88, f32[3,512,2048]{1,2,0:T(8,128)} %copy-done.6, f32[3,512]{1,0:T(4,128)S(1)} %get-tuple-element.87, f32[3,512]{1,0:T(4,128)S(1)} %copy-done.52), kind=kLoop, calls=%fused_computation.5 | loop fusion | flops 12582912 | bytes 31469568 | tf_op jit(solution)/shard_map/convert_element_type | solution.py:231
  448.9 9.2 fusion.141
  458.1 13.5 %reshape.468 = f32[2457600]{0:T(1024)} reshape(f32[2560,960]{1,0:T(8,128)} %fusion.141) | data formatting | bytes 19660800 | tf_op jit(solution)/shard_map/reshape | solution.py:202
  471.6 11.0 reshape.467
  482.5 11.0 reshape.466
  493.6 25.3 %pad_maximum_fusion = f32[7372800]{0:T(1024)} fusion(f32[2457600]{0:T(1024)} %reshape.468, f32[2457600]{0:T(1024)} %reshape.467, f32[2457600]{0:T(1024)} %reshape.466), kind=kLoop, calls=%fused_computation | loop fusion | flops 14745600 | bytes 58982400 | tf_op jit(solution)/shard_map/concatenate | solution.py:201
  559.9 11.0 pad_maximum_fusion.1
  585.4 39.8 %all-reduce.3 = f32[1920]{0:T(1024)S(1)} all-reduce(f32[1920]{0:T(1024)S(1)} %pad_maximum_fusion.6), channel_id=5, replica_groups=mesh['dp'=8,'shard'=4] {'dp','shard'}, use_global_device_ids=true, to_apply=%region_24.25.clone | all-reduce | flops 1920 | bytes 15360
  629.5 513.3 %all-reduce.7.cloned.1.call-done = (f32[2457600]{0:T(1024)}, f32[7372800]{0:T(1024)}) async-done(((f32[2457600]{0:T(1024)}, f32[7372800]{0:T(1024)}), (f32[2457600]{0:T(1024)}, f32[7372800]{0:T(1024)})) %all-reduce.7.cloned.1.call-update) | async-done | bytes 39321616
  (312 shorter events, 247.5 us)
Async XLA Ops:
  7.2 45.7 %copy-start = (s32[16]{0:T(128)S(1)}, s32[16]{0:T(128)}, u32[]{:S(2)}) copy-start(s32[16]{0:T(128)} %param.24) | copy-start | bytes 196
  7.2 74.5 %copy-start.11 = (bf16[512,960]{0,1:T(8,128)(2,1)S(1)}, bf16[512,960]{0,1:T(8,128)(2,1)}, u32[]{:S(2)}) copy-start(bf16[512,960]{0,1:T(8,128)(2,1)} %param.13) | copy-start | bytes 2949124
  7.2 71.4 %all-gather.5.cloned.1.call-start = ((), (), s32[]{:S(2)}) async-start(), calls=%async_computation.1 | async-start | bytes 5068800 | tf_op jit(solution)/shard_map/all_gather | solution.py:91
  9.0 100.5 %all-gather.9.cloned.1.call-start = ((), (), s32[]{:S(2)}) async-start(), calls=%async_computation.3 | async-start | bytes 1638400 | tf_op jit(solution)/shard_map/all_gather | solution.py:149
  54.5 50.9 %copy-start.55 = (f32[512]{0:T(512)}, f32[512]{0:T(512)S(1)}, u32[]{:S(2)}) copy-start(f32[512]{0:T(512)S(1)} %add_rsqrt_fusion.1) | copy-start | bytes 6148
  54.6 50.9 %copy-start.53 = (f32[960]{0:T(1024)}, f32[960]{0:T(1024)S(1)}, u32[]{:S(2)}) copy-start(f32[960]{0:T(1024)S(1)} %get-tuple-element.63) | copy-start | bytes 11524
  54.9 53.4 %copy-start.27 = (f32[512,32]{0,1:T(8,128)}, f32[512,32]{0,1:T(8,128)S(1)}, u32[]{:S(2)}) copy-start(f32[512,32]{0,1:T(8,128)S(1)} %get-tuple-element.64) | copy-start | bytes 196612
  54.9 53.4 %copy-start.29 = (f32[512,32]{0,1:T(8,128)}, f32[512,32]{0,1:T(8,128)S(1)}, u32[]{:S(2)}) copy-start(f32[512,32]{0,1:T(8,128)S(1)} %get-tuple-element.65) | copy-start | bytes 196612
  83.2 36.5 %all-gather.7.cloned.1.call-start = ((), (), s32[]{:S(2)}) async-start(), calls=%async_computation.2 | async-start | bytes 1638400 | tf_op jit(solution)/shard_map/all_gather | solution.py:150
  86.6 141.4 %all-gather.11.cloned.1.call-start = ((), (), s32[]{:S(2)}) async-start(), calls=%async_computation.4 | async-start | bytes 15206400 | tf_op jit(solution)/shard_map/all_gather | solution.py:92
  87.5 461.4 %reduce-scatter.2.cloned.1.call-start = ((), (), s32[]{:S(2)}) async-start(), calls=%async_computation.5 | async-start | bytes 3276800 | tf_op jit(solution)/shard_map/reduce_scatter | solution.py:251
  109.5 17.3 %copy-start.47 = (bf16[512,192]{0,1:T(8,128)(2,1)}, bf16[512,192]{0,1:T(8,128)(2,1)S(1)}, u32[]{:S(2)}) copy-start(bf16[512,192]{0,1:T(8,128)(2,1)S(1)} %get-tuple-element.56) | copy-start | bytes 589828
  109.5 37.7 %copy-start.43 = (bf16[512,192]{0,1:T(8,128)(2,1)}, bf16[512,192]{0,1:T(8,128)(2,1)S(1)}, u32[]{:S(2)}) copy-start(bf16[512,192]{0,1:T(8,128)(2,1)S(1)} %get-tuple-element.54) | copy-start | bytes 589828
  109.5 47.8 %copy-start.41 = (bf16[512,192]{0,1:T(8,128)(2,1)}, bf16[512,192]{0,1:T(8,128)(2,1)S(1)}, u32[]{:S(2)}) copy-start(bf16[512,192]{0,1:T(8,128)(2,1)S(1)} %get-tuple-element.53) | copy-start | bytes 589828
  271.0 20.3 %slice-start.22 = ((s8[4915200]{0:T(1024)(128)(4,1)}), s8[720896]{0:T(1024)(128)(4,1)S(1)}, s32[]{:S(2)}) async-start(s8[4915200]{0:T(1024)(128)(4,1)} %bitcast.327), calls=%async_computation.29 | async-start | bytes 1441792
  448.9 694.0 %all-reduce.7.cloned.1.call-start = ((), (), s32[]{:S(2)}) async-start(), calls=%async_computation.6 | async-start | bytes 78643200
  493.6 25.3 %copy-start.9 = (f32[512,960]{0,1:T(8,128)S(1)}, f32[512,960]{0,1:T(8,128)}, u32[]{:S(2)}) copy-start(f32[512,960]{0,1:T(8,128)} %copy-done.8) | copy-start | bytes 5898244
  493.6 25.3 %copy-start.20 = (bf16[512,960]{0,1:T(8,128)(2,1)S(1)}, bf16[512,960]{0,1:T(8,128)(2,1)}, u32[]{:S(2)}) copy-start(bf16[512,960]{0,1:T(8,128)(2,1)} %copy-done.19) | copy-start | bytes 2949124
  582.2 42.9 %copy-start.60 = (f32[60]{0:T(128)S(1)}, f32[60]{0:T(128)}, u32[]{:S(2)}) copy-start(f32[60]{0:T(128)} %param.17) | copy-start | bytes 724
  582.2 42.9 %copy-start.61 = (f32[60]{0:T(128)S(1)}, f32[60]{0:T(128)}, u32[]{:S(2)}) copy-start(f32[60]{0:T(128)} %param.23) | copy-start | bytes 724
  582.2 42.9 %copy-start.62 = (f32[60]{0:T(128)S(1)}, f32[60]{0:T(128)}, u32[]{:S(2)}) copy-start(f32[60]{0:T(128)} %param.22) | copy-start | bytes 724
  582.2 43.5 %copy-start.10 = (f32[512,960]{0,1:T(8,128)S(1)}, f32[512,960]{0,1:T(8,128)}, u32[]{:S(2)}) copy-start(f32[512,960]{0,1:T(8,128)} %copy-done.8) | copy-start | bytes 5898244
  585.3 557.5 %copy-start.34 = (f32[76800]{0:T(1024)S(1)}, f32[76800]{0:T(1024)}, u32[]{:S(2)}) copy-start(f32[76800]{0:T(1024)} %param.15) | copy-start | bytes 921604
  625.8 523.3 %copy-start.1 = (s32[16]{0:T(128)S(1)}, s32[16]{0:T(128)}, u32[]{:S(2)}) copy-start(s32[16]{0:T(128)} %param.24) | copy-start | bytes 196
  (70 other events, 413.1 us)
Sparse Core Ops, SparseCore 0:
  11.4 67.1 all-gather.4
  83.3 16.4 all-gather.8
  101.4 18.1 all-gather.6
  122.9 105.0 all-gather.10
  449.0 32.7 reduce-scatter.1
  571.1 571.6 all-reduce.6
where the time goes:
time: 1160 us
  waiting for transfers between devices  595 us (51%)
  matrix products  201 us (17%)
  local copies, waits for them, and re-layouts  137 us (12%)
  other arithmetic  124 us (11%)
  blocking collectives  82.7 us (7%)
  between operations  15.4 us (1%)
    unnamed x7, waiting for transfers between devices  513 us
    unnamed x2, blocking collectives  82.7 us
    all_gather x1, waiting for transfers between devices, local(): lax.all_gather(master_feedforward.astype(jnp.bfloat16), ('dp', 'shard'),...  58.3 us
    convert_element_type x5, other arithmetic, local(): d_scores = (probs * (d_probs - delta)).astype(jnp.bfloat16)  56.6 us
    dot_general x5, matrix products, local(): jnp.einsum('tgd,sd->gts', upstream, value_head, preferred_element_type=jn...  38.7 us
    concatenate x1, other arithmetic, local(): jnp.concatenate([d_gate_weight.reshape(-1), d_up_weight.reshape(-1), d_do...  25.3 us
    dot_general x5, matrix products, local(): jnp.einsum('gts,tgd->sd', d_scores, query_head, preferred_element_type=jn...  23.9 us
    all_gather x1, waiting for transfers between devices, local(): lax.all_gather(master_attention.astype(jnp.bfloat16), ('dp', 'shard'), ax...  23.7 us
  transfers between devices with their start and end apart: 6, of which 3 were waited for; matrix products, arithmetic and copies ran while one was open for 16% of the time, Pallas kernels for 0%

commit v1 on v0

v1 whole, which is shorter than its diff:
```python
import functools
import math

import jax
import jax.numpy as jnp
from jax import lax
from jax.experimental import pallas as pl
from jax.experimental.pallas import tpu as pltpu
from jax.sharding import PartitionSpec as P

MODEL_WIDTH = 960
QUERY_HEADS = 15
KEY_VALUE_HEADS = 5
GROUPED = QUERY_HEADS // KEY_VALUE_HEADS
HEAD_SIZE = 64
FF = 2560
BLK = 128
ADAM_STEP = 10
TOK_DEV = 512
KV_WIDTH = KEY_VALUE_HEADS * HEAD_SIZE
TILE = 256
WIDE = GROUPED * BLK
UNITS = 32
LINES = 600
GAIN_LINES = 8
ALL_AXES = ("dp", "shard")

epsilon = 1e-05
masked_value = -1e30
learning_rate = 0.03
weight_decay = 0.1
score_scale = 1.0 / math.sqrt(HEAD_SIZE)
f32 = jnp.float32
bf16 = jnp.bfloat16


def lines_to_rows_2560(scratch, base, rows, store):
    for c in range(20):
        store(c, scratch[pl.ds(base + c, rows, stride=20), :])


def rows_to_lines_2560(load, scratch, base, rows):
    for c in range(20):
        scratch[pl.ds(base + c, rows, stride=20), :] = load(c)


def lane_low(rows):
    return lax.broadcasted_iota(jnp.int32, (rows, 128), 1) < 64


def lines_to_rows_960(scratch, base, rows, mid, store):
    half = rows // 2
    low = lane_low(half)
    line = [scratch[pl.ds(base + k, half, stride=15), :] for k in range(15)]
    turned = [None] * 7 + [pltpu.roll(line[k], 64, 1) for k in range(7, 15)]
    for c in range(8):
        mid[pl.ds(0, half, stride=2), :] = line[c]
        odd = jnp.where(low, turned[7 + c], turned[8 + c]) if c < 7 else turned[14]
        mid[pl.ds(1, half, stride=2), :] = odd
        store(c, mid[pl.ds(0, rows), :])


def rows_to_lines_960(load, scratch, base, rows, mid):
    half = rows // 2
    low = lane_low(half)
    odds = []
    for c in range(8):
        mid[pl.ds(0, rows), :] = load(c)
        even = mid[pl.ds(0, half, stride=2), :]
        odd = pltpu.roll(mid[pl.ds(1, half, stride=2), :], 64, 1)
        odds.append(odd)
        if c < 7:
            scratch[pl.ds(base + c, half, stride=15), :] = even
        else:
            scratch[pl.ds(base + 7, half, stride=15), :] = jnp.where(low, even, odds[0])
        if c > 0:
            scratch[pl.ds(base + 7 + c, half, stride=15), :] = jnp.where(low, odds[c - 1], odd)


def half_chunks(lines):
    even = [(lines[0], 0), (lines[0], 1), (lines[1], 0), (lines[1], 1), (lines[2], 0)]
    odd = [(lines[2], 1), (lines[3], 0), (lines[3], 1), (lines[4], 0), (lines[4], 1)]
    return even, odd


def placed(chunk, upper):
    line, side = chunk
    return line if side == upper else pltpu.roll(line, 64, 1)


def unpack_ff_kernel(lines_ref, gate_ref, up_ref, down_ref, scratch, mid):
    phase = pl.program_id(0)
    scratch[...] = lines_ref[...].astype(f32)
    for number, out in ((0, gate_ref), (1, up_ref)):

        @pl.when(phase == number)
        def _():
            def store(c, value):
                out[:, 128 * c : 128 * c + 128] = value.astype(bf16)

            lines_to_rows_2560(scratch, 0, 96, store)

    @pl.when(phase == 2)
    def _():
        def store(c, value):
            if c < 7:
                down_ref[:, 128 * c : 128 * c + 128] = value.astype(bf16)
            else:
                down_ref[:, 896:960] = value[:, :64].astype(bf16)

        lines_to_rows_960(scratch, 0, 256, mid, store)


def pinned(phase):
    def index(p, j):
        return (jnp.where(p == phase, j, jnp.where(p < phase, 0, 9)), 0)

    return index


def unpack_ff(lines):
    return pl.pallas_call(
        unpack_ff_kernel,
        grid=(3, 10),
        in_specs=[pl.BlockSpec((1920, 128), lambda p, j: (p * 10 + j, 0))],
        out_specs=[
            pl.BlockSpec((96, FF), pinned(0)),
            pl.BlockSpec((96, FF), pinned(1)),
            pl.BlockSpec((256, MODEL_WIDTH), pinned(2)),
        ],
        out_shape=[
            jax.ShapeDtypeStruct((MODEL_WIDTH, FF), bf16),
            jax.ShapeDtypeStruct((MODEL_WIDTH, FF), bf16),
            jax.ShapeDtypeStruct((FF, MODEL_WIDTH), bf16),
        ],
        scratch_shapes=[pltpu.VMEM((1920, 128), f32), pltpu.VMEM((256, 128), f32)],
        name="unpack_feedforward",
    )(lines)


def pack_ff_kernel(gate_ref, up_ref, down_ref, lines_ref, scratch, mid):
    phase = pl.program_id(0)
    for number, source in ((0, gate_ref), (1, up_ref)):

        @pl.when(phase == number)
        def _():
            rows_to_lines_2560(
                lambda c: source[:, 128 * c : 128 * c + 128].astype(f32), scratch, 0, 96
            )

    @pl.when(phase == 2)
    def _():
        def load(c):
            if c < 7:
                return down_ref[:, 128 * c : 128 * c + 128].astype(f32)
            tail = down_ref[:, 896:960].astype(f32)
            return jnp.concatenate([tail, tail], axis=1)

        rows_to_lines_960(load, scratch, 0, 256, mid)

    lines_ref[...] = scratch[...].astype(bf16)


def pack_ff(gate, up, down):
    return pl.pallas_call(
        pack_ff_kernel,
        grid=(3, 10),
        in_specs=[
            pl.BlockSpec((96, FF), pinned(0)),
            pl.BlockSpec((96, FF), pinned(1)),
            pl.BlockSpec((256, MODEL_WIDTH), pinned(2)),
        ],
        out_specs=pl.BlockSpec((1920, 128), lambda p, j: (p * 10 + j, 0)),
        out_shape=jax.ShapeDtypeStruct((3 * 19200, 128), bf16),
        scratch_shapes=[pltpu.VMEM((1920, 128), f32), pltpu.VMEM((256, 128), f32)],
        name="pack_feedforward",
    )(gate, up, down)


def unpack_wide_kernel(lines_ref, out_ref, scratch, mid):
    for u in range(4):
        scratch[...] = lines_ref[u].astype(f32)
        base = u * 80

        def store(c, value):
            if c < 7:
                out_ref[base : base + 80, 128 * c : 128 * c + 128] = value.astype(bf16)
            else:
                out_ref[base : base + 80, 896:960] = value[:, :64].astype(bf16)

        lines_to_rows_960(scratch, 0, 80, mid, store)


def unpack_wide(lines, first):
    depth = lines.shape[1]
    return pl.pallas_call(
        unpack_wide_kernel,
        grid=(3,),
        in_specs=[pl.BlockSpec((4, depth, 128), lambda j: (first // 4 + j, 0, 0))],
        out_specs=pl.BlockSpec((320, MODEL_WIDTH), lambda j: (j, 0)),
        out_shape=jax.ShapeDtypeStruct((MODEL_WIDTH, MODEL_WIDTH), bf16),
        scratch_shapes=[pltpu.VMEM((depth, 128), f32), pltpu.VMEM((80, 128), f32)],
        name="unpack_attention",
    )(lines)


def unpack_kv_kernel(key_ref, value_ref, out_ref, key_lines, value_lines, mid):
    low = lane_low(120)
    key_lines[...] = key_ref[0].astype(f32)
    value_lines[...] = value_ref[0].astype(f32)
    keys = half_chunks([key_lines[pl.ds(k, 120, stride=5), :] for k in range(5)])
    values = half_chunks([value_lines[pl.ds(k, 120, stride=5), :] for k in range(5)])
    for h in range(KEY_VALUE_HEADS):
        for parity in range(2):
            mid[pl.ds(parity, 120, stride=2), :] = jnp.where(
                low, placed(keys[parity][h], 0), placed(values[parity][h], 1)
            )
        out_ref[:, 128 * h : 128 * h + 128] = mid[...].astype(bf16)


def unpack_kv(lines):
    depth = lines.shape[1]
    return pl.pallas_call(
        unpack_kv_kernel,
        grid=(4,),
        in_specs=[
            pl.BlockSpec((1, depth, 128), lambda j: (12 + j, 0, 0)),
            pl.BlockSpec((1, depth, 128), lambda j: (16 + j, 0, 0)),
        ],
        out_specs=pl.BlockSpec((240, 2 * KV_WIDTH), lambda j: (j, 0)),
        out_shape=jax.ShapeDtypeStruct((MODEL_WIDTH, 2 * KV_WIDTH), bf16),
        scratch_shapes=[
            pltpu.VMEM((depth, 128), f32),
            pltpu.VMEM((depth, 128), f32),
            pltpu.VMEM((240, 128), f32),
        ],
        name="unpack_key_value",
    )(lines, lines)


def pack_attention_kernel(query_ref, kv_ref, out_weight_ref, gains_ref, lines_ref, scratch, mid):
    step = pl.program_id(0)

    def wide(source):
        for u in range(4):
            base = u * 80

            def load(c):
                if c < 7:
                    return source[base : base + 80, 128 * c : 128 * c + 128].astype(f32)
                tail = source[base : base + 80, 896:960].astype(f32)
                return jnp.concatenate([tail, tail], axis=1)

            rows_to_lines_960(load, scratch, 0, 80, mid)
            lines_ref[u, :LINES, :] = scratch[...].astype(bf16)

    @pl.when(step < 3)
    def _():
        wide(query_ref)

    @pl.when(step >= 5)
    def _():
        wide(out_weight_ref)

    for number, upper in ((3, 0), (4, 1)):

        @pl.when(step == number)
        def _():
            low = lane_low(120)
            for u in range(4):
                evens, odds = [], []
                for h in range(KEY_VALUE_HEADS):
                    mid[...] = kv_ref[
                        240 * u : 240 * u + 240, 128 * h : 128 * h + 128
                    ].astype(f32)
                    evens.append((mid[pl.ds(0, 120, stride=2), :], upper))
                    odds.append((mid[pl.ds(1, 120, stride=2), :], upper))
                run = evens + odds
                for k in range(5):
                    scratch[pl.ds(k, 120, stride=5), :] = jnp.where(
                        low, placed(run[2 * k], 0), placed(run[2 * k + 1], 1)
                    )
                lines_ref[u, :LINES, :] = scratch[...].astype(bf16)

    for u in range(4):
        lines_ref[u, LINES:, :] = gains_ref[u]


def pack_attention(d_query, d_kv, d_out, gains):
    return pl.pallas_call(
        pack_attention_kernel,
        grid=(8,),
        in_specs=[
            pl.BlockSpec((320, MODEL_WIDTH), lambda s: (jnp.minimum(s, 2), 0)),
            pl.BlockSpec((MODEL_WIDTH, 2 * KV_WIDTH), lambda s: (0, 0)),
            pl.BlockSpec((320, MODEL_WIDTH), lambda s: (jnp.maximum(s - 5, 0), 0)),
            pl.BlockSpec((4, GAIN_LINES, 128), lambda s: (s, 0, 0)),
        ],
        out_specs=pl.BlockSpec((4, LINES + GAIN_LINES, 128), lambda s: (s, 0, 0)),
        out_shape=jax.ShapeDtypeStruct((UNITS, LINES + GAIN_LINES, 128), bf16),
        scratch_shapes=[pltpu.VMEM((LINES, 128), f32), pltpu.VMEM((240, 128), f32)],
        name="pack_attention",
    )(d_query, d_kv, d_out, gains)


def tile_range(starts_ref, fills_ref, block):
    first_slot = starts_ref[block] * BLK
    last_slot = block * BLK + fills_ref[block]
    tile_first = first_slot // TILE
    tile_last = (block * BLK) // TILE
    ragged_first = jnp.logical_and(first_slot % TILE != 0, tile_first < tile_last)
    return first_slot, last_slot, tile_first, tile_last, ragged_first.astype(jnp.int32)


def allowed_pairs(tile, block, first_slot, last_slot):
    key_slot = tile * TILE + lax.broadcasted_iota(jnp.int32, (TILE, WIDE), 0)
    lane = lax.broadcasted_iota(jnp.int32, (TILE, WIDE), 1)
    query_slot = block * BLK + lax.rem(lane, BLK)
    return jnp.logical_and(
        jnp.logical_and(key_slot >= first_slot, key_slot <= query_slot),
        jnp.logical_or(key_slot < last_slot, key_slot == query_slot),
    )


def over_tiles(span, block, step):
    first_slot, last_slot, tile_first, tile_last, ragged = span

    def masked(tile):
        step(tile, allowed_pairs(tile, block, first_slot, last_slot))

    def edge(k, carry):
        masked(jnp.where(k == ragged, tile_last, tile_first))
        return carry

    lax.fori_loop(0, 1 + ragged, edge, 0)

    def inner(tile, carry):
        step(tile, None)
        return carry

    lax.fori_loop(tile_first + ragged, tile_last, inner, 0)


def transpose_kv(kv_ref, turned, tiles):
    def body(t, carry):
        rows = pl.ds(pl.multiple_of(t * TILE, TILE), TILE)
        for h in range(KEY_VALUE_HEADS):
            turned[t, 128 * h : 128 * h + 128, :] = kv_ref[rows, 128 * h : 128 * h + 128].T
        return carry

    lax.fori_loop(0, tiles, body, 0)


def heads_beside(ref, h):
    return jnp.concatenate(
        [
            ref[HEAD_SIZE * (GROUPED * h + g) : HEAD_SIZE * (GROUPED * h + g + 1), :]
            for g in range(GROUPED)
        ],
        axis=1,
    )


def attention_forward_kernel(
    starts_ref, fills_ref, place_ref, query_ref, kv_ref, mixed_ref, log_ref, turned, pairs, tops, totals, sums
):
    i = pl.program_id(0)
    block = place_ref[0] * (TOK_DEV // BLK) + i

    @pl.when(i == 0)
    def _():
        transpose_kv(kv_ref, turned, kv_ref.shape[0] // TILE)

    for h in range(KEY_VALUE_HEADS):
        pairs[h, :HEAD_SIZE, :] = heads_beside(query_ref, h)
        pairs[h, HEAD_SIZE:, :] = jnp.zeros((HEAD_SIZE, WIDE), bf16)
    tops[...] = jnp.full(tops.shape, masked_value, f32)
    totals[...] = jnp.zeros(totals.shape, f32)
    sums[...] = jnp.zeros(sums.shape, f32)

    def step(tile, allowed):
        rows = pl.ds(pl.multiple_of(tile * TILE, TILE), TILE)
        for h in range(KEY_VALUE_HEADS):
            scores = jnp.dot(
                kv_ref[rows, 128 * h : 128 * h + 128], pairs[h], preferred_element_type=f32
            )
            if allowed is not None:
                scores = jnp.where(allowed, scores, masked_value)
            top_old = tops[h]
            top = jnp.maximum(top_old, jnp.max(scores, axis=0, keepdims=True))
            weights = jnp.exp(scores - top)
            shrink = jnp.exp(top_old - top)
            tops[h] = top
            totals[h] = totals[h] * shrink + jnp.sum(weights, axis=0, keepdims=True)
            sums[h] = sums[h] * shrink + jnp.dot(
                turned[tile, 128 * h + HEAD_SIZE : 128 * h + 128, :],
                weights.astype(bf16),
                preferred_element_type=f32,
            )

    over_tiles(tile_range(starts_ref, fills_ref, block), block, step)
    for h in range(KEY_VALUE_HEADS):
        outcome = (sums[h] / totals[h]).astype(bf16)
        log_total = tops[h] + jnp.log(totals[h])
        for g in range(GROUPED):
            head = GROUPED * h + g
            mixed_ref[HEAD_SIZE * head : HEAD_SIZE * (head + 1), :] = outcome[:, BLK * g : BLK * (g + 1)]
            log_ref[head : head + 1, :] = log_total[:, BLK * g : BLK * (g + 1)]
    log_ref[QUERY_HEADS:, :] = jnp.zeros((1, BLK), f32)


def token_block(rows):
    return pl.BlockSpec((rows, BLK), lambda i, *_: (0, i))


def whole(shape):
    return pl.BlockSpec(shape, lambda i, *_: (0,) * len(shape))


def attention_forward(starts, fills, place, query, kv):
    group = kv.shape[0]
    return pl.pallas_call(
        attention_forward_kernel,
        grid_spec=pltpu.PrefetchScalarGridSpec(
            num_scalar_prefetch=3,
            grid=(TOK_DEV // BLK,),
            in_specs=[token_block(MODEL_WIDTH), whole((group, 2 * KV_WIDTH))],
            out_specs=[token_block(MODEL_WIDTH), token_block(16)],
            scratch_shapes=[
                pltpu.VMEM((group // TILE, 2 * KV_WIDTH, TILE), bf16),
                pltpu.VMEM((KEY_VALUE_HEADS, 2 * HEAD_SIZE, WIDE), bf16),
                pltpu.VMEM((KEY_VALUE_HEADS, 1, WIDE), f32),
                pltpu.VMEM((KEY_VALUE_HEADS, 1, WIDE), f32),
                pltpu.VMEM((KEY_VALUE_HEADS, HEAD_SIZE, WIDE), f32),
            ],
        ),
        out_shape=[
            jax.ShapeDtypeStruct((MODEL_WIDTH, TOK_DEV), bf16),
            jax.ShapeDtypeStruct((16, TOK_DEV), f32),
        ],
        name="attention_forward",
    )(starts, fills, place, query, kv)


def attention_backward_kernel(
    starts_ref,
    fills_ref,
    place_ref,
    query_ref,
    upstream_ref,
    mixed_ref,
    log_ref,
    cosine_ref,
    sine_ref,
    kv_ref,
    d_query_ref,
    d_kv_ref,
    turned,
    pairs,
    query_rows,
    upstream_rows,
    deltas,
    logs,
    sums,
    kv_sums,
):
    i = pl.program_id(0)
    block = place_ref[0] * (TOK_DEV // BLK) + i
    tiles = kv_ref.shape[0] // TILE

    @pl.when(i == 0)
    def _():
        transpose_kv(kv_ref, turned, tiles)

        def clear(t, carry):
            kv_sums[:, pl.ds(pl.multiple_of(t * TILE, TILE), TILE), :] = jnp.zeros(
                (KEY_VALUE_HEADS, TILE, 128), f32
            )
            return carry

        lax.fori_loop(0, tiles, clear, 0)

    blank = jnp.zeros((HEAD_SIZE, WIDE), bf16)
    for h in range(KEY_VALUE_HEADS):
        query = heads_beside(query_ref, h)
        upstream = heads_beside(upstream_ref, h)
        pairs[h, :HEAD_SIZE, :WIDE] = query
        pairs[h, HEAD_SIZE:, :WIDE] = blank
        pairs[h, :HEAD_SIZE, WIDE:] = blank
        pairs[h, HEAD_SIZE:, WIDE:] = upstream
        query_rows[h] = pairs[h, :, :WIDE].T
        upstream_rows[h] = pairs[h, :, WIDE:].T
        deltas[h] = jnp.sum(
            upstream.astype(f32) * heads_beside(mixed_ref, h).astype(f32), axis=0, keepdims=True
        )
        logs[h] = jnp.concatenate(
            [log_ref[GROUPED * h + g : GROUPED * h + g + 1, :] for g in range(GROUPED)], axis=1
        )
    sums[...] = jnp.zeros(sums.shape, f32)

    def step(tile, allowed):
        rows = pl.ds(pl.multiple_of(tile * TILE, TILE), TILE)
        for h in range(KEY_VALUE_HEADS):
            both = jnp.dot(
                kv_ref[rows, 128 * h : 128 * h + 128], pairs[h], preferred_element_type=f32
            )
            scores = both[:, :WIDE]
            if allowed is not None:
                scores = jnp.where(allowed, scores, masked_value)
            probs = jnp.exp(scores - logs[h])
            d_scores = (probs * (both[:, WIDE:] - deltas[h])).astype(bf16)
            kv_sums[h, rows, :] += jnp.dot(
                d_scores, query_rows[h], preferred_element_type=f32
            ) + jnp.dot(probs.astype(bf16), upstream_rows[h], preferred_element_type=f32)
            sums[h] += jnp.dot(
                turned[tile, 128 * h : 128 * h + HEAD_SIZE, :], d_scores, preferred_element_type=f32
            )

    over_tiles(tile_range(starts_ref, fills_ref, block), block, step)
    cosine = cosine_ref[...]
    sine = sine_ref[...]
    half = HEAD_SIZE // 2
    for h in range(KEY_VALUE_HEADS):
        for g in range(GROUPED):
            head = GROUPED * h + g
            front = sums[h, :half, BLK * g : BLK * (g + 1)] * score_scale
            back = sums[h, half:, BLK * g : BLK * (g + 1)] * score_scale
            d_query_ref[HEAD_SIZE * head : HEAD_SIZE * head + half, :] = (
                front * cosine + back * sine
            ).astype(bf16)
            d_query_ref[HEAD_SIZE * head + half : HEAD_SIZE * (head + 1), :] = (
                back * cosine - front * sine
            ).astype(bf16)

    @pl.when(i == pl.num_programs(0) - 1)
    def _():
        def emit(t, carry):
            rows = pl.ds(pl.multiple_of(t * TILE, TILE), TILE)
            for h in range(KEY_VALUE_HEADS):
                d_kv_ref[rows, 128 * h : 128 * h + 128] = kv_sums[h, rows, :].astype(bf16)
            return carry

        lax.fori_loop(0, tiles, emit, 0)


def attention_backward(starts, fills, place, query, upstream, mixed, logs, cosine, sine, kv):
    group = kv.shape[0]
    half = HEAD_SIZE // 2
    return pl.pallas_call(
        attention_backward_kernel,
        grid_spec=pltpu.PrefetchScalarGridSpec(
            num_scalar_prefetch=3,
            grid=(TOK_DEV // BLK,),
            in_specs=[
                token_block(MODEL_WIDTH),
                token_block(MODEL_WIDTH),
                token_block(MODEL_WIDTH),
                token_block(16),
                token_block(half),
                token_block(half),
                whole((group, 2 * KV_WIDTH)),
            ],
            out_specs=[token_block(MODEL_WIDTH), whole((group, 2 * KV_WIDTH))],
            scratch_shapes=[
                pltpu.VMEM((group // TILE, 2 * KV_WIDTH, TILE), bf16),
                pltpu.VMEM((KEY_VALUE_HEADS, 2 * HEAD_SIZE, 2 * WIDE), bf16),
                pltpu.VMEM((KEY_VALUE_HEADS, WIDE, 128), bf16),
                pltpu.VMEM((KEY_VALUE_HEADS, WIDE, 128), bf16),
                pltpu.VMEM((KEY_VALUE_HEADS, 1, WIDE), f32),
                pltpu.VMEM((KEY_VALUE_HEADS, 1, WIDE), f32),
                pltpu.VMEM((KEY_VALUE_HEADS, HEAD_SIZE, WIDE), f32),
                pltpu.VMEM((KEY_VALUE_HEADS, group, 128), f32),
            ],
        ),
        out_shape=[
            jax.ShapeDtypeStruct((MODEL_WIDTH, TOK_DEV), bf16),
            jax.ShapeDtypeStruct((group, 2 * KV_WIDTH), bf16),
        ],
        name="attention_backward",
    )(starts, fills, place, query, upstream, mixed, logs, cosine, sine, kv)


def dot_of(left, right, left_dim, right_dim):
    return lax.dot_general(
        left, right, (((left_dim,), (right_dim,)), ((), ())), preferred_element_type=f32
    )


SLOTS = 3
FORM = 640
PIECES = (240, 240, 160)
GAIN_LINE = 560
PAD_WIDTH = 1024
CHUNK = 640
CORE_BIT = ("shard", 1)
NEAR_BITS = (("shard", 2), ("dp", 1), ("dp", 2))
FAR_BITS = (("dp", 4),)


def stages(colour):
    return (CORE_BIT,) + NEAR_BITS[colour:] + NEAR_BITS[:colour] + FAR_BITS


def swap(value, bit):
    axis, mask = bit
    size = lax.axis_size(axis)
    return lax.ppermute(value, axis, [(i, i ^ mask) for i in range(size)])


def gather_colour(own, colour):
    held = own[None]
    for bit in reversed(stages(colour)[1:]):
        held = jnp.concatenate([held, swap(held, bit)], axis=0)
    return held, swap(held, CORE_BIT)


def scatter_colour(keep, send, colour):
    for bit in stages(colour):
        got = swap(send, bit)
        half = keep.shape[0] // 2
        if half == 0:
            return keep[0], got[0]
        send = keep[half:] + got[half:]
        keep = keep[:half] + got[:half]


def positions():
    device = jnp.arange(UNITS, dtype=jnp.int32)
    width = lax.axis_size("shard")
    apart = {
        "dp": (device // width) ^ lax.axis_index("dp").astype(jnp.int32),
        "shard": (device % width) ^ lax.axis_index("shard").astype(jnp.int32),
    }
    tables = []
    for colour in range(SLOTS):
        place = jnp.zeros((UNITS,), jnp.int32)
        for axis, mask in stages(colour):
            place = 2 * place + (apart[axis] & mask) // mask
        tables.append(place)
    return jnp.concatenate(tables)


def copy_from(halves, place, dst, sem, pick=lambda ref: ref):
    for number, ref in enumerate(halves):

        @pl.when(place // 16 == number)
        def _():
            pltpu.make_async_copy(pick(ref.at[lax.rem(place, 16)]), dst, sem).start()


def copy_to(src, halves, place, sem, pick=lambda ref: ref):
    for number, ref in enumerate(halves):

        @pl.when(place // 16 == number)
        def _():
            pltpu.make_async_copy(src, pick(ref.at[lax.rem(place, 16)]), sem).start()


def wait_for(ref, sem):
    pltpu.make_async_copy(ref, ref, sem).wait()


def form_attention_kernel(wide_ref, lines_ref, gains_ref, a_ref, b_ref, c_ref, mid, form):
    @pl.when(wide_ref[0] == 1)
    def _():
        def store(c, value):
            if c == 7:
                value = jnp.where(lane_low(80), value, 0.0)
            form[80 * c : 80 * c + 80, :] = value

        lines_to_rows_960(lines_ref, 0, 80, mid, store)

    @pl.when(wide_ref[0] == 0)
    def _():
        low = lane_low(120)
        line = [lines_ref[pl.ds(k, 120, stride=5), :] for k in range(5)]
        turned = [None, None] + [pltpu.roll(line[k], 64, 1) for k in range(2, 5)]
        form[pl.ds(0, 120, stride=2), :] = line[0]
        form[pl.ds(1, 120, stride=2), :] = jnp.where(low, turned[2], turned[3])
        form[pl.ds(240, 120, stride=2), :] = line[1]
        form[pl.ds(241, 120, stride=2), :] = jnp.where(low, turned[3], turned[4])
        mid[pl.ds(0, 120, stride=2), :] = line[2]
        mid[pl.ds(1, 120, stride=2), :] = turned[4]
        low = lane_low(80)
        form[480:560, :] = jnp.where(low, mid[0:80, :], pltpu.roll(mid[160:240, :], 64, 1))
        form[560:640, :] = jnp.where(low, mid[80:160, :], 0.0)

    form[GAIN_LINE : GAIN_LINE + 1, :] = jnp.where(
        lane_low(1), form[GAIN_LINE : GAIN_LINE + 1, :], gains_ref[...]
    )
    a_ref[...] = form[0:240, :].astype(bf16)
    b_ref[...] = form[240:480, :].astype(bf16)
    c_ref[...] = form[480:640, :].astype(bf16)


SMEM_SPEC = pl.BlockSpec(memory_space=pltpu.SMEM)
ANY_SPEC = pl.BlockSpec(memory_space=pl.ANY)


def form_attention(wide, lines, gains):
    return pl.pallas_call(
        form_attention_kernel,
        in_specs=[SMEM_SPEC, pl.BlockSpec((LINES, 128)), pl.BlockSpec((1, 128))],
        out_shape=[jax.ShapeDtypeStruct((n, 128), bf16) for n in PIECES],
        scratch_shapes=[pltpu.VMEM((240, 128), f32), pltpu.VMEM((FORM, 128), f32)],
        name="form_attention",
    )(wide, lines, gains)


def unform_attention_kernel(wide_ref, *refs):
    pieces, (lines_ref, gains_ref, mid, form) = refs[:6], refs[6:]
    base = 0
    for n, keep, got in zip(PIECES, pieces[0::2], pieces[1::2]):
        form[base : base + n, :] = keep[...].astype(f32) + got[...].astype(f32)
        base += n
    gains_ref[...] = form[GAIN_LINE : GAIN_LINE + 1, :]

    @pl.when(wide_ref[0] == 1)
    def _():
        rows_to_lines_960(lambda c: form[80 * c : 80 * c + 80, :], lines_ref, 0, 80, mid)

    @pl.when(wide_ref[0] == 0)
    def _():
        low = lane_low(120)
        mid[0:80, :] = form[480:560, :]
        mid[80:160, :] = form[560:640, :]
        mid[160:240, :] = pltpu.roll(form[480:560, :], 64, 1)
        even = [form[pl.ds(0, 120, stride=2), :], form[pl.ds(240, 120, stride=2), :]]
        odd = [form[pl.ds(1, 120, stride=2), :], form[pl.ds(241, 120, stride=2), :]]
        even.append(mid[pl.ds(0, 120, stride=2), :])
        odd.append(mid[pl.ds(1, 120, stride=2), :])
        odd = [pltpu.roll(value, 64, 1) for value in odd]
        lines_ref[pl.ds(0, 120, stride=5), :] = even[0]
        lines_ref[pl.ds(1, 120, stride=5), :] = even[1]
        lines_ref[pl.ds(2, 120, stride=5), :] = jnp.where(low, even[2], odd[0])
        lines_ref[pl.ds(3, 120, stride=5), :] = jnp.where(low, odd[0], odd[1])
        lines_ref[pl.ds(4, 120, stride=5), :] = jnp.where(low, odd[1], odd[2])


def unform_attention(wide, addends):
    return pl.pallas_call(
        unform_attention_kernel,
        in_specs=[SMEM_SPEC] + [pl.BlockSpec((n, 128)) for n in PIECES for _ in range(2)],
        out_shape=[jax.ShapeDtypeStruct((LINES, 128), f32), jax.ShapeDtypeStruct((1, 128), f32)],
        scratch_shapes=[pltpu.VMEM((240, 128), f32), pltpu.VMEM((FORM, 128), f32)],
        name="unform_attention",
    )(wide, *addends)


def wide_pieces(c):
    return [((80 * c + 16 * m) // 32, (80 * c + 16 * m) % 32, 16 * m) for m in range(5)]


def form_feedforward_kernel(narrow_ref, lines_ref, *refs):
    outs, mid = refs[:SLOTS], refs[SLOTS]
    for s, out in enumerate(outs):

        @pl.when(narrow_ref[s] == 1)
        def _():
            mid[30:32, :] = jnp.zeros((2, 128), f32)
            for c in range(20):
                mid[0:30, :] = lines_ref[pl.ds(LINES * s + c, 30, stride=20), :]
                out[c] = mid[0:32, :].astype(bf16)

        @pl.when(narrow_ref[s] == 0)
        def _():
            def store(c, value):
                if c == 7:
                    value = jnp.where(lane_low(80), value, 0.0)
                for k, r, m in wide_pieces(c):
                    out[k, r : r + 16, :] = value[m : m + 16].astype(bf16)

            lines_to_rows_960(lines_ref, LINES * s, 80, mid, store)


def form_feedforward(narrow, lines):
    return pl.pallas_call(
        form_feedforward_kernel,
        in_specs=[SMEM_SPEC, pl.BlockSpec((SLOTS * LINES, 128))],
        out_shape=[jax.ShapeDtypeStruct((20, 32, 128), bf16)] * SLOTS,
        scratch_shapes=[pltpu.VMEM((80, 128), f32)],
        name="form_feedforward",
    )(narrow, lines)


def unform_feedforward_kernel(narrow_ref, *refs):
    pieces, (lines_ref, mid) = refs[: 2 * SLOTS], refs[2 * SLOTS :]
    for s in range(SLOTS):
        keep, got = pieces[2 * s], pieces[2 * s + 1]

        @pl.when(narrow_ref[s] == 1)
        def _():
            for c in range(20):
                mid[0:32, :] = keep[c].astype(f32) + got[c].astype(f32)
                lines_ref[pl.ds(LINES * s + c, 30, stride=20), :] = mid[0:30, :]

        @pl.when(narrow_ref[s] == 0)
        def _():
            def load(c):
                return jnp.concatenate(
                    [
                        keep[k, r : r + 16, :].astype(f32) + got[k, r : r + 16, :].astype(f32)
                        for k, r, m in wide_pieces(c)
                    ],
                    axis=0,
                )

            rows_to_lines_960(load, lines_ref, LINES * s, 80, mid)


def unform_feedforward(narrow, addends):
    return pl.pallas_call(
        unform_feedforward_kernel,
        in_specs=[SMEM_SPEC] + [pl.BlockSpec((20, 32, 128))] * (2 * SLOTS),
        out_shape=jax.ShapeDtypeStruct((SLOTS * LINES, 128), f32),
        scratch_shapes=[pltpu.VMEM((80, 128), f32)],
        name="unform_feedforward",
    )(narrow, *addends)


def place_attention_kernel(table_ref, *refs):
    halves = [refs[2 * k : 2 * k + 2] for k in range(SLOTS)]
    query_ref, kv_ref, out_ref, gains_ref, units, sem = refs[2 * SLOTS :]

    def start(d, carry):
        base = 0
        for k, n in enumerate(PIECES):
            copy_from(halves[k], table_ref[UNITS * k + d], units.at[d, base : base + n, :], sem)
            base += n
        return carry

    lax.fori_loop(0, UNITS, start, 0)
    wait_for(units, sem)

    def wide(out, first):
        def body(u, carry):
            rows = pl.ds(pl.multiple_of(80 * u, 16), 80)
            for c in range(7):
                out[rows, 128 * c : 128 * c + 128] = units[first + u, 80 * c : 80 * c + 80, :]
            out[rows, 896:960] = units[first + u, 560:640, :64]
            return carry

        lax.fori_loop(0, 12, body, 0)

    def keyed(j, carry):
        low = lane_low(240)
        chunks = []
        for first in (12, 16):
            unit = units[first + j].astype(f32)
            last = jnp.concatenate(
                [unit[480:640], pltpu.roll(unit[480:560], 64, 1)], axis=0
            )
            lines = (unit[0:240], unit[240:480], last)
            chunks.append([(lines[h // 2], h % 2) for h in range(KEY_VALUE_HEADS)])
        rows = pl.ds(pl.multiple_of(240 * j, 16), 240)
        for h in range(KEY_VALUE_HEADS):
            kv_ref[rows, 128 * h : 128 * h + 128] = jnp.where(
                low, placed(chunks[0][h], 0), placed(chunks[1][h], 1)
            ).astype(bf16)
        return carry

    lax.fori_loop(0, 4, keyed, 0)
    wide(query_ref, 0)
    wide(out_ref, 20)
    for u in range(UNITS):
        gains_ref[u : u + 1, :] = units[u, GAIN_LINE : GAIN_LINE + 1, :].astype(f32)


def place_attention(table, gathered):
    return pl.pallas_call(
        place_attention_kernel,
        in_specs=[SMEM_SPEC] + [ANY_SPEC] * (2 * SLOTS),
        out_shape=[
            jax.ShapeDtypeStruct((MODEL_WIDTH, MODEL_WIDTH), bf16),
            jax.ShapeDtypeStruct((MODEL_WIDTH, 2 * KV_WIDTH), bf16),
            jax.ShapeDtypeStruct((MODEL_WIDTH, MODEL_WIDTH), bf16),
            jax.ShapeDtypeStruct((UNITS, 128), f32),
        ],
        scratch_shapes=[pltpu.VMEM((UNITS, FORM, 128), bf16), pltpu.SemaphoreType.DMA],
        name="place_attention",
    )(table, *gathered)


def split_attention_kernel(table_ref, query_ref, kv_ref, out_ref, gains_ref, *refs):
    halves = [refs[2 * k : 2 * k + 2] for k in range(SLOTS)]
    units, sem = refs[2 * SLOTS :]

    def send(d):
        row = lax.broadcasted_iota(jnp.int32, (16, 128), 0)
        lane = lax.broadcasted_iota(jnp.int32, (16, 128), 1)
        block = units[d, GAIN_LINE : GAIN_LINE + 16, :].astype(f32)
        units[d, GAIN_LINE : GAIN_LINE + 16, :] = jnp.where(
            jnp.logical_and(row == 0, lane >= 64), gains_ref[pl.ds(d, 1), :], block
        ).astype(bf16)
        base = 0
        for k, n in enumerate(PIECES):
            copy_to(units.at[d, base : base + n, :], halves[k], table_ref[UNITS * k + d], sem)
            base += n

    def wide(source, first):
        def body(u, carry):
            rows = pl.ds(pl.multiple_of(80 * u, 16), 80)
            for c in range(7):
                units[first + u, 80 * c : 80 * c + 80, :] = source[rows, 128 * c : 128 * c + 128]
            tail = source[rows, 896:960]
            units[first + u, 560:640, :] = jnp.concatenate([tail, jnp.zeros_like(tail)], axis=1)
            send(first + u)
            return carry

        lax.fori_loop(0, 12, body, 0)

    def keyed(j, carry):
        low = lane_low(240)
        rows = pl.ds(pl.multiple_of(240 * j, 16), 240)
        for upper, first in ((0, 12), (1, 16)):
            heads = [
                (kv_ref[rows, 128 * h : 128 * h + 128].astype(f32), upper)
                for h in range(KEY_VALUE_HEADS)
            ]
            for c in range(2):
                units[first + j, 240 * c : 240 * c + 240, :] = jnp.where(
                    low, placed(heads[2 * c], 0), placed(heads[2 * c + 1], 1)
                ).astype(bf16)
            last = placed(heads[4], 0)
            turned = placed(heads[4], 1)
            units[first + j, 480:560, :] = jnp.where(
                lane_low(80), last[0:80], turned[160:240]
            ).astype(bf16)
            units[first + j, 560:640, :] = jnp.where(lane_low(80), last[80:160], 0.0).astype(bf16)
            send(first + j)
        return carry

    lax.fori_loop(0, 4, keyed, 0)
    wide(query_ref, 0)
    wide(out_ref, 20)
    wait_for(units, sem)


def split_attention(table, d_query, d_kv, d_out, gains):
    return pl.pallas_call(
        split_attention_kernel,
        in_specs=[
            SMEM_SPEC,
            pl.BlockSpec((MODEL_WIDTH, MODEL_WIDTH)),
            pl.BlockSpec((MODEL_WIDTH, 2 * KV_WIDTH)),
            pl.BlockSpec((MODEL_WIDTH, MODEL_WIDTH)),
            pl.BlockSpec((UNITS, 128)),
        ],
        out_specs=[ANY_SPEC] * (2 * SLOTS),
        out_shape=[jax.ShapeDtypeStruct((16, n, 128), bf16) for n in PIECES for _ in range(2)],
        scratch_shapes=[pltpu.VMEM((UNITS, FORM, 128), bf16), pltpu.SemaphoreType.DMA],
        name="split_attention",
    )(table, d_query, d_kv, d_out, gains)


def feedforward_kernel(table_ref, hidden_ref, turned_ref, grad_ref, *refs):
    sources = [refs[2 * s : 2 * s + 2] for s in range(SLOTS)]
    out_ref, d_hidden_ref = refs[6:8]
    targets = [refs[8 + 2 * s : 10 + 2 * s] for s in range(SLOTS)]
    (
        both_in,
        down_in,
        down,
        inner_rows,
        inner_turned,
        d_both,
        both_out,
        down_out,
        in_sem,
        out_sem,
    ) = refs[14:]
    q = pl.program_id(0)
    chunks = pl.num_programs(0)
    slot = lax.rem(q, 2)

    def narrow_units(move, chunk, buffer):
        columns = lambda ref: ref.at[pl.ds(5 * chunk, 5)]
        for u in range(2 * UNITS):
            device, s = divmod(u, SLOTS)
            piece = buffer.at[pl.ds(5 * (u // UNITS), 5), pl.ds(32 * (u % UNITS), 32), :]
            move(s, table_ref[UNITS * s + device], piece, columns)

    def down_units(move, chunk, buffer):
        for v in range(8):
            unit = 2 * UNITS + 8 * chunk + v
            device = unit // SLOTS
            for s in range(SLOTS):

                @pl.when(unit - SLOTS * device == s)
                def _():
                    move(s, table_ref[UNITS * s + device], buffer.at[v], lambda ref: ref)

    def start_in(chunk, carry):
        side = lax.rem(chunk, 2)
        narrow_units(
            lambda s, place, piece, pick: copy_from(
                sources[s], place, piece, in_sem.at[side, 0], pick
            ),
            chunk,
            both_in.at[side],
        )
        down_units(
            lambda s, place, piece, pick: copy_from(
                sources[s], place, piece, in_sem.at[side, 1], pick
            ),
            chunk,
            down_in.at[side],
        )
        return carry

    lax.fori_loop(jnp.where(q == 0, 0, q + 1), jnp.minimum(q + 2, chunks), start_in, 0)
    wait_for(both_in.at[slot], in_sem.at[slot, 0])
    wait_for(down_in.at[slot], in_sem.at[slot, 1])

    for v in range(8):
        for c in range(8):
            for k, r, m in wide_pieces(c):
                down[80 * v + m : 80 * v + m + 16, 128 * c : 128 * c + 128] = down_in[
                    slot, v, k, r : r + 16, :
                ]

    @pl.when(q == 0)
    def _():
        out_ref[...] = jnp.zeros(out_ref.shape, f32)
        d_hidden_ref[...] = jnp.zeros(d_hidden_ref.shape, f32)

    def rows_step(i, carry):
        rows = pl.ds(pl.multiple_of(256 * i, 256), 256)
        weights = jnp.concatenate([both_in[slot, c] for c in range(10)], axis=1)
        both = jnp.dot(hidden_ref[rows, :], weights, preferred_element_type=f32)
        gate, upper = both[:, :CHUNK], both[:, CHUNK:]
        sigmoid_gate = jax.nn.sigmoid(gate)
        activated = gate * sigmoid_gate
        inner = (activated * upper).astype(bf16)
        inner_rows[rows, :] = inner
        out_ref[rows, :] += jnp.dot(inner, down[...], preferred_element_type=f32)
        d_inner = dot_of(grad_ref[rows, :], down[...], 1, 1)
        d_gate = d_inner * upper * sigmoid_gate * (1.0 + gate * (1.0 - sigmoid_gate))
        d_upper = d_inner * activated
        d_pair = jnp.concatenate([d_gate, d_upper], axis=1).astype(bf16)
        d_both[rows, :] = d_pair
        d_hidden_ref[rows, :] += dot_of(d_pair, weights, 1, 1)
        return carry

    lax.fori_loop(0, 2, rows_step, 0)
    inner_turned[...] = inner_rows[...].T

    @pl.when(q >= 2)
    def _():
        wait_for(both_out.at[slot], out_sem.at[slot, 0])
        wait_for(down_out.at[slot], out_sem.at[slot, 1])

    def both_step(i, carry):
        rows = pl.ds(pl.multiple_of(256 * i, 256), 256)
        terms = jnp.dot(turned_ref[rows, :], d_both[...], preferred_element_type=f32)
        for c in range(10):
            both_out[slot, c, rows, :] = terms[:, 128 * c : 128 * c + 128].astype(bf16)
        return carry

    lax.fori_loop(0, 4, both_step, 0)

    def down_step(i, carry):
        rows = pl.ds(pl.multiple_of(320 * i, 16), 320)
        terms = jnp.dot(
            inner_turned[rows, :], grad_ref[...], preferred_element_type=f32
        ).astype(bf16)
        for v in range(4):
            for c in range(8):
                for k, r, m in wide_pieces(c):
                    down_out[slot, 4 * i + v, k, r : r + 16, :] = terms[
                        80 * v + m : 80 * v + m + 16, 128 * c : 128 * c + 128
                    ]
        return carry

    lax.fori_loop(0, 2, down_step, 0)
    narrow_units(
        lambda s, place, piece, pick: copy_to(
            piece, targets[s], place, out_sem.at[slot, 0], pick
        ),
        q,
        both_out.at[slot],
    )
    down_units(
        lambda s, place, piece, pick: copy_to(
            piece, targets[s], place, out_sem.at[slot, 1], pick
        ),
        q,
        down_out.at[slot],
    )

    @pl.when(q == chunks - 1)
    def _():
        for side in range(2):
            wait_for(both_out.at[side], out_sem.at[side, 0])
            wait_for(down_out.at[side], out_sem.at[side, 1])


def feedforward(table, hidden, turned, grad, gathered):
    block = jax.ShapeDtypeStruct((16, 20, 32, 128), bf16)
    full = lambda shape: pl.BlockSpec(shape, lambda q: (0, 0))
    return pl.pallas_call(
        feedforward_kernel,
        grid=(FF // CHUNK,),
        in_specs=[
            SMEM_SPEC,
            full((TOK_DEV, PAD_WIDTH)),
            full((PAD_WIDTH, TOK_DEV)),
            full((TOK_DEV, PAD_WIDTH)),
        ]
        + [ANY_SPEC] * (2 * SLOTS),
        out_specs=[full((TOK_DEV, PAD_WIDTH))] * 2 + [ANY_SPEC] * (2 * SLOTS),
        out_shape=[jax.ShapeDtypeStruct((TOK_DEV, PAD_WIDTH), f32)] * 2 + [block] * (2 * SLOTS),
        scratch_shapes=[
            pltpu.VMEM((2, 10, PAD_WIDTH, 128), bf16),
            pltpu.VMEM((2, 8, 20, 32, 128), bf16),
            pltpu.VMEM((CHUNK, PAD_WIDTH), bf16),
            pltpu.VMEM((TOK_DEV, CHUNK), bf16),
            pltpu.VMEM((CHUNK, TOK_DEV), bf16),
            pltpu.VMEM((TOK_DEV, 2 * CHUNK), bf16),
            pltpu.VMEM((2, 10, PAD_WIDTH, 128), bf16),
            pltpu.VMEM((2, 8, 20, 32, 128), bf16),
            pltpu.SemaphoreType.DMA((2, 2)),
            pltpu.SemaphoreType.DMA((2, 2)),
        ],
        compiler_params=pltpu.CompilerParams(vmem_limit_bytes=60 * 2**20),
        name="feedforward",
    )(table, hidden, turned, grad, *gathered)


def spread_matrix():
    column = jnp.arange(PAD_WIDTH, dtype=jnp.int32)
    entry = jnp.where(column % 32 < 30, 30 * (column // 32) + column % 32, -1)
    return (jnp.arange(MODEL_WIDTH, dtype=jnp.int32)[:, None] == entry[None, :]).astype(bf16)


def rope_tables(positions):
    steps = jnp.arange(HEAD_SIZE // 2, dtype=f32) * (2.0 / HEAD_SIZE)
    inverse = jnp.exp(-math.log(10000.0) * steps)
    angles = inverse[:, None] * positions.astype(f32)[None, :]
    return (jnp.cos(angles), jnp.sin(angles))


def norm_scale(field):
    return lax.rsqrt(jnp.mean(field * field, axis=1, keepdims=True) + epsilon)


def norm_back(upstream, normed, scale, gain):
    scaled = upstream * gain[None, :]
    return scale * (scaled - normed * jnp.mean(scaled * normed, axis=1, keepdims=True))


def adam_step(grad, moment, second, master):
    moment_new = 0.9 * moment + 0.1 * grad
    second_new = 0.999 * second + 0.001 * grad * grad
    corrected = moment_new / (1.0 - 0.9**ADAM_STEP)
    scaled = second_new / (1.0 - 0.999**ADAM_STEP)
    update = -learning_rate * (corrected / (jnp.sqrt(scaled) + 1e-08) + weight_decay * master)
    return (moment_new, second_new, update)


def gather_lines(block):
    return lax.all_gather(block, ALL_AXES, axis=0, tiled=True)


def scatter_lines(lines):
    return lax.psum_scatter(lines, ALL_AXES, scatter_dimension=0, tiled=True)


def local(
    layer_input,
    cotangent,
    master_attention,
    master_feedforward,
    master_gains,
    first_attention,
    second_attention,
    first_feedforward,
    second_feedforward,
    first_gains,
    second_gains,
    block_start,
    block_fill,
):
    devices = lax.axis_size(ALL_AXES)
    attention_lines = master_attention.shape[0] // 128
    feedforward_lines = master_feedforward.shape[0] // 128
    gain_count = master_gains.shape[0]
    padded = (attention_lines // 16 + 1) * 16

    in_units = devices == UNITS
    if in_units:
        table = positions()
        device = (
            lax.axis_index("dp") * lax.axis_size("shard") + lax.axis_index("shard")
        ).astype(jnp.int32)
        wide = jnp.logical_or(device < 12, device >= 20).astype(jnp.int32)[None]
        narrow = (SLOTS * device + jnp.arange(SLOTS, dtype=jnp.int32) < 2 * UNITS).astype(jnp.int32)
        gain_row = jnp.pad(
            master_gains.reshape(1, gain_count), ((0, 0), (64, 64 - gain_count))
        )
        pieces = form_attention(wide, master_attention.reshape(LINES, 128), gain_row)
        gathered = [half for k in range(SLOTS) for half in gather_colour(pieces[k], k)]
        forms = form_feedforward(narrow, master_feedforward.reshape(SLOTS * LINES, 128))
        feedforward_all = [half for k in range(SLOTS) for half in gather_colour(forms[k], k)]
        query_weight, kv_weight, out_weight, gain_rows = place_attention(table, gathered)
        gains_all = gain_rows[:, 64 : 64 + gain_count].reshape(-1)
    else:
        gain_lines = jnp.pad(
            master_gains.astype(bf16).reshape(1, gain_count),
            ((0, padded - attention_lines - 1), (0, 128 - gain_count)),
        )
        attention_block = jnp.concatenate(
            [master_attention.astype(bf16).reshape(attention_lines, 128), gain_lines], axis=0
        )
        by_device = gather_lines(attention_block).reshape(devices, padded, 128)
        feedforward_all = gather_lines(
            master_feedforward.astype(bf16).reshape(feedforward_lines, 128)
        )
        gains_all = by_device[:, attention_lines, :gain_count].reshape(-1).astype(f32)
        units = by_device[:, :attention_lines].reshape(UNITS, LINES, 128)
        query_weight = unpack_wide(units, 0)
        kv_weight = unpack_kv(units)
        out_weight = unpack_wide(units, 20)
    gain_one, gain_two = gains_all[:MODEL_WIDTH], gains_all[MODEL_WIDTH:]

    shard = lax.axis_index("shard").astype(jnp.int32)
    place = shard[None]
    first_row = shard * TOK_DEV
    first_block = shard * (TOK_DEV // BLK)
    local_slots = first_row + jnp.arange(TOK_DEV, dtype=jnp.int32)
    local_starts = lax.dynamic_slice_in_dim(block_start, first_block, TOK_DEV // BLK)
    local_fills = lax.dynamic_slice_in_dim(block_fill, first_block, TOK_DEV // BLK)
    live_rows = local_slots % BLK < jnp.repeat(local_fills, BLK)
    cosine_table, sine_table = rope_tables(local_slots - jnp.repeat(local_starts, BLK) * BLK)

    def rotate(field, scale):
        heads = field.shape[0]
        front = field[:, : HEAD_SIZE // 2]
        back = field[:, HEAD_SIZE // 2 :]
        return (
            jnp.concatenate(
                [
                    front * cosine_table[None] - back * sine_table[None],
                    back * cosine_table[None] + front * sine_table[None],
                ],
                axis=1,
            ).astype(bf16)
            * bf16(scale)
        ).reshape(heads * HEAD_SIZE, TOK_DEV)

    inputs = layer_input.astype(f32)
    scale_one = norm_scale(inputs)
    normed_one = inputs * scale_one
    first_hidden = (normed_one * gain_one[None, :]).astype(bf16)
    kv_turned = dot_of(kv_weight, first_hidden, 0, 1).reshape(
        KEY_VALUE_HEADS, 2, HEAD_SIZE, TOK_DEV
    )
    keys = rotate(kv_turned[:, 0], 1.0).reshape(KEY_VALUE_HEADS, 1, HEAD_SIZE, TOK_DEV)
    values = kv_turned[:, 1:].astype(bf16)
    kv_rows = jnp.concatenate([keys, values], axis=1).reshape(2 * KV_WIDTH, TOK_DEV).T
    kv_all = lax.all_gather(kv_rows, "shard", axis=0, tiled=True)
    query_turned = rotate(
        dot_of(query_weight, first_hidden, 0, 1).reshape(QUERY_HEADS, HEAD_SIZE, TOK_DEV),
        score_scale,
    )
    mixed_turned, logs = attention_forward(block_start, block_fill, place, query_turned, kv_all)
    middle = inputs + dot_of(mixed_turned, out_weight, 0, 0)
    scale_two = norm_scale(middle)
    normed_two = middle * scale_two
    hidden_two = (normed_two * gain_two[None, :]).astype(bf16)

    grad_out = cotangent.astype(f32) * live_rows[:, None].astype(f32)
    grad_low = grad_out.astype(bf16)
    if in_units:
        spread = spread_matrix()
        outcome, d_spread, *ff_terms = feedforward(
            table,
            dot_of(hidden_two, spread, 1, 0).astype(bf16),
            dot_of(spread, hidden_two, 0, 1).astype(bf16),
            jnp.pad(grad_low, ((0, 0), (0, PAD_WIDTH - MODEL_WIDTH))),
            feedforward_all,
        )
        layer_output = middle + outcome[:, :MODEL_WIDTH]
        d_coarse = lax.reduce_precision(d_spread, 8, 7)
        d_hidden_two = dot_of(d_coarse.astype(bf16), spread, 1, 1) + dot_of(
            (d_spread - d_coarse).astype(bf16), spread, 1, 1
        )
        ff_addends = [
            addend
            for k in range(SLOTS)
            for addend in scatter_colour(ff_terms[2 * k], ff_terms[2 * k + 1], k)
        ]
        feedforward_gradient = unform_feedforward(narrow, ff_addends).reshape(-1)
    else:
        gate_weight, up_weight, down_weight = unpack_ff(feedforward_all)
        gate = dot_of(hidden_two, gate_weight, 1, 0)
        upper = dot_of(hidden_two, up_weight, 1, 0)
        sigmoid_gate = jax.nn.sigmoid(gate)
        activated = gate * sigmoid_gate
        inner = (activated * upper).astype(bf16)
        layer_output = middle + dot_of(inner, down_weight, 1, 0)
        d_down_weight = dot_of(inner, grad_low, 0, 0).astype(bf16)
        d_inner = dot_of(grad_low, down_weight, 1, 1)
        d_gate = (
            d_inner * upper * sigmoid_gate * (1.0 + gate * (1.0 - sigmoid_gate))
        ).astype(bf16)
        d_upper = (d_inner * activated).astype(bf16)
        d_gate_weight = dot_of(hidden_two, d_gate, 0, 0).astype(bf16)
        d_up_weight = dot_of(hidden_two, d_upper, 0, 0).astype(bf16)
        d_hidden_two = dot_of(d_gate, gate_weight, 1, 1) + dot_of(d_upper, up_weight, 1, 1)
        feedforward_gradient = (
            scatter_lines(pack_ff(d_gate_weight, d_up_weight, d_down_weight))
            .astype(f32)
            .reshape(-1)
        )

    d_gain_two = jnp.sum(d_hidden_two * normed_two, axis=0)
    d_middle = grad_out + norm_back(d_hidden_two, normed_two, scale_two, gain_two)

    d_branch = d_middle.astype(bf16)
    d_out_weight = dot_of(mixed_turned, d_branch, 1, 0).astype(bf16)
    d_mixed = dot_of(out_weight, d_branch, 1, 1).astype(bf16)
    d_query, d_kv = attention_backward(
        block_start,
        block_fill,
        place,
        query_turned,
        d_mixed,
        mixed_turned,
        logs,
        cosine_table,
        sine_table,
        kv_all,
    )
    d_kv_rows = lax.psum_scatter(d_kv, "shard", scatter_dimension=0, tiled=True)
    d_kv_turned = d_kv_rows.T.reshape(KEY_VALUE_HEADS, 2, HEAD_SIZE, TOK_DEV)
    d_front = d_kv_turned[:, 0, : HEAD_SIZE // 2].astype(f32)
    d_back = d_kv_turned[:, 0, HEAD_SIZE // 2 :].astype(f32)
    d_keys = jnp.concatenate(
        [
            d_front * cosine_table[None] + d_back * sine_table[None],
            d_back * cosine_table[None] - d_front * sine_table[None],
        ],
        axis=1,
    ).astype(bf16)
    d_kv_lin = jnp.concatenate([d_keys[:, None], d_kv_turned[:, 1:]], axis=1).reshape(
        2 * KV_WIDTH, TOK_DEV
    )
    d_query_weight = dot_of(first_hidden, d_query, 0, 1).astype(bf16)
    d_kv_weight = dot_of(first_hidden, d_kv_lin, 0, 1).astype(bf16)
    d_hidden_one = dot_of(d_query, query_weight, 0, 1) + dot_of(d_kv_lin, kv_weight, 0, 1)
    d_gain_one = jnp.sum(d_hidden_one * normed_one, axis=0)
    input_gradient = d_middle + norm_back(d_hidden_one, normed_one, scale_one, gain_one)

    gain_terms = jnp.concatenate([d_gain_one, d_gain_two])
    if in_units:
        gain_rows = jnp.pad(
            gain_terms.reshape(UNITS, gain_count), ((0, 0), (64, 64 - gain_count))
        )
        terms = split_attention(table, d_query_weight, d_kv_weight, d_out_weight, gain_rows)
        addends = [
            addend
            for k in range(SLOTS)
            for addend in scatter_colour(terms[2 * k], terms[2 * k + 1], k)
        ]
        attention_sum, gain_sum = unform_attention(wide, addends)
        attention_gradient = attention_sum.reshape(-1)
        gains_gradient = gain_sum[0, 64 : 64 + gain_count]
    else:
        no_gains = jnp.zeros((UNITS, GAIN_LINES, 128), bf16)
        terms = pack_attention(d_query_weight, d_kv_weight, d_out_weight, no_gains)
        terms = jnp.concatenate(
            [
                terms[:, :LINES].reshape(devices, attention_lines, 128),
                jnp.pad(
                    gain_terms.astype(bf16).reshape(devices, 1, gain_count),
                    ((0, 0), (0, padded - attention_lines - 1), (0, 128 - gain_count)),
                ),
            ],
            axis=1,
        )
        summed = scatter_lines(terms.reshape(devices * padded, 128)).astype(f32)
        attention_gradient = summed[:attention_lines].reshape(-1)
        gains_gradient = summed[attention_lines, :gain_count]

    attention_first, attention_second, attention_update = adam_step(
        attention_gradient, first_attention, second_attention, master_attention
    )
    feedforward_first, feedforward_second, feedforward_update = adam_step(
        feedforward_gradient, first_feedforward, second_feedforward, master_feedforward
    )
    gains_first, gains_second, gains_update = adam_step(
        gains_gradient, first_gains, second_gains, master_gains
    )
    return (
        layer_output,
        input_gradient,
        attention_gradient,
        feedforward_gradient,
        gains_gradient,
        attention_first,
        attention_second,
        feedforward_first,
        feedforward_second,
        gains_first,
        gains_second,
        attention_update,
        feedforward_update,
        gains_update,
    )


def solution(mesh):
    rows = P(ALL_AXES, None)
    flat = P(ALL_AXES)
    return jax.shard_map(
        local,
        mesh=mesh,
        in_specs=(rows, rows) + (flat,) * 9 + (P("dp"), P("dp")),
        out_specs=(rows, rows) + (flat,) * 12,
        check_vma=False,
    )
```

time: 1160 us -> 489 us (0.42)
  waiting for transfers between devices: 595 us -> 85.2 us
  matrix products: 201 us -> 32 us
  starting transfers between devices: 0.25 us -> 157 us
  Pallas kernels: 0 us -> 97.8 us
  local copies, waits for them, and re-layouts: 137 us -> 45.9 us
  blocking collectives: 82.7 us -> 0 us
  other arithmetic: 124 us -> 47.8 us
    unnamed x7 -> x2, waiting for transfers between devices: 513 us -> 0.03 us
    dot_general x51 -> x13, matrix products: 201 us -> 32 us  [dot_of(): lax.dot_general(left, right, (((left_dim,), (right_dim,)), ((), ())), pre...]
    ppermute x0 -> x60, starting transfers between devices: none -> 157 us  [swap(): return lax.ppermute(value, axis, [(i, i ^ mask) for i in range(size)])]
    pallas_call x0 -> x9, Pallas kernels: none -> 97.8 us  [the longest x1 47.3 us: feedforward(): pl.pallas_call(feedforward_kernel, grid=(FF // CHUNK,), in_specs=[SMEM_SP...]
    ppermute x0 -> x60, waiting for transfers between devices: none -> 85.2 us  [swap(): return lax.ppermute(value, axis, [(i, i ^ mask) for i in range(size)])]
    unnamed x2 -> x0, blocking collectives: 82.7 us -> none
    all_gather x4 -> x1, waiting for transfers between devices: 82.1 us -> 0.01 us  [local(): kv_all = lax.all_gather(kv_rows, 'shard', axis=0, tiled=True)]
    convert_element_type x12 -> x4, other arithmetic: 60.9 us -> 0.92 us  [the longest x1 0.54 us: local(): (SLOTS * device + jnp.arange(SLOTS, dtype=jnp.int32) < 2 * UNITS).astype(...]
  transfers between devices with their start and end apart: 6 -> 62, of which waited for: 3 -> 19; matrix products, arithmetic and copies ran while one was open for 16% -> 23% of each run, Pallas kernels for 0% -> 9%
where the time goes in v1:
time: 489 us; the launch traced here: 481 us
  starting transfers between devices  157 us (32%)
  Pallas kernels  97.8 us (20%)
  waiting for transfers between devices  85.2 us (17%)
  other arithmetic  47.8 us (10%)
  local copies, waits for them, and re-layouts  45.9 us (9%)
  matrix products  32 us (7%)
  between operations  15.4 us (3%)
    ppermute x60, starting transfers between devices, swap(): return lax.ppermute(value, axis, [(i, i ^ mask) for i in range(size)])  157 us
    ppermute x60, waiting for transfers between devices, swap(): return lax.ppermute(value, axis, [(i, i ^ mask) for i in range(size)])  85.2 us
    pallas_call x1, Pallas kernels, feedforward(): pl.pallas_call(feedforward_kernel, grid=(FF // CHUNK,), in_specs=[SMEM_SP...  47.3 us
    dot_general x13, matrix products, dot_of(): lax.dot_general(left, right, (((left_dim,), (right_dim,)), ((), ())), pre...  32 us
    unnamed x148, local copies, waits for them, and re-layouts  31.1 us
    pallas_call x1, Pallas kernels, attention_backward(): pl.pallas_call(attention_backward_kernel, grid_spec=pltpu.PrefetchScalarG...  16.4 us
    add x18, other arithmetic, scatter_colour(): keep = keep[:half] + got[:half]  14.9 us
    concatenate x18, other arithmetic, gather_colour(): held = jnp.concatenate([held, swap(held, bit)], axis=0)  14.2 us
  transfers between devices with their start and end apart: 62, of which 19 were waited for; matrix products, arithmetic and copies ran while one was open for 23% of the time, Pallas kernels for 9%

profile of v1, /device:TPU:0, one launch (start us, length us, event | category | flops | bytes accessed | tf_op | source)
XLA Modules:
  0.0 481.4 jit_solution(8377814931913737741)
XLA Ops:
  10.3 4.1 collective-permute-start.10
  63.0 9.9 %collective-permute-done.25 = bf16[1,20,32,128]{3,2,1,0:T(8,128)(2,1)S(1)} collective-permute-done((bf16[1,20,32,128]{3,2,1,0:T(8,128)(2,1)S(1)}, bf16[1,20,32,128]{3,2,1,0:T(8,128)(2,1)S(1)}, u32[]{:S(2)}, u32[]{:S(2)}) %collective-permute-start.25) | collective-permute-done | bytes 163872 | tf_op jit(solution)/shard_map/ppermute | solution.py:607
  76.4 5.3 %collective-permute-done.21 = bf16[2,20,32,128]{3,2,1,0:T(8,128)(2,1)S(1)} collective-permute-done((bf16[2,20,32,128]{3,2,1,0:T(8,128)(2,1)S(1)}, bf16[2,20,32,128]{3,2,1,0:T(8,128)(2,1)S(1)}, u32[]{:S(2)}, u32[]{:S(2)}) %collective-permute-start.21) | collective-permute-done | bytes 327712 | tf_op jit(solution)/shard_map/ppermute | solution.py:607
  86.8 7.1 %place_attention.1 = (bf16[960,960]{1,0:T(8,128)(2,1)}, bf16[960,640]{1,0:T(8,128)(2,1)}, bf16[960,960]{1,0:T(8,128)(2,1)}, f32[32,128]{1,0:T(8,128)}) custom-call(s32[96]{0:T(128)} %pad_add_fusion.table_ref, bf16[16,240,128]{2,1,0:T(8,128)(2,1)} %constant_dynamic-update-slice_fusion.refs_0_, bf16[16,240,128]{2,1,0:T(8,128)(2,1)} %collective-permute-done.4.refs_1_, ...), custom_call_target="tpu_custom_call" | custom-call | tf_op jit(solution)/shard_map/place_attention/pallas_call | solution.py:870
  111.4 8.5 %collective-permute-done.17 = bf16[4,20,32,128]{3,2,1,0:T(8,128)(2,1)S(1)} collective-permute-done((bf16[4,20,32,128]{3,2,1,0:T(8,128)(2,1)S(1)}, bf16[4,20,32,128]{3,2,1,0:T(8,128)(2,1)S(1)}, u32[]{:S(2)}, u32[]{:S(2)}) %collective-permute-start.17) | collective-permute-done | bytes 655392 | tf_op jit(solution)/shard_map/ppermute | solution.py:607
  130.8 6.5 %collective-permute-done.28 = bf16[8,20,32,128]{3,2,1,0:T(8,128)(2,1)S(1)} collective-permute-done((bf16[8,20,32,128]{3,2,1,0:T(8,128)(2,1)S(1)}, bf16[8,20,32,128]{3,2,1,0:T(8,128)(2,1)S(1)}, u32[]{:S(2)}, u32[]{:S(2)}) %collective-permute-start.28) | collective-permute-done | bytes 1310752 | tf_op jit(solution)/shard_map/ppermute | solution.py:607
  138.6 6.6 %collective-permute-done.23 = bf16[8,20,32,128]{3,2,1,0:T(8,128)(2,1)S(1)} collective-permute-done((bf16[8,20,32,128]{3,2,1,0:T(8,128)(2,1)S(1)}, bf16[8,20,32,128]{3,2,1,0:T(8,128)(2,1)S(1)}, u32[]{:S(2)}, u32[]{:S(2)}) %collective-permute-start.23) | collective-permute-done | bytes 1310752 | tf_op jit(solution)/shard_map/ppermute | solution.py:607
  146.5 7.8 %collective-permute-done.18 = bf16[8,20,32,128]{3,2,1,0:T(8,128)(2,1)S(1)} collective-permute-done((bf16[8,20,32,128]{3,2,1,0:T(8,128)(2,1)S(1)}, bf16[8,20,32,128]{3,2,1,0:T(8,128)(2,1)S(1)}, u32[]{:S(2)}, u32[]{:S(2)}) %collective-permute-start.18) | collective-permute-done | bytes 1310752 | tf_op jit(solution)/shard_map/ppermute | solution.py:607
  161.7 13.2 %attention_forward.1 = (bf16[960,512]{1,0:T(8,128)(2,1)}, f32[16,512]{1,0:T(8,128)}) custom-call(s32[16]{0:T(128)} %starts_ref.3, s32[16]{0:T(128)} %fills_ref.3, s32[1]{0:T(128)} %bitcast.place_ref, bf16[960,512]{1,0:T(8,128)(2,1)} %bitcast.76, bf16[2048,640]{1,0:T(8,128)(2,1)} %all-gather.2.cloned.1.call-done.kv_ref), custom_call_target="tpu_custom_call" | custom-call | tf_op jit(solution)/shard_map/attention_forward/pallas_call | solution.py:422
  174.9 3.2 multiply_reduce_fusion.2
  182.9 47.3 %feedforward.1 = (f32[512,1024]{1,0:T(8,128)}, f32[512,1024]{1,0:T(8,128)}, bf16[16,20,32,128]{3,2,1,0:T(8,128)(2,1)}, bf16[16,20,32,128]{3,2,1,0:T(8,128)(2,1)}...) custom-call(s32[96]{0:T(128)} %pad_add_fusion.table_ref, ...), custom_call_target="tpu_custom_call" | custom-call | tf_op jit(solution)/shard_map/feedforward/pallas_call | solution.py:1101
  230.2 4.0 collective-permute-start.45
  243.8 16.4 %attention_backward.1 = (bf16[960,512]{1,0:T(8,128)(2,1)}, bf16[2048,640]{1,0:T(8,128)(2,1)}) custom-call(s32[16]{0:T(128)} %starts_ref.3, s32[16]{0:T(128)} %fills_ref.3, s32[1]{0:T(128)} %bitcast.place_ref, bf16[960,512]{1,0:T(8,128)(2,1)} %bitcast.77, bf16[960,512]{1,0:T(8,128)(2,1)} %convolution_convert_fusion.3.upstream_ref, ...), custom_call_target="tpu_custom_call" | custom-call | tf_op jit(solution)/shard_map/attention_backward/pallas_call | solution.py:549
  263.1 6.4 %collective-permute-start.46 = (bf16[8,20,32,128]{3,2,1,0:T(8,128)(2,1)S(1)}, bf16[8,20,32,128]{3,2,1,0:T(8,128)(2,1)S(1)}, u32[]{:S(2)}, u32[]{:S(2)}) collective-permute-start(bf16[8,20,32,128]{3,2,1,0:T(8,128)(2,1)S(1)} %get-tuple-element.121), channel_id=1, source_target_pairs={{0,2},{1,3},{2,0},{3,1},{4,6},{5,7},{6,4},{7,5},{8,10},{9,11},{10,... | collective-permute-start | bytes 3932168 | tf_op jit(solution)/shard_map/ppermute | solution.py:607
  274.0 55.8 %collective-permute-start.56 = (bf16[8,20,32,128]{3,2,1,0:T(8,128)(2,1)S(1)}, bf16[8,20,32,128]{3,2,1,0:T(8,128)(2,1)S(1)}, u32[]{:S(2)}, u32[]{:S(2)}) collective-permute-start(bf16[8,20,32,128]{3,2,1,0:T(8,128)(2,1)S(1)} %get-tuple-element.117), channel_id=1, source_target_pairs={{0,8},{4,12},{8,0},{12,4},{16,24},{20,28},{24,16},{28,20},{1,9},{5... | collective-permute-start | bytes 3932168 | tf_op jit(solution)/shard_map/ppermute | solution.py:607
  333.9 15.1 %collective-permute-start.52 = (bf16[4,20,32,128]{3,2,1,0:T(8,128)(2,1)}, bf16[4,20,32,128]{3,2,1,0:T(8,128)(2,1)}, u32[]{:S(2)}, u32[]{:S(2)}) collective-permute-start(bf16[4,20,32,128]{3,2,1,0:T(8,128)(2,1)} %get-tuple-element.125), channel_id=1, source_target_pairs={{0,8},{4,12},{8,0},{12,4},{16,24},{20,28},{24,16},{28,20},{1,9},{5... | collective-permute-start | bytes 1966088 | tf_op jit(solution)/shard_map/ppermute | solution.py:607
  356.4 7.3 %collective-permute-start.48 = (bf16[2,20,32,128]{3,2,1,0:T(8,128)(2,1)S(1)}, bf16[2,20,32,128]{3,2,1,0:T(8,128)(2,1)S(1)}, u32[]{:S(2)}, u32[]{:S(2)}) collective-permute-start(bf16[2,20,32,128]{3,2,1,0:T(8,128)(2,1)S(1)} %get-tuple-element.141), channel_id=1, source_target_pairs={{0,8},{4,12},{8,0},{12,4},{16,24},{20,28},{24,16},{28,20},{1,9},{5... | collective-permute-start | bytes 983048 | tf_op jit(solution)/shard_map/ppermute | solution.py:607
  381.8 5.5 %collective-permute-done.59 = bf16[1,20,32,128]{3,2,1,0:T(8,128)(2,1)S(1)} collective-permute-done((bf16[1,20,32,128]{3,2,1,0:T(8,128)(2,1)S(1)}, bf16[1,20,32,128]{3,2,1,0:T(8,128)(2,1)S(1)}, u32[]{:S(2)}, u32[]{:S(2)}) %collective-permute-start.59) | collective-permute-done | bytes 163872 | tf_op jit(solution)/shard_map/ppermute | solution.py:607
  399.5 5.2 %split_attention.1 = (bf16[16,240,128]{2,1,0:T(8,128)(2,1)}, bf16[16,240,128]{2,1,0:T(8,128)(2,1)}, bf16[16,240,128]{2,1,0:T(8,128)(2,1)}, bf16[16,240,128]{2,1,...) custom-call(s32[96]{0:T(128)} %pad_add_fusion.table_ref, ...), custom_call_target="tpu_custom_call" | custom-call | tf_op jit(solution)/shard_map/split_attention/pallas_call | solution.py:940
  404.7 20.0 %collective-permute-start.40 = (bf16[16,160,128]{2,1,0:T(8,128)(2,1)}, bf16[16,160,128]{2,1,0:T(8,128)(2,1)S(1)}, u32[]{:S(2)}, u32[]{:S(2)}) collective-permute-start(bf16[16,160,128]{2,1,0:T(8,128)(2,1)} %get-tuple-element.65), channel_id=1, source_target_pairs={{0,1},{1,0},{2,3},{3,2},{4,5},{5,4},{6,7},{7,6},{8,9},{9,8},{10,11... | collective-permute-start | bytes 1966088 | tf_op jit(solution)/shard_map/ppermute | solution.py:607
  425.2 3.4 add_multiply_fusion
  431.9 6.6 %collective-permute-done.41 = bf16[8,160,128]{2,1,0:T(8,128)(2,1)S(1)} collective-permute-done((bf16[8,160,128]{2,1,0:T(8,128)(2,1)S(1)}, bf16[8,160,128]{2,1,0:T(8,128)(2,1)S(1)}, u32[]{:S(2)}, u32[]{:S(2)}) %collective-permute-start.41) | collective-permute-done | bytes 327712 | tf_op jit(solution)/shard_map/ppermute | solution.py:607
  439.1 7.7 %collective-permute-done.42 = bf16[4,160,128]{2,1,0:T(8,128)(2,1)S(1)} collective-permute-done((bf16[4,160,128]{2,1,0:T(8,128)(2,1)S(1)}, bf16[4,160,128]{2,1,0:T(8,128)(2,1)S(1)}, u32[]{:S(2)}, u32[]{:S(2)}) %collective-permute-start.42) | collective-permute-done | bytes 163872 | tf_op jit(solution)/shard_map/ppermute | solution.py:607
  457.1 3.7 collective-permute-done.33
  (361 shorter events, 189.4 us)
Async XLA Ops:
  7.2 154.5 %all-gather.2.cloned.1.call-start = ((), (), s32[]{:S(2)}) async-start(), calls=%async_computation.1 | async-start | bytes 3276800 | tf_op jit(solution)/shard_map/all_gather | solution.py:1261
  20.3 42.5 %collective-permute-start.20 = (bf16[1,20,32,128]{3,2,1,0:T(8,128)(2,1)}, bf16[1,20,32,128]{3,2,1,0:T(8,128)(2,1)S(1)}, u32[]{:S(2)}, u32[]{:S(2)}) collective-permute-start(bf16[1,20,32,128]{3,2,1,0:T(8,128)(2,1)} %bitcast.84), channel_id=1, source_target_pairs={{0,16},{4,20},{8,24},{12,28},{16,0},{20,4},{24,8},{28,12},{1,17},{... | collective-permute-start | bytes 491528 | tf_op jit(solution)/shard_map/ppermute | solution.py:607
  20.3 53.1 %collective-permute-start.15 = (bf16[1,20,32,128]{3,2,1,0:T(8,128)(2,1)}, bf16[1,20,32,128]{3,2,1,0:T(8,128)(2,1)S(1)}, u32[]{:S(2)}, u32[]{:S(2)}) collective-permute-start(bf16[1,20,32,128]{3,2,1,0:T(8,128)(2,1)} %bitcast.80), channel_id=1, source_target_pairs={{0,16},{4,20},{8,24},{12,28},{16,0},{20,4},{24,8},{28,12},{1,17},{... | collective-permute-start | bytes 491528 | tf_op jit(solution)/shard_map/ppermute | solution.py:607
  60.9 25.9 %collective-permute-start.9 = (bf16[16,240,128]{2,1,0:T(8,128)(2,1)}, bf16[16,240,128]{2,1,0:T(8,128)(2,1)}, u32[]{:S(2)}, u32[]{:S(2)}) collective-permute-start(bf16[16,240,128]{2,1,0:T(8,128)(2,1)} %constant_dynamic-update-slice_fusion.5.refs_2_), channel_id=1, source_target_pairs={{0,1},{1,0},{2,3},{3,2},{4,5},{5,4},{6,7},{7,6},{8,9},{9,8},{10,11... | collective-permute-start | bytes 2949128 | tf_op jit(solution)/shard_map/ppermute | solution.py:607
  61.7 25.1 %collective-permute-start.4 = (bf16[16,240,128]{2,1,0:T(8,128)(2,1)}, bf16[16,240,128]{2,1,0:T(8,128)(2,1)}, u32[]{:S(2)}, u32[]{:S(2)}) collective-permute-start(bf16[16,240,128]{2,1,0:T(8,128)(2,1)} %constant_dynamic-update-slice_fusion.refs_0_), channel_id=1, source_target_pairs={{0,1},{1,0},{2,3},{3,2},{4,5},{5,4},{6,7},{7,6},{8,9},{9,8},{10,11... | collective-permute-start | bytes 2949128 | tf_op jit(solution)/shard_map/ppermute | solution.py:607
  62.8 22.6 %collective-permute-start.14 = (bf16[16,160,128]{2,1,0:T(8,128)(2,1)S(1)}, bf16[16,160,128]{2,1,0:T(8,128)(2,1)S(1)}, u32[]{:S(2)}, u32[]{:S(2)}) collective-permute-start(bf16[16,160,128]{2,1,0:T(8,128)(2,1)S(1)} %constant_dynamic-update-slice_fusion.10.refs_4_), channel_id=1, source_target_pairs={{0,1},{1,0},{2,3},{3,2},{4,5},{5,4},{6,7},{7,6},{8,9},{9,8},{10,11... | collective-permute-start | bytes 1966088 | tf_op jit(solution)/shard_map/ppermute | solution.py:607
  82.5 27.4 %collective-permute-start.22 = (bf16[4,20,32,128]{3,2,1,0:T(8,128)(2,1)}, bf16[4,20,32,128]{3,2,1,0:T(8,128)(2,1)}, u32[]{:S(2)}, u32[]{:S(2)}) collective-permute-start(bf16[4,20,32,128]{3,2,1,0:T(8,128)(2,1)} %pad_maximum_fusion.5), channel_id=1, source_target_pairs={{0,8},{4,12},{8,0},{12,4},{16,24},{20,28},{24,16},{28,20},{1,9},{5... | collective-permute-start | bytes 1966088 | tf_op jit(solution)/shard_map/ppermute | solution.py:607
  86.3 21.3 %collective-permute-start.27 = (bf16[4,20,32,128]{3,2,1,0:T(8,128)(2,1)}, bf16[4,20,32,128]{3,2,1,0:T(8,128)(2,1)}, u32[]{:S(2)}, u32[]{:S(2)}) collective-permute-start(bf16[4,20,32,128]{3,2,1,0:T(8,128)(2,1)} %pad_maximum_fusion.6), channel_id=1, source_target_pairs={{0,2},{1,3},{2,0},{3,1},{4,6},{5,7},{6,4},{7,5},{8,10},{9,11},{10,... | collective-permute-start | bytes 1966088 | tf_op jit(solution)/shard_map/ppermute | solution.py:607
  101.0 289.6 %reduce-scatter.2.cloned.1.call-start = ((), (), s32[]{:S(2)}) async-start(), calls=%async_computation.2 | async-start | bytes 3276800 | tf_op jit(solution)/shard_map/reduce_scatter | solution.py:1335
  108.9 28.4 %collective-permute-start.28 = (bf16[8,20,32,128]{3,2,1,0:T(8,128)(2,1)S(1)}, bf16[8,20,32,128]{3,2,1,0:T(8,128)(2,1)S(1)}, u32[]{:S(2)}, u32[]{:S(2)}) collective-permute-start(bf16[8,20,32,128]{3,2,1,0:T(8,128)(2,1)S(1)} %pad_maximum_fusion.2), channel_id=1, source_target_pairs={{0,8},{4,12},{8,0},{12,4},{16,24},{20,28},{24,16},{28,20},{1,9},{5... | collective-permute-start | bytes 3932168 | tf_op jit(solution)/shard_map/ppermute | solution.py:607
  111.3 33.9 %collective-permute-start.23 = (bf16[8,20,32,128]{3,2,1,0:T(8,128)(2,1)S(1)}, bf16[8,20,32,128]{3,2,1,0:T(8,128)(2,1)S(1)}, u32[]{:S(2)}, u32[]{:S(2)}) collective-permute-start(bf16[8,20,32,128]{3,2,1,0:T(8,128)(2,1)S(1)} %pad_maximum_fusion.1), channel_id=1, source_target_pairs={{0,4},{4,0},{8,12},{12,8},{16,20},{20,16},{24,28},{28,24},{1,5},{5... | collective-permute-start | bytes 3932168 | tf_op jit(solution)/shard_map/ppermute | solution.py:607
  120.0 34.3 %collective-permute-start.18 = (bf16[8,20,32,128]{3,2,1,0:T(8,128)(2,1)S(1)}, bf16[8,20,32,128]{3,2,1,0:T(8,128)(2,1)S(1)}, u32[]{:S(2)}, u32[]{:S(2)}) collective-permute-start(bf16[8,20,32,128]{3,2,1,0:T(8,128)(2,1)S(1)} %pad_maximum_fusion), channel_id=1, source_target_pairs={{0,2},{1,3},{2,0},{3,1},{4,6},{5,7},{6,4},{7,5},{8,10},{9,11},{10,... | collective-permute-start | bytes 3932168 | tf_op jit(solution)/shard_map/ppermute | solution.py:607
  138.6 44.3 %collective-permute-start.29 = (bf16[16,20,32,128]{3,2,1,0:T(8,128)(2,1)}, bf16[16,20,32,128]{3,2,1,0:T(8,128)(2,1)}, u32[]{:S(2)}, u32[]{:S(2)}) collective-permute-start(bf16[16,20,32,128]{3,2,1,0:T(8,128)(2,1)} %constant_dynamic-update-slice_fusion.25.refs_4_), channel_id=1, source_target_pairs={{0,1},{1,0},{2,3},{3,2},{4,5},{5,4},{6,7},{7,6},{8,9},{9,8},{10,11... | collective-permute-start | bytes 7864328 | tf_op jit(solution)/shard_map/ppermute | solution.py:607
  146.5 36.4 %collective-permute-start.24 = (bf16[16,20,32,128]{3,2,1,0:T(8,128)(2,1)}, bf16[16,20,32,128]{3,2,1,0:T(8,128)(2,1)}, u32[]{:S(2)}, u32[]{:S(2)}) collective-permute-start(bf16[16,20,32,128]{3,2,1,0:T(8,128)(2,1)} %constant_dynamic-update-slice_fusion.20.refs_2_), channel_id=1, source_target_pairs={{0,1},{1,0},{2,3},{3,2},{4,5},{5,4},{6,7},{7,6},{8,9},{9,8},{10,11... | collective-permute-start | bytes 7864328 | tf_op jit(solution)/shard_map/ppermute | solution.py:607
  155.6 27.2 %collective-permute-start.19 = (bf16[16,20,32,128]{3,2,1,0:T(8,128)(2,1)}, bf16[16,20,32,128]{3,2,1,0:T(8,128)(2,1)}, u32[]{:S(2)}, u32[]{:S(2)}) collective-permute-start(bf16[16,20,32,128]{3,2,1,0:T(8,128)(2,1)} %constant_dynamic-update-slice_fusion.15.refs_0_), channel_id=1, source_target_pairs={{0,1},{1,0},{2,3},{3,2},{4,5},{5,4},{6,7},{7,6},{8,9},{9,8},{10,11... | collective-permute-start | bytes 7864328 | tf_op jit(solution)/shard_map/ppermute | solution.py:607
  230.2 30.0 %collective-permute-start.45 = (bf16[16,20,32,128]{3,2,1,0:T(8,128)(2,1)}, bf16[16,20,32,128]{3,2,1,0:T(8,128)(2,1)}, u32[]{:S(2)}, u32[]{:S(2)}) collective-permute-start(bf16[16,20,32,128]{3,2,1,0:T(8,128)(2,1)} %get-tuple-element.68), channel_id=1, source_target_pairs={{0,1},{1,0},{2,3},{3,2},{4,5},{5,4},{6,7},{7,6},{8,9},{9,8},{10,11... | collective-permute-start | bytes 7864328 | tf_op jit(solution)/shard_map/ppermute | solution.py:607
  234.2 35.4 %collective-permute-start.50 = (bf16[16,20,32,128]{3,2,1,0:T(8,128)(2,1)}, bf16[16,20,32,128]{3,2,1,0:T(8,128)(2,1)}, u32[]{:S(2)}, u32[]{:S(2)}) collective-permute-start(bf16[16,20,32,128]{3,2,1,0:T(8,128)(2,1)} %get-tuple-element.70), channel_id=1, source_target_pairs={{0,1},{1,0},{2,3},{3,2},{4,5},{5,4},{6,7},{7,6},{8,9},{9,8},{10,11... | collective-permute-start | bytes 7864328 | tf_op jit(solution)/shard_map/ppermute | solution.py:607
  234.2 37.5 %collective-permute-start.55 = (bf16[16,20,32,128]{3,2,1,0:T(8,128)(2,1)}, bf16[16,20,32,128]{3,2,1,0:T(8,128)(2,1)}, u32[]{:S(2)}, u32[]{:S(2)}) collective-permute-start(bf16[16,20,32,128]{3,2,1,0:T(8,128)(2,1)} %get-tuple-element.72), channel_id=1, source_target_pairs={{0,1},{1,0},{2,3},{3,2},{4,5},{5,4},{6,7},{7,6},{8,9},{9,8},{10,11... | collective-permute-start | bytes 7864328 | tf_op jit(solution)/shard_map/ppermute | solution.py:607
  263.1 66.7 %collective-permute-start.46 = (bf16[8,20,32,128]{3,2,1,0:T(8,128)(2,1)S(1)}, bf16[8,20,32,128]{3,2,1,0:T(8,128)(2,1)S(1)}, u32[]{:S(2)}, u32[]{:S(2)}) collective-permute-start(bf16[8,20,32,128]{3,2,1,0:T(8,128)(2,1)S(1)} %get-tuple-element.121), channel_id=1, source_target_pairs={{0,2},{1,3},{2,0},{3,1},{4,6},{5,7},{6,4},{7,5},{8,10},{9,11},{10,... | collective-permute-start | bytes 3932168 | tf_op jit(solution)/shard_map/ppermute | solution.py:607
  271.7 61.0 %collective-permute-start.51 = (bf16[8,20,32,128]{3,2,1,0:T(8,128)(2,1)S(1)}, bf16[8,20,32,128]{3,2,1,0:T(8,128)(2,1)S(1)}, u32[]{:S(2)}, u32[]{:S(2)}) collective-permute-start(bf16[8,20,32,128]{3,2,1,0:T(8,128)(2,1)S(1)} %get-tuple-element.119), channel_id=1, source_target_pairs={{0,4},{4,0},{8,12},{12,8},{16,20},{20,16},{24,28},{28,24},{1,5},{5... | collective-permute-start | bytes 3932168 | tf_op jit(solution)/shard_map/ppermute | solution.py:607
  274.0 74.9 %collective-permute-start.56 = (bf16[8,20,32,128]{3,2,1,0:T(8,128)(2,1)S(1)}, bf16[8,20,32,128]{3,2,1,0:T(8,128)(2,1)S(1)}, u32[]{:S(2)}, u32[]{:S(2)}) collective-permute-start(bf16[8,20,32,128]{3,2,1,0:T(8,128)(2,1)S(1)} %get-tuple-element.117), channel_id=1, source_target_pairs={{0,8},{4,12},{8,0},{12,4},{16,24},{20,28},{24,16},{28,20},{1,9},{5... | collective-permute-start | bytes 3932168 | tf_op jit(solution)/shard_map/ppermute | solution.py:607
  331.0 24.0 %collective-permute-start.47 = (bf16[4,20,32,128]{3,2,1,0:T(8,128)(2,1)}, bf16[4,20,32,128]{3,2,1,0:T(8,128)(2,1)}, u32[]{:S(2)}, u32[]{:S(2)}) collective-permute-start(bf16[4,20,32,128]{3,2,1,0:T(8,128)(2,1)} %get-tuple-element.127), channel_id=1, source_target_pairs={{0,4},{4,0},{8,12},{12,8},{16,20},{20,16},{24,28},{28,24},{1,5},{5... | collective-permute-start | bytes 1966088 | tf_op jit(solution)/shard_map/ppermute | solution.py:607
  333.9 31.0 %collective-permute-start.52 = (bf16[4,20,32,128]{3,2,1,0:T(8,128)(2,1)}, bf16[4,20,32,128]{3,2,1,0:T(8,128)(2,1)}, u32[]{:S(2)}, u32[]{:S(2)}) collective-permute-start(bf16[4,20,32,128]{3,2,1,0:T(8,128)(2,1)} %get-tuple-element.125), channel_id=1, source_target_pairs={{0,8},{4,12},{8,0},{12,4},{16,24},{20,28},{24,16},{28,20},{1,9},{5... | collective-permute-start | bytes 1966088 | tf_op jit(solution)/shard_map/ppermute | solution.py:607
  404.7 23.9 %collective-permute-start.40 = (bf16[16,160,128]{2,1,0:T(8,128)(2,1)}, bf16[16,160,128]{2,1,0:T(8,128)(2,1)S(1)}, u32[]{:S(2)}, u32[]{:S(2)}) collective-permute-start(bf16[16,160,128]{2,1,0:T(8,128)(2,1)} %get-tuple-element.65), channel_id=1, source_target_pairs={{0,1},{1,0},{2,3},{3,2},{4,5},{5,4},{6,7},{7,6},{8,9},{9,8},{10,11... | collective-permute-start | bytes 1966088 | tf_op jit(solution)/shard_map/ppermute | solution.py:607
  (99 other events, 1173.6 us)
Sparse Core Ops, SparseCore 0:
  101.1 33.6 all-gather.1
  260.3 108.1 reduce-scatter.1

commit v2 on v1

--- a/solution.py
+++ b/solution.py
@@ -351,6 +351,13 @@
     lax.fori_loop(0, tiles, body, 0)
 
 
+def lay_out_kv(blocks, kv_ref, place):
+    size = blocks[0].shape[0]
+    for apart, block in enumerate(blocks):
+        spot = apart if len(blocks) == 1 else place ^ apart
+        kv_ref[pl.ds(pl.multiple_of(spot * size, TILE), size), :] = block[...]
+
+
 def heads_beside(ref, h):
     return jnp.concatenate(
         [
@@ -362,13 +369,16 @@
 
 
 def attention_forward_kernel(
-    starts_ref, fills_ref, place_ref, query_ref, kv_ref, mixed_ref, log_ref, turned, pairs, tops, totals, sums
+    starts_ref, fills_ref, place_ref, query_ref, *refs
 ):
+    kv_blocks = refs[:-8]
+    mixed_ref, log_ref, kv_ref, turned, pairs, tops, totals, sums = refs[-8:]
     i = pl.program_id(0)
     block = place_ref[0] * (TOK_DEV // BLK) + i
 
     @pl.when(i == 0)
     def _():
+        lay_out_kv(kv_blocks, kv_ref, place_ref[0])
         transpose_kv(kv_ref, turned, kv_ref.shape[0] // TILE)
 
     for h in range(KEY_VALUE_HEADS):
@@ -418,15 +428,16 @@
 
 
 def attention_forward(starts, fills, place, query, kv):
-    group = kv.shape[0]
+    group = sum(block.shape[0] for block in kv)
     return pl.pallas_call(
         attention_forward_kernel,
         grid_spec=pltpu.PrefetchScalarGridSpec(
             num_scalar_prefetch=3,
             grid=(TOK_DEV // BLK,),
-            in_specs=[token_block(MODEL_WIDTH), whole((group, 2 * KV_WIDTH))],
+            in_specs=[token_block(MODEL_WIDTH)] + [whole(block.shape) for block in kv],
             out_specs=[token_block(MODEL_WIDTH), token_block(16)],
             scratch_shapes=[
+                pltpu.VMEM((group, 2 * KV_WIDTH), bf16),
                 pltpu.VMEM((group // TILE, 2 * KV_WIDTH, TILE), bf16),
                 pltpu.VMEM((KEY_VALUE_HEADS, 2 * HEAD_SIZE, WIDE), bf16),
                 pltpu.VMEM((KEY_VALUE_HEADS, 1, WIDE), f32),
@@ -439,7 +450,7 @@
             jax.ShapeDtypeStruct((16, TOK_DEV), f32),
         ],
         name="attention_forward",
-    )(starts, fills, place, query, kv)
+    )(starts, fills, place, query, *kv)
 
 
 def attention_backward_kernel(
@@ -452,24 +463,28 @@
     log_ref,
     cosine_ref,
     sine_ref,
-    kv_ref,
-    d_query_ref,
-    d_kv_ref,
-    turned,
-    pairs,
-    query_rows,
-    upstream_rows,
-    deltas,
-    logs,
-    sums,
-    kv_sums,
+    *refs,
 ):
+    count = (len(refs) - 10) // 2
+    kv_blocks, d_query_ref, d_kv_blocks = refs[:count], refs[count], refs[count + 1 : 2 * count + 1]
+    (
+        kv_ref,
+        turned,
+        pairs,
+        query_rows,
+        upstream_rows,
+        deltas,
+        logs,
+        sums,
+        kv_sums,
+    ) = refs[2 * count + 1 :]
     i = pl.program_id(0)
     block = place_ref[0] * (TOK_DEV // BLK) + i
     tiles = kv_ref.shape[0] // TILE
 
     @pl.when(i == 0)
     def _():
+        lay_out_kv(kv_blocks, kv_ref, place_ref[0])
         transpose_kv(kv_ref, turned, tiles)
 
         def clear(t, carry):
@@ -534,17 +549,23 @@
 
     @pl.when(i == pl.num_programs(0) - 1)
     def _():
-        def emit(t, carry):
-            rows = pl.ds(pl.multiple_of(t * TILE, TILE), TILE)
-            for h in range(KEY_VALUE_HEADS):
-                d_kv_ref[rows, 128 * h : 128 * h + 128] = kv_sums[h, rows, :].astype(bf16)
-            return carry
-
-        lax.fori_loop(0, tiles, emit, 0)
+        size = kv_blocks[0].shape[0]
+        for apart, block in enumerate(d_kv_blocks):
+            spot = apart if count == 1 else place_ref[0] ^ apart
+
+            def emit(t, carry):
+                rows = pl.ds(pl.multiple_of(spot * size + t * TILE, TILE), TILE)
+                for h in range(KEY_VALUE_HEADS):
+                    block[pl.ds(pl.multiple_of(t * TILE, TILE), TILE), 128 * h : 128 * h + 128] = (
+                        kv_sums[h, rows, :].astype(bf16)
+                    )
+                return carry
+
+            lax.fori_loop(0, size // TILE, emit, 0)
 
 
 def attention_backward(starts, fills, place, query, upstream, mixed, logs, cosine, sine, kv):
-    group = kv.shape[0]
+    group = sum(block.shape[0] for block in kv)
     half = HEAD_SIZE // 2
     return pl.pallas_call(
         attention_backward_kernel,
@@ -558,10 +579,11 @@
                 token_block(16),
                 token_block(half),
                 token_block(half),
-                whole((group, 2 * KV_WIDTH)),
-            ],
-            out_specs=[token_block(MODEL_WIDTH), whole((group, 2 * KV_WIDTH))],
+            ]
+            + [whole(block.shape) for block in kv],
+            out_specs=[token_block(MODEL_WIDTH)] + [whole(block.shape) for block in kv],
             scratch_shapes=[
+                pltpu.VMEM((group, 2 * KV_WIDTH), bf16),
                 pltpu.VMEM((group // TILE, 2 * KV_WIDTH, TILE), bf16),
                 pltpu.VMEM((KEY_VALUE_HEADS, 2 * HEAD_SIZE, 2 * WIDE), bf16),
                 pltpu.VMEM((KEY_VALUE_HEADS, WIDE, 128), bf16),
@@ -574,10 +596,10 @@
         ),
         out_shape=[
             jax.ShapeDtypeStruct((MODEL_WIDTH, TOK_DEV), bf16),
-            jax.ShapeDtypeStruct((group, 2 * KV_WIDTH), bf16),
-        ],
+        ]
+        + [jax.ShapeDtypeStruct(block.shape, bf16) for block in kv],
         name="attention_backward",
-    )(starts, fills, place, query, upstream, mixed, logs, cosine, sine, kv)
+    )(starts, fills, place, query, upstream, mixed, logs, cosine, sine, *kv)
 
 
 def dot_of(left, right, left_dim, right_dim):
@@ -593,7 +615,8 @@
 PAD_WIDTH = 1024
 CHUNK = 640
 CORE_BIT = ("shard", 1)
-NEAR_BITS = (("shard", 2), ("dp", 1), ("dp", 2))
+ROW_BIT = ("shard", 2)
+NEAR_BITS = (ROW_BIT, ("dp", 1), ("dp", 2))
 FAR_BITS = (("dp", 4),)
 
 
@@ -751,16 +774,15 @@
     return [((80 * c + 16 * m) // 32, (80 * c + 16 * m) % 32, 16 * m) for m in range(5)]
 
 
-def form_feedforward_kernel(narrow_ref, lines_ref, *refs):
-    outs, mid = refs[:SLOTS], refs[SLOTS]
-    for s, out in enumerate(outs):
+def form_feedforward_kernel(narrow_ref, lines_ref, out, mid):
+    for s in range(SLOTS):
 
         @pl.when(narrow_ref[s] == 1)
         def _():
             mid[30:32, :] = jnp.zeros((2, 128), f32)
             for c in range(20):
                 mid[0:30, :] = lines_ref[pl.ds(LINES * s + c, 30, stride=20), :]
-                out[c] = mid[0:32, :].astype(bf16)
+                out[s, c] = mid[0:32, :].astype(bf16)
 
         @pl.when(narrow_ref[s] == 0)
         def _():
@@ -768,7 +790,7 @@
                 if c == 7:
                     value = jnp.where(lane_low(80), value, 0.0)
                 for k, r, m in wide_pieces(c):
-                    out[k, r : r + 16, :] = value[m : m + 16].astype(bf16)
+                    out[s, k, r : r + 16, :] = value[m : m + 16].astype(bf16)
 
             lines_to_rows_960(lines_ref, LINES * s, 80, mid, store)
 
@@ -777,45 +799,39 @@
     return pl.pallas_call(
         form_feedforward_kernel,
         in_specs=[SMEM_SPEC, pl.BlockSpec((SLOTS * LINES, 128))],
-        out_shape=[jax.ShapeDtypeStruct((20, 32, 128), bf16)] * SLOTS,
+        out_shape=jax.ShapeDtypeStruct((SLOTS, 20, 32, 128), bf16),
         scratch_shapes=[pltpu.VMEM((80, 128), f32)],
         name="form_feedforward",
     )(narrow, lines)
 
 
-def unform_feedforward_kernel(narrow_ref, *refs):
-    pieces, (lines_ref, mid) = refs[: 2 * SLOTS], refs[2 * SLOTS :]
+def unform_feedforward_kernel(narrow_ref, terms, lines_ref, mid):
     for s in range(SLOTS):
-        keep, got = pieces[2 * s], pieces[2 * s + 1]
 
         @pl.when(narrow_ref[s] == 1)
         def _():
             for c in range(20):
-                mid[0:32, :] = keep[c].astype(f32) + got[c].astype(f32)
+                mid[0:32, :] = terms[s, c].astype(f32)
                 lines_ref[pl.ds(LINES * s + c, 30, stride=20), :] = mid[0:30, :]
 
         @pl.when(narrow_ref[s] == 0)
         def _():
             def load(c):
                 return jnp.concatenate(
-                    [
-                        keep[k, r : r + 16, :].astype(f32) + got[k, r : r + 16, :].astype(f32)
-                        for k, r, m in wide_pieces(c)
-                    ],
-                    axis=0,
+                    [terms[s, k, r : r + 16, :].astype(f32) for k, r, m in wide_pieces(c)], axis=0
                 )
 
             rows_to_lines_960(load, lines_ref, LINES * s, 80, mid)
 
 
-def unform_feedforward(narrow, addends):
+def unform_feedforward(narrow, terms):
     return pl.pallas_call(
         unform_feedforward_kernel,
-        in_specs=[SMEM_SPEC] + [pl.BlockSpec((20, 32, 128))] * (2 * SLOTS),
+        in_specs=[SMEM_SPEC, pl.BlockSpec((SLOTS, 20, 32, 128))],
         out_shape=jax.ShapeDtypeStruct((SLOTS * LINES, 128), f32),
         scratch_shapes=[pltpu.VMEM((80, 128), f32)],
         name="unform_feedforward",
-    )(narrow, *addends)
+    )(narrow, terms)
 
 
 def place_attention_kernel(table_ref, *refs):
@@ -953,70 +969,47 @@
     )(table, d_query, d_kv, d_out, gains)
 
 
-def feedforward_kernel(table_ref, hidden_ref, turned_ref, grad_ref, *refs):
-    sources = [refs[2 * s : 2 * s + 2] for s in range(SLOTS)]
-    out_ref, d_hidden_ref = refs[6:8]
-    targets = [refs[8 + 2 * s : 10 + 2 * s] for s in range(SLOTS)]
-    (
-        both_in,
-        down_in,
-        down,
-        inner_rows,
-        inner_turned,
-        d_both,
-        both_out,
-        down_out,
-        in_sem,
-        out_sem,
-    ) = refs[14:]
+def feedforward_kernel(
+    hidden_ref,
+    turned_ref,
+    grad_ref,
+    gate_ref,
+    up_ref,
+    down_ref,
+    out_ref,
+    d_hidden_ref,
+    terms_ref,
+    down,
+    inner_rows,
+    inner_turned,
+    d_both,
+    both_out,
+    down_out,
+    sems,
+):
     q = pl.program_id(0)
     chunks = pl.num_programs(0)
     slot = lax.rem(q, 2)
 
-    def narrow_units(move, chunk, buffer):
-        columns = lambda ref: ref.at[pl.ds(5 * chunk, 5)]
-        for u in range(2 * UNITS):
-            device, s = divmod(u, SLOTS)
-            piece = buffer.at[pl.ds(5 * (u // UNITS), 5), pl.ds(32 * (u % UNITS), 32), :]
-            move(s, table_ref[UNITS * s + device], piece, columns)
-
-    def down_units(move, chunk, buffer):
-        for v in range(8):
-            unit = 2 * UNITS + 8 * chunk + v
-            device = unit // SLOTS
-            for s in range(SLOTS):
-
-                @pl.when(unit - SLOTS * device == s)
-                def _():
-                    move(s, table_ref[UNITS * s + device], buffer.at[v], lambda ref: ref)
-
-    def start_in(chunk, carry):
-        side = lax.rem(chunk, 2)
-        narrow_units(
-            lambda s, place, piece, pick: copy_from(
-                sources[s], place, piece, in_sem.at[side, 0], pick
+    def copies(side, chunk):
+        columns = pl.ds(5 * chunk, 5)
+        return (
+            pltpu.make_async_copy(
+                both_out.at[side, 0], terms_ref.at[pl.ds(0, 32), columns], sems.at[side, 0]
             ),
-            chunk,
-            both_in.at[side],
+            pltpu.make_async_copy(
+                both_out.at[side, 1], terms_ref.at[pl.ds(32, 32), columns], sems.at[side, 1]
+            ),
+            pltpu.make_async_copy(
+                down_out.at[side], terms_ref.at[pl.ds(64 + 8 * chunk, 8)], sems.at[side, 2]
+            ),
         )
-        down_units(
-            lambda s, place, piece, pick: copy_from(
-                sources[s], place, piece, in_sem.at[side, 1], pick
-            ),
-            chunk,
-            down_in.at[side],
-        )
-        return carry
-
-    lax.fori_loop(jnp.where(q == 0, 0, q + 1), jnp.minimum(q + 2, chunks), start_in, 0)
-    wait_for(both_in.at[slot], in_sem.at[slot, 0])
-    wait_for(down_in.at[slot], in_sem.at[slot, 1])
 
     for v in range(8):
         for c in range(8):
             for k, r, m in wide_pieces(c):
-                down[80 * v + m : 80 * v + m + 16, 128 * c : 128 * c + 128] = down_in[
-                    slot, v, k, r : r + 16, :
+                down[80 * v + m : 80 * v + m + 16, 128 * c : 128 * c + 128] = down_ref[
+                    v, k, r : r + 16, :
                 ]
 
     @pl.when(q == 0)
@@ -1026,7 +1019,10 @@
 
     def rows_step(i, carry):
         rows = pl.ds(pl.multiple_of(256 * i, 256), 256)
-        weights = jnp.concatenate([both_in[slot, c] for c in range(10)], axis=1)
+        weights = jnp.concatenate(
+            [ref[:, c].reshape(PAD_WIDTH, 128) for ref in (gate_ref, up_ref) for c in range(5)],
+            axis=1,
+        )
         both = jnp.dot(hidden_ref[rows, :], weights, preferred_element_type=f32)
         gate, upper = both[:, :CHUNK], both[:, CHUNK:]
         sigmoid_gate = jax.nn.sigmoid(gate)
@@ -1047,14 +1043,17 @@
 
     @pl.when(q >= 2)
     def _():
-        wait_for(both_out.at[slot], out_sem.at[slot, 0])
-        wait_for(down_out.at[slot], out_sem.at[slot, 1])
+        for copy in copies(slot, q - 2):
+            copy.wait()
 
     def both_step(i, carry):
         rows = pl.ds(pl.multiple_of(256 * i, 256), 256)
-        terms = jnp.dot(turned_ref[rows, :], d_both[...], preferred_element_type=f32)
+        terms = jnp.dot(turned_ref[rows, :], d_both[...], preferred_element_type=f32).astype(bf16)
+        units = pl.ds(8 * i, 8)
         for c in range(10):
-            both_out[slot, c, rows, :] = terms[:, 128 * c : 128 * c + 128].astype(bf16)
+            both_out[slot, c // 5, units, c % 5] = terms[:, 128 * c : 128 * c + 128].reshape(
+                8, 32, 128
+            )
         return carry
 
     lax.fori_loop(0, 4, both_step, 0)
@@ -1073,58 +1072,43 @@
         return carry
 
     lax.fori_loop(0, 2, down_step, 0)
-    narrow_units(
-        lambda s, place, piece, pick: copy_to(
-            piece, targets[s], place, out_sem.at[slot, 0], pick
-        ),
-        q,
-        both_out.at[slot],
-    )
-    down_units(
-        lambda s, place, piece, pick: copy_to(
-            piece, targets[s], place, out_sem.at[slot, 1], pick
-        ),
-        q,
-        down_out.at[slot],
-    )
+    for copy in copies(slot, q):
+        copy.start()
 
     @pl.when(q == chunks - 1)
     def _():
-        for side in range(2):
-            wait_for(both_out.at[side], out_sem.at[side, 0])
-            wait_for(down_out.at[side], out_sem.at[side, 1])
-
-
-def feedforward(table, hidden, turned, grad, gathered):
-    block = jax.ShapeDtypeStruct((16, 20, 32, 128), bf16)
+        for copy in copies(1 - slot, q - 1) + copies(slot, q):
+            copy.wait()
+
+
+def feedforward(hidden, turned, grad, weights):
     full = lambda shape: pl.BlockSpec(shape, lambda q: (0, 0))
     return pl.pallas_call(
         feedforward_kernel,
         grid=(FF // CHUNK,),
         in_specs=[
-            SMEM_SPEC,
             full((TOK_DEV, PAD_WIDTH)),
             full((PAD_WIDTH, TOK_DEV)),
             full((TOK_DEV, PAD_WIDTH)),
-        ]
-        + [ANY_SPEC] * (2 * SLOTS),
-        out_specs=[full((TOK_DEV, PAD_WIDTH))] * 2 + [ANY_SPEC] * (2 * SLOTS),
-        out_shape=[jax.ShapeDtypeStruct((TOK_DEV, PAD_WIDTH), f32)] * 2 + [block] * (2 * SLOTS),
+            pl.BlockSpec((32, 5, 32, 128), lambda q: (0, q, 0, 0)),
+            pl.BlockSpec((32, 5, 32, 128), lambda q: (1, q, 0, 0)),
+            pl.BlockSpec((8, 20, 32, 128), lambda q: (8 + q, 0, 0, 0)),
+        ],
+        out_specs=[full((TOK_DEV, PAD_WIDTH))] * 2 + [ANY_SPEC],
+        out_shape=[jax.ShapeDtypeStruct((TOK_DEV, PAD_WIDTH), f32)] * 2
+        + [jax.ShapeDtypeStruct((3 * UNITS, 20, 32, 128), bf16)],
         scratch_shapes=[
-            pltpu.VMEM((2, 10, PAD_WIDTH, 128), bf16),
-            pltpu.VMEM((2, 8, 20, 32, 128), bf16),
             pltpu.VMEM((CHUNK, PAD_WIDTH), bf16),
             pltpu.VMEM((TOK_DEV, CHUNK), bf16),
             pltpu.VMEM((CHUNK, TOK_DEV), bf16),
             pltpu.VMEM((TOK_DEV, 2 * CHUNK), bf16),
-            pltpu.VMEM((2, 10, PAD_WIDTH, 128), bf16),
+            pltpu.VMEM((2, 2, 32, 5, 32, 128), bf16),
             pltpu.VMEM((2, 8, 20, 32, 128), bf16),
-            pltpu.SemaphoreType.DMA((2, 2)),
-            pltpu.SemaphoreType.DMA((2, 2)),
+            pltpu.SemaphoreType.DMA((2, 3)),
         ],
         compiler_params=pltpu.CompilerParams(vmem_limit_bytes=60 * 2**20),
         name="feedforward",
-    )(table, hidden, turned, grad, *gathered)
+    )(hidden, turned, grad, weights, weights, weights)
 
 
 def spread_matrix():
@@ -1201,7 +1185,7 @@
         pieces = form_attention(wide, master_attention.reshape(LINES, 128), gain_row)
         gathered = [half for k in range(SLOTS) for half in gather_colour(pieces[k], k)]
         forms = form_feedforward(narrow, master_feedforward.reshape(SLOTS * LINES, 128))
-        feedforward_all = [half for k in range(SLOTS) for half in gather_colour(forms[k], k)]
+        feedforward_all = gather_lines(forms.reshape(SLOTS * FORM, 128))
         query_weight, kv_weight, out_weight, gain_rows = place_attention(table, gathered)
         gains_all = gain_rows[:, 64 : 64 + gain_count].reshape(-1)
     else:
@@ -1258,7 +1242,11 @@
     keys = rotate(kv_turned[:, 0], 1.0).reshape(KEY_VALUE_HEADS, 1, HEAD_SIZE, TOK_DEV)
     values = kv_turned[:, 1:].astype(bf16)
     kv_rows = jnp.concatenate([keys, values], axis=1).reshape(2 * KV_WIDTH, TOK_DEV).T
-    kv_all = lax.all_gather(kv_rows, "shard", axis=0, tiled=True)
+    if in_units:
+        across = swap(kv_rows, ROW_BIT)
+        kv_all = [kv_rows, swap(kv_rows, CORE_BIT), across, swap(across, CORE_BIT)]
+    else:
+        kv_all = [lax.all_gather(kv_rows, "shard", axis=0, tiled=True)]
     query_turned = rotate(
         dot_of(query_weight, first_hidden, 0, 1).reshape(QUERY_HEADS, HEAD_SIZE, TOK_DEV),
         score_scale,
@@ -1273,24 +1261,19 @@
     grad_low = grad_out.astype(bf16)
     if in_units:
         spread = spread_matrix()
-        outcome, d_spread, *ff_terms = feedforward(
-            table,
+        outcome, d_spread, ff_terms = feedforward(
             dot_of(hidden_two, spread, 1, 0).astype(bf16),
             dot_of(spread, hidden_two, 0, 1).astype(bf16),
             jnp.pad(grad_low, ((0, 0), (0, PAD_WIDTH - MODEL_WIDTH))),
-            feedforward_all,
+            feedforward_all.reshape(3 * UNITS, 20, 32, 128),
         )
         layer_output = middle + outcome[:, :MODEL_WIDTH]
         d_coarse = lax.reduce_precision(d_spread, 8, 7)
         d_hidden_two = dot_of(d_coarse.astype(bf16), spread, 1, 1) + dot_of(
             (d_spread - d_coarse).astype(bf16), spread, 1, 1
         )
-        ff_addends = [
-            addend
-            for k in range(SLOTS)
-            for addend in scatter_colour(ff_terms[2 * k], ff_terms[2 * k + 1], k)
-        ]
-        feedforward_gradient = unform_feedforward(narrow, ff_addends).reshape(-1)
+        ff_sum = scatter_lines(ff_terms.reshape(SLOTS * UNITS * FORM, 128))
+        feedforward_gradient = unform_feedforward(narrow, ff_sum.reshape(SLOTS, 20, 32, 128)).reshape(-1)
     else:
         gate_weight, up_weight, down_weight = unpack_ff(feedforward_all)
         gate = dot_of(hidden_two, gate_weight, 1, 0)
@@ -1320,7 +1303,7 @@
     d_branch = d_middle.astype(bf16)
     d_out_weight = dot_of(mixed_turned, d_branch, 1, 0).astype(bf16)
     d_mixed = dot_of(out_weight, d_branch, 1, 1).astype(bf16)
-    d_query, d_kv = attention_backward(
+    d_query, *d_kv = attention_backward(
         block_start,
         block_fill,
         place,
@@ -1332,7 +1315,11 @@
         sine_table,
         kv_all,
     )
-    d_kv_rows = lax.psum_scatter(d_kv, "shard", scatter_dimension=0, tiled=True)
+    if in_units:
+        across = d_kv[2] + swap(d_kv[3], CORE_BIT)
+        d_kv_rows = d_kv[0] + swap(d_kv[1], CORE_BIT) + swap(across, ROW_BIT)
+    else:
+        d_kv_rows = lax.psum_scatter(d_kv[0], "shard", scatter_dimension=0, tiled=True)
     d_kv_turned = d_kv_rows.T.reshape(KEY_VALUE_HEADS, 2, HEAD_SIZE, TOK_DEV)
     d_front = d_kv_turned[:, 0, : HEAD_SIZE // 2].astype(f32)
     d_back = d_kv_turned[:, 0, HEAD_SIZE // 2 :].astype(f32)

time: 489 us -> 431 us (0.88)
  starting transfers between devices: 157 us -> 110 us
  waiting for transfers between devices: 85.2 us -> 125 us
  local copies, waits for them, and re-layouts: 45.9 us -> 18.8 us
  other arithmetic: 47.8 us -> 24.8 us
    ppermute x60 -> x36, starting transfers between devices: 157 us -> 110 us  [swap(): return lax.ppermute(value, axis, [(i, i ^ mask) for i in range(size)])]
    ppermute x60 -> x36, waiting for transfers between devices: 85.2 us -> 104 us  [swap(): return lax.ppermute(value, axis, [(i, i ^ mask) for i in range(size)])]
    unnamed x148 -> x113, local copies, waits for them, and re-layouts: 31.1 us -> 12.7 us
    reduce_scatter x1, waiting for transfers between devices: 0.01 us -> 16.6 us  [scatter_lines(): return lax.psum_scatter(lines, ALL_AXES, scatter_dimension=0, tiled=True)]
    concatenate x18 -> x9, other arithmetic: 14.2 us -> 0.25 us  [gather_colour(): held = jnp.concatenate([held, swap(held, bit)], axis=0)]
    add x18 -> x9, other arithmetic: 14.9 us -> 6.06 us  [scatter_colour(): keep = keep[:half] + got[:half]]
    pallas_call x2, Pallas kernels: 49.9 us -> 44.2 us  [the longest x1 41.9 us: feedforward(): pl.pallas_call(feedforward_kernel, grid=(FF // CHUNK,), in_specs=[full((T...]
  transfers between devices with their start and end apart: 62 -> 38, of which waited for: 19 -> 23; matrix products, arithmetic and copies ran while one was open for 23% -> 16% of each run, Pallas kernels for 9% -> 12%
where the time goes in v2:
time: 431 us; the launch traced here: 424 us
  waiting for transfers between devices  125 us (29%)
  starting transfers between devices  110 us (26%)
  Pallas kernels  96.2 us (22%)
  matrix products  33.8 us (8%)
  other arithmetic  24.8 us (6%)
  local copies, waits for them, and re-layouts  18.8 us (4%)
  between operations  15.2 us (4%)
    ppermute x36, starting transfers between devices, swap(): return lax.ppermute(value, axis, [(i, i ^ mask) for i in range(size)])  110 us
    ppermute x36, waiting for transfers between devices, swap(): return lax.ppermute(value, axis, [(i, i ^ mask) for i in range(size)])  104 us
    pallas_call x1, Pallas kernels, feedforward(): pl.pallas_call(feedforward_kernel, grid=(FF // CHUNK,), in_specs=[full((T...  41.9 us
    dot_general x13, matrix products, dot_of(): lax.dot_general(left, right, (((left_dim,), (right_dim,)), ((), ())), pre...  33.8 us
    pallas_call x1, Pallas kernels, attention_backward(): pl.pallas_call(attention_backward_kernel, grid_spec=pltpu.PrefetchScalarG...  18.4 us
    reduce_scatter x1, waiting for transfers between devices, scatter_lines(): return lax.psum_scatter(lines, ALL_AXES, scatter_dimension=0, tiled=True)  16.6 us
    pallas_call x1, Pallas kernels, attention_forward(): pl.pallas_call(attention_forward_kernel, grid_spec=pltpu.PrefetchScalarGr...  14.9 us
    unnamed x113, local copies, waits for them, and re-layouts  12.7 us
  transfers between devices with their start and end apart: 38, of which 23 were waited for; matrix products, arithmetic and copies ran while one was open for 16% of the time, Pallas kernels for 12%

profile of v2, /device:TPU:0, one launch (start us, length us, event | category | flops | bytes accessed | tf_op | source)
XLA Modules:
  0.0 423.8 jit_solution(6442953145073277215)
XLA Ops:
  13.2 4.1 collective-permute-start.10
  28.1 3.8 collective-permute-done.6
  33.4 4.5 %collective-permute-done.1 = bf16[2,240,128]{2,1,0:T(8,128)(2,1)S(1)} collective-permute-done((bf16[2,240,128]{2,1,0:T(8,128)(2,1)S(1)}, bf16[2,240,128]{2,1,0:T(8,128)(2,1)S(1)}, u32[]{:S(2)}, u32[]{:S(2)}) %collective-permute-start.1) | collective-permute-done | bytes 122912 | tf_op jit(solution)/shard_map/ppermute | solution.py:630
  40.7 3.9 collective-permute-done.7
  48.2 16.9 %collective-permute-done.8 = bf16[8,240,128]{2,1,0:T(8,128)(2,1)S(1)} collective-permute-done((bf16[8,240,128]{2,1,0:T(8,128)(2,1)S(1)}, bf16[8,240,128]{2,1,0:T(8,128)(2,1)S(1)}, u32[]{:S(2)}, u32[]{:S(2)}) %collective-permute-start.8) | collective-permute-done | bytes 491552 | tf_op jit(solution)/shard_map/ppermute | solution.py:630
  73.9 7.1 %place_attention.1 = (bf16[960,960]{1,0:T(8,128)(2,1)}, bf16[960,640]{1,0:T(8,128)(2,1)}, bf16[960,960]{1,0:T(8,128)(2,1)}, f32[32,128]{1,0:T(8,128)}) custom-call(s32[96]{0:T(128)} %pad_add_fusion.table_ref, bf16[16,240,128]{2,1,0:T(8,128)(2,1)} %copy-done.19, bf16[16,240,128]{2,1,0:T(8,128)(2,1)} %collective-permute-done.4.refs_1_, ...), custom_call_target="tpu_custom_call" | custom-call | tf_op jit(solution)/shard_map/place_attention/pallas_call | solution.py:886
  90.6 24.5 %collective-permute-done.16.refs_2_ = bf16[512,640]{1,0:T(8,128)(2,1)S(1)} collective-permute-done((bf16[512,640]{1,0:T(8,128)(2,1)S(1)}, bf16[512,640]{1,0:T(8,128)(2,1)S(1)}, u32[]{:S(2)}, u32[]{:S(2)}) %collective-permute-start.16) | collective-permute-done | bytes 655392 | tf_op jit(solution)/shard_map/ppermute | solution.py:630
  115.1 3.2 fusion.65
  120.7 14.9 %attention_forward.1 = (bf16[960,512]{1,0:T(8,128)(2,1)}, f32[16,512]{1,0:T(8,128)}) custom-call(s32[16]{0:T(128)} %starts_ref.3, s32[16]{0:T(128)} %fills_ref.3, s32[1]{0:T(128)} %bitcast.place_ref, bf16[960,512]{1,0:T(8,128)(2,1)} %bitcast.70, bf16[512,640]{1,0:T(8,128)(2,1)} %bitcast.74, bf16[512,640]{1,0:T(8,128)(2,1)} %collective-permute-done.15.refs_1_, ...), custom_call_target="tpu_custom_call" | custom-call | tf_op jit(solution)/shard_map/attention_forward/pallas_call | solution.py:432
  135.7 3.3 multiply_reduce_fusion.2
  143.8 3.7 all-gather.2.cloned.1.call-done
  147.5 41.9 %feedforward.1 = (f32[512,1024]{1,0:T(8,128)}, f32[512,1024]{1,0:T(8,128)}, bf16[96,20,32,128]{3,2,1,0:T(8,128)(2,1)}) custom-call(bf16[512,1024]{1,0:T(8,128)(2,1)} %fusion.27.hidden_ref, bf16[1024,512]{1,0:T(8,128)(2,1)} %fusion.24.turned_ref, bf16[512,1024]{1,0:T(8,128)(2,1)} %pad.13.grad_ref, bf16[96,20,32,128]{3,2,1,0:T(8,128)(2,1)} %bitcast.66, ...), custom_call_target="tpu_custom_call" | custom-call | tf_op jit(solution)/shard_map/feedforward/pallas_call | solution.py:1086
  198.6 18.4 %attention_backward.1 = (bf16[960,512]{1,0:T(8,128)(2,1)}, bf16[512,640]{1,0:T(8,128)(2,1)}, bf16[512,640]{1,0:T(8,128)(2,1)}, bf16[512,640]{1,0:T(8,128)(2,1)}, bf16[512,640]{1,0:T(8,128)(2,1)}) custom-call(s32[16]{0:T(128)} %starts_ref.3, s32[16]{0:T(128)} %fills_ref.3, s32[1]{0:T(128)} %bitcast.place_ref, bf16[960,512]{1,0:T(8,128)(2,1)} %bitcast.71, ...), custom_call_target="tpu_custom_call" | custom-call | tf_op jit(solution)/shard_map/attention_backward/pallas_call | solution.py:570
  217.0 3.4 collective-permute-start.19
  223.5 6.2 %collective-permute-start.20 = (bf16[512,640]{1,0:T(8,128)(2,1)S(1)}, bf16[512,640]{1,0:T(8,128)(2,1)S(1)}, u32[]{:S(2)}, u32[]{:S(2)}) collective-permute-start(bf16[512,640]{1,0:T(8,128)(2,1)S(1)} %add.330), channel_id=1, source_target_pairs={{0,2},{1,3},{2,0},{3,1},{4,6},{5,7},{6,4},{7,5},{8,10},{9,11},{10,... | collective-permute-start | bytes 1966088 | tf_op jit(solution)/shard_map/ppermute | solution.py:630
  229.7 4.3 %convolution_convert_fusion.1.query_ref = bf16[960,960]{1,0:T(8,128)(2,1)} fusion(bf16[960,512]{1,0:T(8,128)(2,1)} %get-tuple-element.50, bf16[512,960]{1,0:T(8,128)(2,1)S(1)} %copy.43, f32[960]{0:T(1024)S(1)} %mul.415, f32[512]{0:T(512)S(1)} %copy-done.37), kind=kOutput, calls=%fused_computation.36 | convolution fusion | flops 946606080 | bytes 3815168 | tf_op jit(solution)/shard_map/dot_general | solution.py:606
  236.6 8.3 %collective-permute-done.20 = bf16[512,640]{1,0:T(8,128)(2,1)S(1)} collective-permute-done((bf16[512,640]{1,0:T(8,128)(2,1)S(1)}, bf16[512,640]{1,0:T(8,128)(2,1)S(1)}, u32[]{:S(2)}, u32[]{:S(2)}) %collective-permute-start.20) | collective-permute-done | bytes 655392 | tf_op jit(solution)/shard_map/ppermute | solution.py:630
  254.1 5.6 %split_attention.1 = (bf16[16,240,128]{2,1,0:T(8,128)(2,1)}, bf16[16,240,128]{2,1,0:T(8,128)(2,1)}, bf16[16,240,128]{2,1,0:T(8,128)(2,1)}, bf16[16,240,128]{2,1,...) custom-call(s32[96]{0:T(128)} %pad_add_fusion.table_ref, ...), custom_call_target="tpu_custom_call" | custom-call | tf_op jit(solution)/shard_map/split_attention/pallas_call | solution.py:956
  266.1 8.3 %collective-permute-done.32 = bf16[8,160,128]{2,1,0:T(8,128)(2,1)} collective-permute-done((bf16[8,160,128]{2,1,0:T(8,128)(2,1)}, bf16[8,160,128]{2,1,0:T(8,128)(2,1)}, u32[]{:S(2)}, u32[]{:S(2)}) %collective-permute-start.32) | collective-permute-done | bytes 327712 | tf_op jit(solution)/shard_map/ppermute | solution.py:630
  281.1 61.3 %collective-permute-start.27 = (bf16[8,240,128]{2,1,0:T(8,128)(2,1)S(1)}, bf16[8,240,128]{2,1,0:T(8,128)(2,1)S(1)}, u32[]{:S(2)}, u32[]{:S(2)}) collective-permute-start(bf16[8,240,128]{2,1,0:T(8,128)(2,1)S(1)} %get-tuple-element.111), channel_id=1, source_target_pairs={{0,4},{4,0},{8,12},{12,8},{16,20},{20,16},{24,28},{28,24},{1,5},{5... | collective-permute-start | bytes 1474568 | tf_op jit(solution)/shard_map/ppermute | solution.py:630
  343.9 9.5 %collective-permute-start.23 = (bf16[4,240,128]{2,1,0:T(8,128)(2,1)S(1)}, bf16[4,240,128]{2,1,0:T(8,128)(2,1)S(1)}, u32[]{:S(2)}, u32[]{:S(2)}) collective-permute-start(bf16[4,240,128]{2,1,0:T(8,128)(2,1)S(1)} %get-tuple-element.119), channel_id=1, source_target_pairs={{0,4},{4,0},{8,12},{12,8},{16,20},{20,16},{24,28},{28,24},{1,5},{5... | collective-permute-start | bytes 737288 | tf_op jit(solution)/shard_map/ppermute | solution.py:630
  356.9 8.4 %collective-permute-done.23 = bf16[4,240,128]{2,1,0:T(8,128)(2,1)S(1)} collective-permute-done((bf16[4,240,128]{2,1,0:T(8,128)(2,1)S(1)}, bf16[4,240,128]{2,1,0:T(8,128)(2,1)S(1)}, u32[]{:S(2)}, u32[]{:S(2)}) %collective-permute-start.23) | collective-permute-done | bytes 245792 | tf_op jit(solution)/shard_map/ppermute | solution.py:630
  365.4 8.2 %collective-permute-done.28 = bf16[4,240,128]{2,1,0:T(8,128)(2,1)S(1)} collective-permute-done((bf16[4,240,128]{2,1,0:T(8,128)(2,1)S(1)}, bf16[4,240,128]{2,1,0:T(8,128)(2,1)S(1)}, u32[]{:S(2)}, u32[]{:S(2)}) %collective-permute-start.28) | collective-permute-done | bytes 245792 | tf_op jit(solution)/shard_map/ppermute | solution.py:630
  394.5 16.6 %reduce-scatter.2.cloned.1.call-done = bf16[1920,128]{1,0:T(8,128)(2,1)} async-done(((bf16[61440,128]{1,0:T(8,128)(2,1)}), bf16[1920,128]{1,0:T(8,128)(2,1)}) %reduce-scatter.2.cloned.1.call-update) | async-done | bytes 491536 | tf_op jit(solution)/shard_map/reduce_scatter | solution.py:1150
  (256 shorter events, 118.3 us)
Async XLA Ops:
  7.2 140.3 %all-gather.2.cloned.1.call-start = ((), (), s32[]{:S(2)}) async-start(), calls=%async_computation.1 | async-start | bytes 16220160 | tf_op jit(solution)/shard_map/all_gather | solution.py:1146
  10.1 400.9 %reduce-scatter.2.cloned.1.call-start = ((), (), s32[]{:S(2)}) async-start(), calls=%async_computation.2 | async-start | bytes 16220160 | tf_op jit(solution)/shard_map/reduce_scatter | solution.py:1150
  22.5 16.9 %collective-permute-start.11 = (bf16[2,160,128]{2,1,0:T(8,128)(2,1)S(1)}, bf16[2,160,128]{2,1,0:T(8,128)(2,1)S(1)}, u32[]{:S(2)}, u32[]{:S(2)}) collective-permute-start(bf16[2,160,128]{2,1,0:T(8,128)(2,1)S(1)} %pad_maximum_fusion.10), channel_id=1, source_target_pairs={{0,4},{4,0},{8,12},{12,8},{16,20},{20,16},{24,28},{28,24},{1,5},{5... | collective-permute-start | bytes 245768 | tf_op jit(solution)/shard_map/ppermute | solution.py:630
  27.1 10.8 %collective-permute-start.1 = (bf16[2,240,128]{2,1,0:T(8,128)(2,1)S(1)}, bf16[2,240,128]{2,1,0:T(8,128)(2,1)S(1)}, u32[]{:S(2)}, u32[]{:S(2)}) collective-permute-start(bf16[2,240,128]{2,1,0:T(8,128)(2,1)S(1)} %pad_maximum_fusion.8), channel_id=1, source_target_pairs={{0,8},{4,12},{8,0},{12,4},{16,24},{20,28},{24,16},{28,20},{1,9},{5... | collective-permute-start | bytes 368648 | tf_op jit(solution)/shard_map/ppermute | solution.py:630
  31.9 12.7 %collective-permute-start.7 = (bf16[4,240,128]{2,1,0:T(8,128)(2,1)S(1)}, bf16[4,240,128]{2,1,0:T(8,128)(2,1)S(1)}, u32[]{:S(2)}, u32[]{:S(2)}) collective-permute-start(bf16[4,240,128]{2,1,0:T(8,128)(2,1)S(1)} %pad_maximum_fusion.6), channel_id=1, source_target_pairs={{0,8},{4,12},{8,0},{12,4},{16,24},{20,28},{24,16},{28,20},{1,9},{5... | collective-permute-start | bytes 737288 | tf_op jit(solution)/shard_map/ppermute | solution.py:630
  44.6 20.5 %collective-permute-start.8 = (bf16[8,240,128]{2,1,0:T(8,128)(2,1)S(1)}, bf16[8,240,128]{2,1,0:T(8,128)(2,1)S(1)}, u32[]{:S(2)}, u32[]{:S(2)}) collective-permute-start(bf16[8,240,128]{2,1,0:T(8,128)(2,1)S(1)} %pad_maximum_fusion.3), channel_id=1, source_target_pairs={{0,4},{4,0},{8,12},{12,8},{16,20},{20,16},{24,28},{28,24},{1,5},{5... | collective-permute-start | bytes 1474568 | tf_op jit(solution)/shard_map/ppermute | solution.py:630
  46.2 19.5 %collective-permute-start.3 = (bf16[8,240,128]{2,1,0:T(8,128)(2,1)S(1)}, bf16[8,240,128]{2,1,0:T(8,128)(2,1)S(1)}, u32[]{:S(2)}, u32[]{:S(2)}) collective-permute-start(bf16[8,240,128]{2,1,0:T(8,128)(2,1)S(1)} %pad_maximum_fusion.2), channel_id=1, source_target_pairs={{0,2},{1,3},{2,0},{3,1},{4,6},{5,7},{6,4},{7,5},{8,10},{9,11},{10,... | collective-permute-start | bytes 1474568 | tf_op jit(solution)/shard_map/ppermute | solution.py:630
  47.9 21.1 %collective-permute-start.13 = (bf16[8,160,128]{2,1,0:T(8,128)(2,1)S(1)}, bf16[8,160,128]{2,1,0:T(8,128)(2,1)S(1)}, u32[]{:S(2)}, u32[]{:S(2)}) collective-permute-start(bf16[8,160,128]{2,1,0:T(8,128)(2,1)S(1)} %pad_maximum_fusion.4), channel_id=1, source_target_pairs={{0,8},{4,12},{8,0},{12,4},{16,24},{20,28},{24,16},{28,20},{1,9},{5... | collective-permute-start | bytes 983048 | tf_op jit(solution)/shard_map/ppermute | solution.py:630
  84.8 30.3 %collective-permute-start.16 = (bf16[512,640]{1,0:T(8,128)(2,1)S(1)}, bf16[512,640]{1,0:T(8,128)(2,1)S(1)}, u32[]{:S(2)}, u32[]{:S(2)}) collective-permute-start(bf16[512,640]{1,0:T(8,128)(2,1)S(1)} %bitcast.72), channel_id=1, source_target_pairs={{0,2},{1,3},{2,0},{3,1},{4,6},{5,7},{6,4},{7,5},{8,10},{9,11},{10,... | collective-permute-start | bytes 1966088 | tf_op jit(solution)/shard_map/ppermute | solution.py:630
  89.8 30.1 %collective-permute-start.15 = (bf16[512,640]{1,0:T(8,128)(2,1)S(1)}, bf16[512,640]{1,0:T(8,128)(2,1)}, u32[]{:S(2)}, u32[]{:S(2)}) collective-permute-start(bf16[512,640]{1,0:T(8,128)(2,1)S(1)} %bitcast.73), channel_id=1, source_target_pairs={{0,1},{1,0},{2,3},{3,2},{4,5},{5,4},{6,7},{7,6},{8,9},{9,8},{10,11... | collective-permute-start | bytes 1966088 | tf_op jit(solution)/shard_map/ppermute | solution.py:630
  220.4 16.1 %collective-permute-start.18 = (bf16[512,640]{1,0:T(8,128)(2,1)}, bf16[512,640]{1,0:T(8,128)(2,1)S(1)}, u32[]{:S(2)}, u32[]{:S(2)}) collective-permute-start(bf16[512,640]{1,0:T(8,128)(2,1)} %get-tuple-element.52), channel_id=1, source_target_pairs={{0,1},{1,0},{2,3},{3,2},{4,5},{5,4},{6,7},{7,6},{8,9},{9,8},{10,11... | collective-permute-start | bytes 1966088 | tf_op jit(solution)/shard_map/ppermute | solution.py:630
  223.5 21.3 %collective-permute-start.20 = (bf16[512,640]{1,0:T(8,128)(2,1)S(1)}, bf16[512,640]{1,0:T(8,128)(2,1)S(1)}, u32[]{:S(2)}, u32[]{:S(2)}) collective-permute-start(bf16[512,640]{1,0:T(8,128)(2,1)S(1)} %add.330), channel_id=1, source_target_pairs={{0,2},{1,3},{2,0},{3,1},{4,6},{5,7},{6,4},{7,5},{8,10},{9,11},{10,... | collective-permute-start | bytes 1966088 | tf_op jit(solution)/shard_map/ppermute | solution.py:630
  259.8 17.5 %collective-permute-start.21 = (bf16[16,240,128]{2,1,0:T(8,128)(2,1)}, bf16[16,240,128]{2,1,0:T(8,128)(2,1)}, u32[]{:S(2)}, u32[]{:S(2)}) collective-permute-start(bf16[16,240,128]{2,1,0:T(8,128)(2,1)} %get-tuple-element.56), channel_id=1, source_target_pairs={{0,1},{1,0},{2,3},{3,2},{4,5},{5,4},{6,7},{7,6},{8,9},{9,8},{10,11... | collective-permute-start | bytes 2949128 | tf_op jit(solution)/shard_map/ppermute | solution.py:630
  260.3 19.5 %collective-permute-start.26 = (bf16[16,240,128]{2,1,0:T(8,128)(2,1)}, bf16[16,240,128]{2,1,0:T(8,128)(2,1)}, u32[]{:S(2)}, u32[]{:S(2)}) collective-permute-start(bf16[16,240,128]{2,1,0:T(8,128)(2,1)} %get-tuple-element.58), channel_id=1, source_target_pairs={{0,1},{1,0},{2,3},{3,2},{4,5},{5,4},{6,7},{7,6},{8,9},{9,8},{10,11... | collective-permute-start | bytes 2949128 | tf_op jit(solution)/shard_map/ppermute | solution.py:630
  264.3 10.1 %collective-permute-start.32 = (bf16[8,160,128]{2,1,0:T(8,128)(2,1)}, bf16[8,160,128]{2,1,0:T(8,128)(2,1)}, u32[]{:S(2)}, u32[]{:S(2)}) collective-permute-start(bf16[8,160,128]{2,1,0:T(8,128)(2,1)} %get-tuple-element.115), channel_id=1, source_target_pairs={{0,8},{4,12},{8,0},{12,4},{16,24},{20,28},{24,16},{28,20},{1,9},{5... | collective-permute-start | bytes 983048 | tf_op jit(solution)/shard_map/ppermute | solution.py:630
  275.4 67.0 %collective-permute-start.33 = (bf16[4,160,128]{2,1,0:T(8,128)(2,1)S(1)}, bf16[4,160,128]{2,1,0:T(8,128)(2,1)S(1)}, u32[]{:S(2)}, u32[]{:S(2)}) collective-permute-start(bf16[4,160,128]{2,1,0:T(8,128)(2,1)S(1)} %get-tuple-element.125), channel_id=1, source_target_pairs={{0,2},{1,3},{2,0},{3,1},{4,6},{5,7},{6,4},{7,5},{8,10},{9,11},{10,... | collective-permute-start | bytes 491528 | tf_op jit(solution)/shard_map/ppermute | solution.py:630
  278.9 64.9 %collective-permute-start.22 = (bf16[8,240,128]{2,1,0:T(8,128)(2,1)S(1)}, bf16[8,240,128]{2,1,0:T(8,128)(2,1)S(1)}, u32[]{:S(2)}, u32[]{:S(2)}) collective-permute-start(bf16[8,240,128]{2,1,0:T(8,128)(2,1)S(1)} %get-tuple-element.113), channel_id=1, source_target_pairs={{0,2},{1,3},{2,0},{3,1},{4,6},{5,7},{6,4},{7,5},{8,10},{9,11},{10,... | collective-permute-start | bytes 1474568 | tf_op jit(solution)/shard_map/ppermute | solution.py:630
  281.1 73.0 %collective-permute-start.27 = (bf16[8,240,128]{2,1,0:T(8,128)(2,1)S(1)}, bf16[8,240,128]{2,1,0:T(8,128)(2,1)S(1)}, u32[]{:S(2)}, u32[]{:S(2)}) collective-permute-start(bf16[8,240,128]{2,1,0:T(8,128)(2,1)S(1)} %get-tuple-element.111), channel_id=1, source_target_pairs={{0,4},{4,0},{8,12},{12,8},{16,20},{20,16},{24,28},{28,24},{1,5},{5... | collective-permute-start | bytes 1474568 | tf_op jit(solution)/shard_map/ppermute | solution.py:630
  342.4 13.8 %collective-permute-start.34 = (bf16[2,160,128]{2,1,0:T(8,128)(2,1)S(1)}, bf16[2,160,128]{2,1,0:T(8,128)(2,1)S(1)}, u32[]{:S(2)}, u32[]{:S(2)}) collective-permute-start(bf16[2,160,128]{2,1,0:T(8,128)(2,1)S(1)} %get-tuple-element.131), channel_id=1, source_target_pairs={{0,4},{4,0},{8,12},{12,8},{16,20},{20,16},{24,28},{28,24},{1,5},{5... | collective-permute-start | bytes 245768 | tf_op jit(solution)/shard_map/ppermute | solution.py:630
  343.9 21.4 %collective-permute-start.23 = (bf16[4,240,128]{2,1,0:T(8,128)(2,1)S(1)}, bf16[4,240,128]{2,1,0:T(8,128)(2,1)S(1)}, u32[]{:S(2)}, u32[]{:S(2)}) collective-permute-start(bf16[4,240,128]{2,1,0:T(8,128)(2,1)S(1)} %get-tuple-element.119), channel_id=1, source_target_pairs={{0,4},{4,0},{8,12},{12,8},{16,20},{20,16},{24,28},{28,24},{1,5},{5... | collective-permute-start | bytes 737288 | tf_op jit(solution)/shard_map/ppermute | solution.py:630
  354.2 19.4 %collective-permute-start.28 = (bf16[4,240,128]{2,1,0:T(8,128)(2,1)S(1)}, bf16[4,240,128]{2,1,0:T(8,128)(2,1)S(1)}, u32[]{:S(2)}, u32[]{:S(2)}) collective-permute-start(bf16[4,240,128]{2,1,0:T(8,128)(2,1)S(1)} %get-tuple-element.117), channel_id=1, source_target_pairs={{0,8},{4,12},{8,0},{12,4},{16,24},{20,28},{24,16},{28,20},{1,9},{5... | collective-permute-start | bytes 737288 | tf_op jit(solution)/shard_map/ppermute | solution.py:630
  356.9 27.6 %collective-permute-start.35 = (bf16[1,160,128]{2,1,0:T(8,128)(2,1)}, bf16[1,160,128]{2,1,0:T(8,128)(2,1)S(1)}, u32[]{:S(2)}, u32[]{:S(2)}) collective-permute-start(bf16[1,160,128]{2,1,0:T(8,128)(2,1)} %get-tuple-element.136), channel_id=1, source_target_pairs={{0,16},{4,20},{8,24},{12,28},{16,0},{20,4},{24,8},{28,12},{1,17},{... | collective-permute-start | bytes 122888 | tf_op jit(solution)/shard_map/ppermute | solution.py:630
  365.4 12.5 %collective-permute-start.24 = (bf16[2,240,128]{2,1,0:T(8,128)(2,1)S(1)}, bf16[2,240,128]{2,1,0:T(8,128)(2,1)S(1)}, u32[]{:S(2)}, u32[]{:S(2)}) collective-permute-start(bf16[2,240,128]{2,1,0:T(8,128)(2,1)S(1)} %get-tuple-element.129), channel_id=1, source_target_pairs={{0,8},{4,12},{8,0},{12,4},{16,24},{20,28},{24,16},{28,20},{1,9},{5... | collective-permute-start | bytes 368648 | tf_op jit(solution)/shard_map/ppermute | solution.py:630
  379.5 9.7 %collective-permute-start.30 = (bf16[1,240,128]{2,1,0:T(8,128)(2,1)}, bf16[1,240,128]{2,1,0:T(8,128)(2,1)}, u32[]{:S(2)}, u32[]{:S(2)}) collective-permute-start(bf16[1,240,128]{2,1,0:T(8,128)(2,1)} %get-tuple-element.132), channel_id=1, source_target_pairs={{0,16},{4,20},{8,24},{12,28},{16,0},{20,4},{24,8},{28,12},{1,17},{... | collective-permute-start | bytes 184328 | tf_op jit(solution)/shard_map/ppermute | solution.py:630
  (63 other events, 835.3 us)
Sparse Core Ops, SparseCore 0:
  11.5 135.9 all-gather.1
  189.5 221.5 reduce-scatter.1

commit v3 on v2

--- a/solution.py
+++ b/solution.py
@@ -454,6 +454,8 @@
 
 
 def attention_backward_kernel(
+    first,
+    blocks,
     starts_ref,
     fills_ref,
     place_ref,
@@ -465,40 +467,38 @@
     sine_ref,
     *refs,
 ):
-    count = (len(refs) - 10) // 2
-    kv_blocks, d_query_ref, d_kv_blocks = refs[:count], refs[count], refs[count + 1 : 2 * count + 1]
-    (
-        kv_ref,
-        turned,
-        pairs,
-        query_rows,
-        upstream_rows,
-        deltas,
-        logs,
-        sums,
-        kv_sums,
-    ) = refs[2 * count + 1 :]
+    kv_blocks, refs = refs[:blocks], refs[-(blocks + 10) :]
+    d_query_ref, d_kv_blocks = refs[0], refs[1 : blocks + 1]
+    kv_ref, turned, pairs, query_rows, upstream_rows, deltas, logs, sums, kv_sums = refs[blocks + 1 :]
+    count = kv_sums.shape[0]
     i = pl.program_id(0)
     block = place_ref[0] * (TOK_DEV // BLK) + i
     tiles = kv_ref.shape[0] // TILE
 
     @pl.when(i == 0)
     def _():
-        lay_out_kv(kv_blocks, kv_ref, place_ref[0])
-        transpose_kv(kv_ref, turned, tiles)
-
-        def clear(t, carry):
-            kv_sums[:, pl.ds(pl.multiple_of(t * TILE, TILE), TILE), :] = jnp.zeros(
-                (KEY_VALUE_HEADS, TILE, 128), f32
-            )
+        for apart, source in enumerate(kv_blocks):
+            size = source.shape[0]
+            spot = apart if blocks == 1 else place_ref[0] ^ apart
+            kv_ref[pl.ds(pl.multiple_of(spot * size, TILE), size), :] = source[
+                :, 128 * first : 128 * (first + count)
+            ]
+
+        def prepare(t, carry):
+            rows = pl.ds(pl.multiple_of(t * TILE, TILE), TILE)
+            for h in range(count):
+                turned[t, HEAD_SIZE * h : HEAD_SIZE * (h + 1), :] = kv_ref[
+                    rows, 128 * h : 128 * h + 128
+                ].T[:HEAD_SIZE]
+            kv_sums[:, rows, :] = jnp.zeros((count, TILE, 128), f32)
             return carry
 
-        lax.fori_loop(0, tiles, clear, 0)
+        lax.fori_loop(0, tiles, prepare, 0)
 
     blank = jnp.zeros((HEAD_SIZE, WIDE), bf16)
-    for h in range(KEY_VALUE_HEADS):
-        query = heads_beside(query_ref, h)
-        upstream = heads_beside(upstream_ref, h)
+    for h in range(count):
+        query = heads_beside(query_ref, first + h)
+        upstream = heads_beside(upstream_ref, first + h)
         pairs[h, :HEAD_SIZE, :WIDE] = query
         pairs[h, HEAD_SIZE:, :WIDE] = blank
         pairs[h, :HEAD_SIZE, WIDE:] = blank
@@ -506,16 +506,19 @@
         query_rows[h] = pairs[h, :, :WIDE].T
         upstream_rows[h] = pairs[h, :, WIDE:].T
         deltas[h] = jnp.sum(
-            upstream.astype(f32) * heads_beside(mixed_ref, h).astype(f32), axis=0, keepdims=True
+            upstream.astype(f32) * heads_beside(mixed_ref, first + h).astype(f32),
+            axis=0,
+            keepdims=True,
         )
+        line = GROUPED * (first + h)
         logs[h] = jnp.concatenate(
-            [log_ref[GROUPED * h + g : GROUPED * h + g + 1, :] for g in range(GROUPED)], axis=1
+            [log_ref[line + g : line + g + 1, :] for g in range(GROUPED)], axis=1
         )
     sums[...] = jnp.zeros(sums.shape, f32)
 
     def step(tile, allowed):
         rows = pl.ds(pl.multiple_of(tile * TILE, TILE), TILE)
-        for h in range(KEY_VALUE_HEADS):
+        for h in range(count):
             both = jnp.dot(
                 kv_ref[rows, 128 * h : 128 * h + 128], pairs[h], preferred_element_type=f32
             )
@@ -528,14 +531,16 @@
                 d_scores, query_rows[h], preferred_element_type=f32
             ) + jnp.dot(probs.astype(bf16), upstream_rows[h], preferred_element_type=f32)
             sums[h] += jnp.dot(
-                turned[tile, 128 * h : 128 * h + HEAD_SIZE, :], d_scores, preferred_element_type=f32
+                turned[tile, HEAD_SIZE * h : HEAD_SIZE * (h + 1), :],
+                d_scores,
+                preferred_element_type=f32,
             )
 
     over_tiles(tile_range(starts_ref, fills_ref, block), block, step)
     cosine = cosine_ref[...]
     sine = sine_ref[...]
     half = HEAD_SIZE // 2
-    for h in range(KEY_VALUE_HEADS):
+    for h in range(count):
         for g in range(GROUPED):
             head = GROUPED * h + g
             front = sums[h, :half, BLK * g : BLK * (g + 1)] * score_scale
@@ -550,13 +555,13 @@
     @pl.when(i == pl.num_programs(0) - 1)
     def _():
         size = kv_blocks[0].shape[0]
-        for apart, block in enumerate(d_kv_blocks):
-            spot = apart if count == 1 else place_ref[0] ^ apart
+        for apart, out in enumerate(d_kv_blocks):
+            spot = apart if blocks == 1 else place_ref[0] ^ apart
 
             def emit(t, carry):
                 rows = pl.ds(pl.multiple_of(spot * size + t * TILE, TILE), TILE)
-                for h in range(KEY_VALUE_HEADS):
-                    block[pl.ds(pl.multiple_of(t * TILE, TILE), TILE), 128 * h : 128 * h + 128] = (
+                for h in range(count):
+                    out[pl.ds(pl.multiple_of(t * TILE, TILE), TILE), 128 * h : 128 * h + 128] = (
                         kv_sums[h, rows, :].astype(bf16)
                     )
                 return carry
@@ -564,11 +569,14 @@
             lax.fori_loop(0, size // TILE, emit, 0)
 
 
-def attention_backward(starts, fills, place, query, upstream, mixed, logs, cosine, sine, kv):
+def attention_backward(
+    first, count, starts, fills, place, query, upstream, mixed, logs, cosine, sine, kv, after=()
+):
     group = sum(block.shape[0] for block in kv)
     half = HEAD_SIZE // 2
+    outs = [(block.shape[0], 128 * count) for block in kv]
     return pl.pallas_call(
-        attention_backward_kernel,
+        functools.partial(attention_backward_kernel, first, len(kv)),
         grid_spec=pltpu.PrefetchScalarGridSpec(
             num_scalar_prefetch=3,
             grid=(TOK_DEV // BLK,),
@@ -580,26 +588,25 @@
                 token_block(half),
                 token_block(half),
             ]
-            + [whole(block.shape) for block in kv],
-            out_specs=[token_block(MODEL_WIDTH)] + [whole(block.shape) for block in kv],
+            + [whole(block.shape) for block in kv]
+            + [pl.BlockSpec(memory_space=pl.ANY)] * len(after),
+            out_specs=[token_block(GROUPED * HEAD_SIZE * count)] + [whole(shape) for shape in outs],
             scratch_shapes=[
-                pltpu.VMEM((group, 2 * KV_WIDTH), bf16),
-                pltpu.VMEM((group // TILE, 2 * KV_WIDTH, TILE), bf16),
-                pltpu.VMEM((KEY_VALUE_HEADS, 2 * HEAD_SIZE, 2 * WIDE), bf16),
-                pltpu.VMEM((KEY_VALUE_HEADS, WIDE, 128), bf16),
-                pltpu.VMEM((KEY_VALUE_HEADS, WIDE, 128), bf16),
-                pltpu.VMEM((KEY_VALUE_HEADS, 1, WIDE), f32),
-                pltpu.VMEM((KEY_VALUE_HEADS, 1, WIDE), f32),
-                pltpu.VMEM((KEY_VALUE_HEADS, HEAD_SIZE, WIDE), f32),
-                pltpu.VMEM((KEY_VALUE_HEADS, group, 128), f32),
+                pltpu.VMEM((group, 128 * count), bf16),
+                pltpu.VMEM((group // TILE, HEAD_SIZE * count, TILE), bf16),
+                pltpu.VMEM((count, 2 * HEAD_SIZE, 2 * WIDE), bf16),
+                pltpu.VMEM((count, WIDE, 128), bf16),
+                pltpu.VMEM((count, WIDE, 128), bf16),
+                pltpu.VMEM((count, 1, WIDE), f32),
+                pltpu.VMEM((count, 1, WIDE), f32),
+                pltpu.VMEM((count, HEAD_SIZE, WIDE), f32),
+                pltpu.VMEM((count, group, 128), f32),
             ],
         ),
-        out_shape=[
-            jax.ShapeDtypeStruct((MODEL_WIDTH, TOK_DEV), bf16),
-        ]
-        + [jax.ShapeDtypeStruct(block.shape, bf16) for block in kv],
+        out_shape=[jax.ShapeDtypeStruct((GROUPED * HEAD_SIZE * count, TOK_DEV), bf16)]
+        + [jax.ShapeDtypeStruct(shape, bf16) for shape in outs],
         name="attention_backward",
-    )(starts, fills, place, query, upstream, mixed, logs, cosine, sine, *kv)
+    )(starts, fills, place, query, upstream, mixed, logs, cosine, sine, *kv, *after)
 
 
 def dot_of(left, right, left_dim, right_dim):
@@ -610,6 +617,9 @@
 
 SLOTS = 3
 FORM = 640
+PERMUTED = 1
+COLOURS = 2
+SLABS = 20 // COLOURS
 PIECES = (240, 240, 160)
 GAIN_LINE = 560
 PAD_WIDTH = 1024
@@ -618,6 +628,7 @@
 ROW_BIT = ("shard", 2)
 NEAR_BITS = (ROW_BIT, ("dp", 1), ("dp", 2))
 FAR_BITS = (("dp", 4),)
+BACKWARD_CALLS = ((0, 5),)
 
 
 def stages(colour):
@@ -637,14 +648,20 @@
     return held, swap(held, CORE_BIT)
 
 
-def scatter_colour(keep, send, colour):
-    for bit in stages(colour):
-        got = swap(send, bit)
-        half = keep.shape[0] // 2
+def scatter_stage(held, number):
+    outcome = []
+    total = lambda parts: sum(part.astype(f32) for part in parts)
+    for colour, (parts, send) in enumerate(held):
+        got = swap(send, stages(colour)[number])
+        half = got.shape[0] // 2
         if half == 0:
-            return keep[0], got[0]
-        send = keep[half:] + got[half:]
-        keep = keep[:half] + got[:half]
+            outcome.append((total(parts)[0].astype(bf16), got[0]))
+        else:
+            parts = parts + [got]
+            outcome.append(
+                ([part[:half] for part in parts], total([part[half:] for part in parts]).astype(bf16))
+            )
+    return outcome
 
 
 def positions():
@@ -805,33 +822,43 @@
     )(narrow, lines)
 
 
-def unform_feedforward_kernel(narrow_ref, terms, lines_ref, mid):
+def unform_feedforward_kernel(narrow_ref, *refs):
+    addends, (terms, lines_ref, mid) = refs[: 2 * COLOURS], refs[2 * COLOURS :]
+
+    def term(s, k, rows):
+        if s >= PERMUTED:
+            return terms[s - PERMUTED, k, rows, :].astype(f32)
+        keep, got = addends[2 * (k // SLABS) : 2 * (k // SLABS) + 2]
+        return keep[k % SLABS, rows, :].astype(f32) + got[k % SLABS, rows, :].astype(f32)
+
     for s in range(SLOTS):
 
         @pl.when(narrow_ref[s] == 1)
         def _():
             for c in range(20):
-                mid[0:32, :] = terms[s, c].astype(f32)
+                mid[0:32, :] = term(s, c, slice(0, 32))
                 lines_ref[pl.ds(LINES * s + c, 30, stride=20), :] = mid[0:30, :]
 
         @pl.when(narrow_ref[s] == 0)
         def _():
             def load(c):
                 return jnp.concatenate(
-                    [terms[s, k, r : r + 16, :].astype(f32) for k, r, m in wide_pieces(c)], axis=0
+                    [term(s, k, slice(r, r + 16)) for k, r, m in wide_pieces(c)], axis=0
                 )
 
             rows_to_lines_960(load, lines_ref, LINES * s, 80, mid)
 
 
-def unform_feedforward(narrow, terms):
+def unform_feedforward(narrow, addends, terms):
     return pl.pallas_call(
         unform_feedforward_kernel,
-        in_specs=[SMEM_SPEC, pl.BlockSpec((SLOTS, 20, 32, 128))],
+        in_specs=[SMEM_SPEC]
+        + [pl.BlockSpec((SLABS, 32, 128))] * (2 * COLOURS)
+        + [pl.BlockSpec((SLOTS - PERMUTED, 20, 32, 128))],
         out_shape=jax.ShapeDtypeStruct((SLOTS * LINES, 128), f32),
         scratch_shapes=[pltpu.VMEM((80, 128), f32)],
         name="unform_feedforward",
-    )(narrow, terms)
+    )(narrow, *addends, terms)
 
 
 def place_attention_kernel(table_ref, *refs):
@@ -970,6 +997,7 @@
 
 
 def feedforward_kernel(
+    table_ref,
     hidden_ref,
     turned_ref,
     grad_ref,
@@ -978,32 +1006,59 @@
     down_ref,
     out_ref,
     d_hidden_ref,
-    terms_ref,
-    down,
-    inner_rows,
-    inner_turned,
-    d_both,
-    both_out,
-    down_out,
-    sems,
+    *refs,
 ):
+    targets = [refs[2 * k : 2 * k + 2] for k in range(COLOURS)]
+    terms_ref, down, inner_rows, inner_turned, d_both, both_out, down_out, sems = refs[2 * COLOURS :]
     q = pl.program_id(0)
     chunks = pl.num_programs(0)
     slot = lax.rem(q, 2)
 
-    def copies(side, chunk):
-        columns = pl.ds(5 * chunk, 5)
-        return (
-            pltpu.make_async_copy(
-                both_out.at[side, 0], terms_ref.at[pl.ds(0, 32), columns], sems.at[side, 0]
-            ),
-            pltpu.make_async_copy(
-                both_out.at[side, 1], terms_ref.at[pl.ds(32, 32), columns], sems.at[side, 1]
-            ),
-            pltpu.make_async_copy(
-                down_out.at[side], terms_ref.at[pl.ds(64 + 8 * chunk, 8)], sems.at[side, 2]
-            ),
-        )
+    def send_terms():
+        columns = pl.ds(5 * q, 5)
+        for u in range(2 * UNITS):
+            device, s = divmod(u, SLOTS)
+            source = both_out.at[slot, u // UNITS, u % UNITS]
+            if s >= PERMUTED:
+                place = (SLOTS - PERMUTED) * device + s - PERMUTED
+                pltpu.make_async_copy(source, terms_ref.at[place, columns], sems.at[slot, 0]).start()
+                continue
+            for k in range(COLOURS):
+
+                @pl.when(5 * q // SLABS == k)
+                def _():
+                    copy_to(
+                        source,
+                        targets[k],
+                        table_ref[UNITS * k + device],
+                        sems.at[slot, 0],
+                        lambda ref: ref.at[pl.ds(5 * q - SLABS * k, 5)],
+                    )
+
+        for v in range(8):
+            unit = 2 * UNITS + 8 * q + v
+            device = unit // SLOTS
+            s = unit - SLOTS * device
+            source = down_out.at[slot, v]
+
+            @pl.when(s >= PERMUTED)
+            def _():
+                place = (SLOTS - PERMUTED) * device + s - PERMUTED
+                pltpu.make_async_copy(source, terms_ref.at[place], sems.at[slot, 1]).start()
+
+            @pl.when(s < PERMUTED)
+            def _():
+                for k in range(COLOURS):
+                    copy_to(
+                        source.at[pl.ds(SLABS * k, SLABS)],
+                        targets[k],
+                        table_ref[UNITS * k + device],
+                        sems.at[slot, 1],
+                    )
+
+    def wait_terms(side):
+        wait_for(both_out.at[side], sems.at[side, 0])
+        wait_for(down_out.at[side], sems.at[side, 1])
 
     for v in range(8):
         for c in range(8):
@@ -1043,8 +1098,7 @@
 
     @pl.when(q >= 2)
     def _():
-        for copy in copies(slot, q - 2):
-            copy.wait()
+        wait_terms(slot)
 
     def both_step(i, carry):
         rows = pl.ds(pl.multiple_of(256 * i, 256), 256)
@@ -1072,21 +1126,22 @@
         return carry
 
     lax.fori_loop(0, 2, down_step, 0)
-    for copy in copies(slot, q):
-        copy.start()
+    send_terms()
 
     @pl.when(q == chunks - 1)
     def _():
-        for copy in copies(1 - slot, q - 1) + copies(slot, q):
-            copy.wait()
-
-
-def feedforward(hidden, turned, grad, weights):
+        for side in range(2):
+            wait_terms(side)
+
+
+def feedforward(table, hidden, turned, grad, weights):
+    block = jax.ShapeDtypeStruct((16, SLABS, 32, 128), bf16)
     full = lambda shape: pl.BlockSpec(shape, lambda q: (0, 0))
     return pl.pallas_call(
         feedforward_kernel,
         grid=(FF // CHUNK,),
         in_specs=[
+            SMEM_SPEC,
             full((TOK_DEV, PAD_WIDTH)),
             full((PAD_WIDTH, TOK_DEV)),
             full((TOK_DEV, PAD_WIDTH)),
@@ -1094,9 +1149,10 @@
             pl.BlockSpec((32, 5, 32, 128), lambda q: (1, q, 0, 0)),
             pl.BlockSpec((8, 20, 32, 128), lambda q: (8 + q, 0, 0, 0)),
         ],
-        out_specs=[full((TOK_DEV, PAD_WIDTH))] * 2 + [ANY_SPEC],
+        out_specs=[full((TOK_DEV, PAD_WIDTH))] * 2 + [ANY_SPEC] * (2 * COLOURS + 1),
         out_shape=[jax.ShapeDtypeStruct((TOK_DEV, PAD_WIDTH), f32)] * 2
-        + [jax.ShapeDtypeStruct((3 * UNITS, 20, 32, 128), bf16)],
+        + [block] * (2 * COLOURS)
+        + [jax.ShapeDtypeStruct(((SLOTS - PERMUTED) * UNITS, 20, 32, 128), bf16)],
         scratch_shapes=[
             pltpu.VMEM((CHUNK, PAD_WIDTH), bf16),
             pltpu.VMEM((TOK_DEV, CHUNK), bf16),
@@ -1104,11 +1160,11 @@
             pltpu.VMEM((TOK_DEV, 2 * CHUNK), bf16),
             pltpu.VMEM((2, 2, 32, 5, 32, 128), bf16),
             pltpu.VMEM((2, 8, 20, 32, 128), bf16),
-            pltpu.SemaphoreType.DMA((2, 3)),
+            pltpu.SemaphoreType.DMA((2, 2)),
         ],
         compiler_params=pltpu.CompilerParams(vmem_limit_bytes=60 * 2**20),
         name="feedforward",
-    )(hidden, turned, grad, weights, weights, weights)
+    )(table, hidden, turned, grad, weights, weights, weights)
 
 
 def spread_matrix():
@@ -1261,7 +1317,8 @@
     grad_low = grad_out.astype(bf16)
     if in_units:
         spread = spread_matrix()
-        outcome, d_spread, ff_terms = feedforward(
+        outcome, d_spread, *ff_terms, ff_rest = feedforward(
+            table,
             dot_of(hidden_two, spread, 1, 0).astype(bf16),
             dot_of(spread, hidden_two, 0, 1).astype(bf16),
             jnp.pad(grad_low, ((0, 0), (0, PAD_WIDTH - MODEL_WIDTH))),
@@ -1272,8 +1329,8 @@
         d_hidden_two = dot_of(d_coarse.astype(bf16), spread, 1, 1) + dot_of(
             (d_spread - d_coarse).astype(bf16), spread, 1, 1
         )
-        ff_sum = scatter_lines(ff_terms.reshape(SLOTS * UNITS * FORM, 128))
-        feedforward_gradient = unform_feedforward(narrow, ff_sum.reshape(SLOTS, 20, 32, 128)).reshape(-1)
+        ff_held = [([ff_terms[2 * k]], ff_terms[2 * k + 1]) for k in range(COLOURS)]
+        ff_sum = scatter_lines(ff_rest.reshape(-1, 128))
     else:
         gate_weight, up_weight, down_weight = unpack_ff(feedforward_all)
         gate = dot_of(hidden_two, gate_weight, 1, 0)
@@ -1303,7 +1360,9 @@
     d_branch = d_middle.astype(bf16)
     d_out_weight = dot_of(mixed_turned, d_branch, 1, 0).astype(bf16)
     d_mixed = dot_of(out_weight, d_branch, 1, 1).astype(bf16)
-    d_query, *d_kv = attention_backward(
+    backward_of = lambda first, count, after: attention_backward(
+        first,
+        count,
         block_start,
         block_fill,
         place,
@@ -1314,12 +1373,27 @@
         cosine_table,
         sine_table,
         kv_all,
+        after,
     )
     if in_units:
-        across = d_kv[2] + swap(d_kv[3], CORE_BIT)
-        d_kv_rows = d_kv[0] + swap(d_kv[1], CORE_BIT) + swap(across, ROW_BIT)
+        d_query, d_kv_rows = [], []
+        for number, (first, count) in enumerate(BACKWARD_CALLS):
+            ff_held = scatter_stage(ff_held, number)
+            d_query_part, *d_kv = backward_of(first, count, [send for _, send in ff_held])
+            across = d_kv[2] + swap(d_kv[3], CORE_BIT)
+            d_query.append(d_query_part)
+            d_kv_rows.append(d_kv[0] + swap(d_kv[1], CORE_BIT) + swap(across, ROW_BIT))
+        d_query = jnp.concatenate(d_query, axis=0)
+        d_kv_rows = jnp.concatenate(d_kv_rows, axis=1)
+        for number in range(len(BACKWARD_CALLS), len(stages(0))):
+            ff_held = scatter_stage(ff_held, number)
+        ff_addends = [addend for pair in ff_held for addend in pair]
+        feedforward_gradient = unform_feedforward(
+            narrow, ff_addends, ff_sum.reshape(SLOTS - PERMUTED, 20, 32, 128)
+        ).reshape(-1)
     else:
-        d_kv_rows = lax.psum_scatter(d_kv[0], "shard", scatter_dimension=0, tiled=True)
+        d_query, d_kv = backward_of(0, KEY_VALUE_HEADS, ())
+        d_kv_rows = lax.psum_scatter(d_kv, "shard", scatter_dimension=0, tiled=True)
     d_kv_turned = d_kv_rows.T.reshape(KEY_VALUE_HEADS, 2, HEAD_SIZE, TOK_DEV)
     d_front = d_kv_turned[:, 0, : HEAD_SIZE // 2].astype(f32)
     d_back = d_kv_turned[:, 0, HEAD_SIZE // 2 :].astype(f32)
@@ -1345,11 +1419,10 @@
             gain_terms.reshape(UNITS, gain_count), ((0, 0), (64, 64 - gain_count))
         )
         terms = split_attention(table, d_query_weight, d_kv_weight, d_out_weight, gain_rows)
-        addends = [
-            addend
-            for k in range(SLOTS)
-            for addend in scatter_colour(terms[2 * k], terms[2 * k + 1], k)
-        ]
+        held = [([terms[2 * k]], terms[2 * k + 1]) for k in range(SLOTS)]
+        for number in range(len(stages(0))):
+            held = scatter_stage(held, number)
+        addends = [addend for pair in held for addend in pair]
         attention_sum, gain_sum = unform_attention(wide, addends)
         attention_gradient = attention_sum.reshape(-1)
         gains_gradient = gain_sum[0, 64 : 64 + gain_count]

time: 431 us -> 469 us (1.088)
  starting transfers between devices: 110 us -> 154 us
  waiting for transfers between devices: 125 us -> 104 us
  other arithmetic: 24.8 us -> 37.5 us
    ppermute x36 -> x46, starting transfers between devices: 110 us -> 154 us  [swap(): return lax.ppermute(value, axis, [(i, i ^ mask) for i in range(size)])]
    convert_element_type x0 -> x20, other arithmetic: none -> 18.5 us  [scatter_stage(): total([part[half:] for part in parts]).astype(bf16)]
    reduce_scatter x1, waiting for transfers between devices: 16.6 us -> 0.02 us  [scatter_lines(): return lax.psum_scatter(lines, ALL_AXES, scatter_dimension=0, tiled=True)]
    add x12 -> x0, other arithmetic: 8.03 us -> none  [the longest x9 6.06 us: scatter_colour(): keep = keep[:half] + got[:half]]
    ppermute x36 -> x46, waiting for transfers between devices: 104 us -> 98.2 us  [swap(): return lax.ppermute(value, axis, [(i, i ^ mask) for i in range(size)])]
    unnamed x113 -> x121, local copies, waits for them, and re-layouts: 12.7 us -> 13.7 us
  transfers between devices with their start and end apart: 38 -> 48, of which waited for: 23 -> 17; matrix products, arithmetic and copies ran while one was open for 16% -> 18% of each run, Pallas kernels for 12% -> 11%
where the time goes in v3:
time: 469 us; the launch traced here: 462 us
  starting transfers between devices  154 us (33%)
  waiting for transfers between devices  104 us (22%)
  Pallas kernels  97.7 us (21%)
  other arithmetic  37.5 us (8%)
  matrix products  34.7 us (7%)
  local copies, waits for them, and re-layouts  19.2 us (4%)
  between operations  15.5 us (3%)
    ppermute x46, starting transfers between devices, swap(): return lax.ppermute(value, axis, [(i, i ^ mask) for i in range(size)])  154 us
    ppermute x46, waiting for transfers between devices, swap(): return lax.ppermute(value, axis, [(i, i ^ mask) for i in range(size)])  98.2 us
    pallas_call x1, Pallas kernels, feedforward(): pl.pallas_call(feedforward_kernel, grid=(FF // CHUNK,), in_specs=[SMEM_SP...  44 us
    dot_general x13, matrix products, dot_of(): lax.dot_general(left, right, (((left_dim,), (right_dim,)), ((), ())), pre...  34.7 us
    convert_element_type x20, other arithmetic, scatter_stage(): total([part[half:] for part in parts]).astype(bf16)  18.5 us
    pallas_call x1, Pallas kernels, attention_backward(): pl.pallas_call(functools.partial(attention_backward_kernel, first, len(kv...  18 us
    pallas_call x1, Pallas kernels, attention_forward(): pl.pallas_call(attention_forward_kernel, grid_spec=pltpu.PrefetchScalarGr...  14.9 us
    unnamed x121, local copies, waits for them, and re-layouts  13.7 us
  transfers between devices with their start and end apart: 48, of which 17 were waited for; matrix products, arithmetic and copies ran while one was open for 18% of the time, Pallas kernels for 11%

profile of v3, /device:TPU:0, one launch (start us, length us, event | category | flops | bytes accessed | tf_op | source)
XLA Modules:
  0.0 462.1 jit_solution(10887881124688520346)
XLA Ops:
  13.2 4.1 collective-permute-start.10
  28.1 3.7 collective-permute-done.6
  33.4 4.6 collective-permute-done.1
  48.3 16.9 %collective-permute-done.8 = bf16[8,240,128]{2,1,0:T(8,128)(2,1)S(1)} collective-permute-done((bf16[8,240,128]{2,1,0:T(8,128)(2,1)S(1)}, bf16[8,240,128]{2,1,0:T(8,128)(2,1)S(1)}, u32[]{:S(2)}, u32[]{:S(2)}) %collective-permute-start.8) | collective-permute-done | bytes 491552 | tf_op jit(solution)/shard_map/ppermute | solution.py:641
  72.7 7.1 %place_attention.1 = (bf16[960,960]{1,0:T(8,128)(2,1)}, bf16[960,640]{1,0:T(8,128)(2,1)}, bf16[960,960]{1,0:T(8,128)(2,1)}, f32[32,128]{1,0:T(8,128)}) custom-call(s32[96]{0:T(128)} %pad_add_fusion.table_ref, bf16[16,240,128]{2,1,0:T(8,128)(2,1)} %copy-done.23, bf16[16,240,128]{2,1,0:T(8,128)(2,1)} %collective-permute-done.4.refs_1_, ...), custom_call_target="tpu_custom_call" | custom-call | tf_op jit(solution)/shard_map/place_attention/pallas_call | solution.py:913
  90.1 22.6 %collective-permute-done.16.refs_2_ = bf16[512,640]{1,0:T(8,128)(2,1)S(1)} collective-permute-done((bf16[512,640]{1,0:T(8,128)(2,1)S(1)}, bf16[512,640]{1,0:T(8,128)(2,1)S(1)}, u32[]{:S(2)}, u32[]{:S(2)}) %collective-permute-start.16) | collective-permute-done | bytes 655392 | tf_op jit(solution)/shard_map/ppermute | solution.py:641
  118.3 14.9 %attention_forward.1 = (bf16[960,512]{1,0:T(8,128)(2,1)}, f32[16,512]{1,0:T(8,128)}) custom-call(s32[16]{0:T(128)} %starts_ref.3, s32[16]{0:T(128)} %fills_ref.3, s32[1]{0:T(128)} %bitcast.place_ref, bf16[960,512]{1,0:T(8,128)(2,1)} %bitcast.76, bf16[512,640]{1,0:T(8,128)(2,1)} %bitcast.80, bf16[512,640]{1,0:T(8,128)(2,1)} %collective-permute-done.15.refs_1_, ...), custom_call_target="tpu_custom_call" | custom-call | tf_op jit(solution)/shard_map/attention_forward/pallas_call | solution.py:432
  141.3 5.7 %all-gather.2.cloned.1.call-done = bf16[61440,128]{1,0:T(8,128)(2,1)} async-done(((bf16[1920,128]{1,0:T(8,128)(2,1)}), bf16[61440,128]{1,0:T(8,128)(2,1)}) %all-gather.2.cloned.1.call-update) | async-done | bytes 15728656 | tf_op jit(solution)/shard_map/all_gather | solution.py:1202
  147.0 44.0 %feedforward.1 = (f32[512,1024]{1,0:T(8,128)}, f32[512,1024]{1,0:T(8,128)}, bf16[16,10,32,128]{3,2,1,0:T(8,128)(2,1)}, bf16[16,10,32,128]{3,2,1,0:T(8,128)(2,1)}...) custom-call(s32[96]{0:T(128)} %pad_add_fusion.table_ref, ...), custom_call_target="tpu_custom_call" | custom-call | tf_op jit(solution)/shard_map/feedforward/pallas_call | solution.py:1140
  204.9 18.0 %attention_backward.1 = (bf16[960,512]{1,0:T(8,128)(2,1)}, bf16[512,640]{1,0:T(8,128)(2,1)}, bf16[512,640]{1,0:T(8,128)(2,1)}, bf16[512,640]{1,0:T(8,128)(2,1)}, bf16[512,640]{1,0:T(8,128)(2,1)}) custom-call(s32[16]{0:T(128)} %starts_ref.3, s32[16]{0:T(128)} %fills_ref.3, s32[1]{0:T(128)} %bitcast.place_ref, bf16[960,512]{1,0:T(8,128)(2,1)} %bitcast.77, ...), custom_call_target="tpu_custom_call" | custom-call | tf_op jit(solution)/shard_map/attention_backward/pallas_call | solution.py:578
  227.4 3.8 convolution_convert_fusion.out_ref
  231.3 9.7 %collective-permute-start.42 = (bf16[8,10,32,128]{3,2,1,0:T(8,128)(2,1)}, bf16[8,10,32,128]{3,2,1,0:T(8,128)(2,1)}, u32[]{:S(2)}, u32[]{:S(2)}) collective-permute-start(bf16[8,10,32,128]{3,2,1,0:T(8,128)(2,1)} %add_convert_fusion.refs_5_), channel_id=1, source_target_pairs={{0,4},{4,0},{8,12},{12,8},{16,20},{20,16},{24,28},{28,24},{1,5},{5... | collective-permute-start | bytes 1966088 | tf_op jit(solution)/shard_map/ppermute | solution.py:641
  241.0 4.1 convolution_convert_fusion.1.query_ref
  245.1 10.0 %collective-permute-done.38 = bf16[8,10,32,128]{3,2,1,0:T(8,128)(2,1)} collective-permute-done((bf16[8,10,32,128]{3,2,1,0:T(8,128)(2,1)}, bf16[8,10,32,128]{3,2,1,0:T(8,128)(2,1)}, u32[]{:S(2)}, u32[]{:S(2)}) %collective-permute-start.38) | collective-permute-done | bytes 655392 | tf_op jit(solution)/shard_map/ppermute | solution.py:641
  256.4 9.4 %collective-permute-start.39 = (bf16[4,10,32,128]{3,2,1,0:T(8,128)(2,1)S(1)}, bf16[4,10,32,128]{3,2,1,0:T(8,128)(2,1)}, u32[]{:S(2)}, u32[]{:S(2)}) collective-permute-start(bf16[4,10,32,128]{3,2,1,0:T(8,128)(2,1)S(1)} %add_convert_fusion.6), channel_id=1, source_target_pairs={{0,4},{4,0},{8,12},{12,8},{16,20},{20,16},{24,28},{28,24},{1,5},{5... | collective-permute-start | bytes 983048 | tf_op jit(solution)/shard_map/ppermute | solution.py:641
  265.9 16.2 %collective-permute-done.22 = bf16[512,640]{1,0:T(8,128)(2,1)} collective-permute-done((bf16[512,640]{1,0:T(8,128)(2,1)}, bf16[512,640]{1,0:T(8,128)(2,1)}, u32[]{:S(2)}, u32[]{:S(2)}) %collective-permute-start.22) | collective-permute-done | bytes 655392 | tf_op jit(solution)/shard_map/ppermute | solution.py:641
  292.2 5.3 %split_attention.1 = (bf16[16,240,128]{2,1,0:T(8,128)(2,1)}, bf16[16,240,128]{2,1,0:T(8,128)(2,1)}, bf16[16,240,128]{2,1,0:T(8,128)(2,1)}, bf16[16,240,128]{2,1,...) custom-call(s32[96]{0:T(128)} %pad_add_fusion.table_ref, ...), custom_call_target="tpu_custom_call" | custom-call | tf_op jit(solution)/shard_map/split_attention/pallas_call | solution.py:983
  299.6 5.2 %collective-permute-start.43 = (bf16[4,10,32,128]{3,2,1,0:T(8,128)(2,1)}, bf16[4,10,32,128]{3,2,1,0:T(8,128)(2,1)}, u32[]{:S(2)}, u32[]{:S(2)}) collective-permute-start(bf16[4,10,32,128]{3,2,1,0:T(8,128)(2,1)} %add_convert_fusion.5), channel_id=1, source_target_pairs={{0,8},{4,12},{8,0},{12,4},{16,24},{20,28},{24,16},{28,20},{1,9},{5... | collective-permute-start | bytes 983048 | tf_op jit(solution)/shard_map/ppermute | solution.py:641
  308.5 8.6 %collective-permute-done.43 = bf16[4,10,32,128]{3,2,1,0:T(8,128)(2,1)} collective-permute-done((bf16[4,10,32,128]{3,2,1,0:T(8,128)(2,1)}, bf16[4,10,32,128]{3,2,1,0:T(8,128)(2,1)}, u32[]{:S(2)}, u32[]{:S(2)}) %collective-permute-start.43) | collective-permute-done | bytes 327712 | tf_op jit(solution)/shard_map/ppermute | solution.py:641
  324.0 45.0 %collective-permute-start.41 = (bf16[1,10,32,128]{3,2,1,0:T(8,128)(2,1)}, bf16[1,10,32,128]{3,2,1,0:T(8,128)(2,1)S(1)}, u32[]{:S(2)}, u32[]{:S(2)}) collective-permute-start(bf16[1,10,32,128]{3,2,1,0:T(8,128)(2,1)} %get-tuple-element.116), channel_id=1, source_target_pairs={{0,16},{4,20},{8,24},{12,28},{16,0},{20,4},{24,8},{28,12},{1,17},{... | collective-permute-start | bytes 245768 | tf_op jit(solution)/shard_map/ppermute | solution.py:641
  379.0 28.6 %collective-permute-start.29 = (bf16[8,240,128]{2,1,0:T(8,128)(2,1)S(1)}, bf16[8,240,128]{2,1,0:T(8,128)(2,1)S(1)}, u32[]{:S(2)}, u32[]{:S(2)}) collective-permute-start(bf16[8,240,128]{2,1,0:T(8,128)(2,1)S(1)} %add_convert_fusion.2), channel_id=1, source_target_pairs={{0,4},{4,0},{8,12},{12,8},{16,20},{20,16},{24,28},{28,24},{1,5},{5... | collective-permute-start | bytes 1474568 | tf_op jit(solution)/shard_map/ppermute | solution.py:641
  408.5 4.7 %collective-permute-start.36 = (bf16[2,160,128]{2,1,0:T(8,128)(2,1)S(1)}, bf16[2,160,128]{2,1,0:T(8,128)(2,1)S(1)}, u32[]{:S(2)}, u32[]{:S(2)}) collective-permute-start(bf16[2,160,128]{2,1,0:T(8,128)(2,1)S(1)} %add_convert_fusion.20), channel_id=1, source_target_pairs={{0,4},{4,0},{8,12},{12,8},{16,20},{20,16},{24,28},{28,24},{1,5},{5... | collective-permute-start | bytes 245768 | tf_op jit(solution)/shard_map/ppermute | solution.py:641
  413.3 7.2 %collective-permute-start.25 = (bf16[4,240,128]{2,1,0:T(8,128)(2,1)S(1)}, bf16[4,240,128]{2,1,0:T(8,128)(2,1)S(1)}, u32[]{:S(2)}, u32[]{:S(2)}) collective-permute-start(bf16[4,240,128]{2,1,0:T(8,128)(2,1)S(1)} %add_convert_fusion.9), channel_id=1, source_target_pairs={{0,4},{4,0},{8,12},{12,8},{16,20},{20,16},{24,28},{28,24},{1,5},{5... | collective-permute-start | bytes 737288 | tf_op jit(solution)/shard_map/ppermute | solution.py:641
  422.1 6.9 %collective-permute-start.37 = (bf16[1,160,128]{2,1,0:T(8,128)(2,1)}, bf16[1,160,128]{2,1,0:T(8,128)(2,1)}, u32[]{:S(2)}, u32[]{:S(2)}) collective-permute-start(bf16[1,160,128]{2,1,0:T(8,128)(2,1)} %get-tuple-element.126), channel_id=1, source_target_pairs={{0,16},{4,20},{8,24},{12,28},{16,0},{20,4},{24,8},{28,12},{1,17},{... | collective-permute-start | bytes 122888 | tf_op jit(solution)/shard_map/ppermute | solution.py:641
  (292 shorter events, 140.3 us)
Async XLA Ops:
  7.2 139.8 %all-gather.2.cloned.1.call-start = ((), (), s32[]{:S(2)}) async-start(), calls=%async_computation.1 | async-start | bytes 16220160 | tf_op jit(solution)/shard_map/all_gather | solution.py:1202
  10.1 438.4 %reduce-scatter.2.cloned.1.call-start = ((), (), s32[]{:S(2)}) async-start(), calls=%async_computation.2 | async-start | bytes 10813440 | tf_op jit(solution)/shard_map/reduce_scatter | solution.py:1206
  44.6 20.5 %collective-permute-start.8 = (bf16[8,240,128]{2,1,0:T(8,128)(2,1)S(1)}, bf16[8,240,128]{2,1,0:T(8,128)(2,1)S(1)}, u32[]{:S(2)}, u32[]{:S(2)}) collective-permute-start(bf16[8,240,128]{2,1,0:T(8,128)(2,1)S(1)} %pad_maximum_fusion.3), channel_id=1, source_target_pairs={{0,4},{4,0},{8,12},{12,8},{16,20},{20,16},{24,28},{28,24},{1,5},{5... | collective-permute-start | bytes 1474568 | tf_op jit(solution)/shard_map/ppermute | solution.py:641
  46.3 19.5 %collective-permute-start.3 = (bf16[8,240,128]{2,1,0:T(8,128)(2,1)S(1)}, bf16[8,240,128]{2,1,0:T(8,128)(2,1)S(1)}, u32[]{:S(2)}, u32[]{:S(2)}) collective-permute-start(bf16[8,240,128]{2,1,0:T(8,128)(2,1)S(1)} %pad_maximum_fusion.2), channel_id=1, source_target_pairs={{0,2},{1,3},{2,0},{3,1},{4,6},{5,7},{6,4},{7,5},{8,10},{9,11},{10,... | collective-permute-start | bytes 1474568 | tf_op jit(solution)/shard_map/ppermute | solution.py:641
  47.9 20.8 %collective-permute-start.13 = (bf16[8,160,128]{2,1,0:T(8,128)(2,1)S(1)}, bf16[8,160,128]{2,1,0:T(8,128)(2,1)S(1)}, u32[]{:S(2)}, u32[]{:S(2)}) collective-permute-start(bf16[8,160,128]{2,1,0:T(8,128)(2,1)S(1)} %pad_maximum_fusion.4), channel_id=1, source_target_pairs={{0,8},{4,12},{8,0},{12,4},{16,24},{20,28},{24,16},{28,20},{1,9},{5... | collective-permute-start | bytes 983048 | tf_op jit(solution)/shard_map/ppermute | solution.py:641
  83.7 29.1 %collective-permute-start.16 = (bf16[512,640]{1,0:T(8,128)(2,1)S(1)}, bf16[512,640]{1,0:T(8,128)(2,1)S(1)}, u32[]{:S(2)}, u32[]{:S(2)}) collective-permute-start(bf16[512,640]{1,0:T(8,128)(2,1)S(1)} %bitcast.78), channel_id=1, source_target_pairs={{0,2},{1,3},{2,0},{3,1},{4,6},{5,7},{6,4},{7,5},{8,10},{9,11},{10,... | collective-permute-start | bytes 1966088 | tf_op jit(solution)/shard_map/ppermute | solution.py:641
  89.4 28.1 %collective-permute-start.15 = (bf16[512,640]{1,0:T(8,128)(2,1)S(1)}, bf16[512,640]{1,0:T(8,128)(2,1)}, u32[]{:S(2)}, u32[]{:S(2)}) collective-permute-start(bf16[512,640]{1,0:T(8,128)(2,1)S(1)} %bitcast.79), channel_id=1, source_target_pairs={{0,1},{1,0},{2,3},{3,2},{4,5},{5,4},{6,7},{7,6},{8,9},{9,8},{10,11... | collective-permute-start | bytes 1966088 | tf_op jit(solution)/shard_map/ppermute | solution.py:641
  223.3 31.8 %collective-permute-start.38 = (bf16[8,10,32,128]{3,2,1,0:T(8,128)(2,1)}, bf16[8,10,32,128]{3,2,1,0:T(8,128)(2,1)}, u32[]{:S(2)}, u32[]{:S(2)}) collective-permute-start(bf16[8,10,32,128]{3,2,1,0:T(8,128)(2,1)} %add_convert_fusion.1.refs_4_), channel_id=1, source_target_pairs={{0,2},{1,3},{2,0},{3,1},{4,6},{5,7},{6,4},{7,5},{8,10},{9,11},{10,... | collective-permute-start | bytes 1966088 | tf_op jit(solution)/shard_map/ppermute | solution.py:641
  223.3 42.6 %collective-permute-start.20 = (bf16[512,640]{1,0:T(8,128)(2,1)}, bf16[512,640]{1,0:T(8,128)(2,1)}, u32[]{:S(2)}, u32[]{:S(2)}) collective-permute-start(bf16[512,640]{1,0:T(8,128)(2,1)} %get-tuple-element.60), channel_id=1, source_target_pairs={{0,1},{1,0},{2,3},{3,2},{4,5},{5,4},{6,7},{7,6},{8,9},{9,8},{10,11... | collective-permute-start | bytes 1966088 | tf_op jit(solution)/shard_map/ppermute | solution.py:641
  227.4 54.6 %collective-permute-start.22 = (bf16[512,640]{1,0:T(8,128)(2,1)}, bf16[512,640]{1,0:T(8,128)(2,1)}, u32[]{:S(2)}, u32[]{:S(2)}) collective-permute-start(bf16[512,640]{1,0:T(8,128)(2,1)} %add.470), channel_id=1, source_target_pairs={{0,2},{1,3},{2,0},{3,1},{4,6},{5,7},{6,4},{7,5},{8,10},{9,11},{10,... | collective-permute-start | bytes 1966088 | tf_op jit(solution)/shard_map/ppermute | solution.py:641
  231.3 66.3 %collective-permute-start.42 = (bf16[8,10,32,128]{3,2,1,0:T(8,128)(2,1)}, bf16[8,10,32,128]{3,2,1,0:T(8,128)(2,1)}, u32[]{:S(2)}, u32[]{:S(2)}) collective-permute-start(bf16[8,10,32,128]{3,2,1,0:T(8,128)(2,1)} %add_convert_fusion.refs_5_), channel_id=1, source_target_pairs={{0,4},{4,0},{8,12},{12,8},{16,20},{20,16},{24,28},{28,24},{1,5},{5... | collective-permute-start | bytes 1966088 | tf_op jit(solution)/shard_map/ppermute | solution.py:641
  256.4 50.4 %collective-permute-start.39 = (bf16[4,10,32,128]{3,2,1,0:T(8,128)(2,1)S(1)}, bf16[4,10,32,128]{3,2,1,0:T(8,128)(2,1)}, u32[]{:S(2)}, u32[]{:S(2)}) collective-permute-start(bf16[4,10,32,128]{3,2,1,0:T(8,128)(2,1)S(1)} %add_convert_fusion.6), channel_id=1, source_target_pairs={{0,4},{4,0},{8,12},{12,8},{16,20},{20,16},{24,28},{28,24},{1,5},{5... | collective-permute-start | bytes 983048 | tf_op jit(solution)/shard_map/ppermute | solution.py:641
  297.4 21.1 %collective-permute-start.33 = (bf16[16,160,128]{2,1,0:T(8,128)(2,1)}, bf16[16,160,128]{2,1,0:T(8,128)(2,1)}, u32[]{:S(2)}, u32[]{:S(2)}) collective-permute-start(bf16[16,160,128]{2,1,0:T(8,128)(2,1)} %get-tuple-element.68), channel_id=1, source_target_pairs={{0,1},{1,0},{2,3},{3,2},{4,5},{5,4},{6,7},{7,6},{8,9},{9,8},{10,11... | collective-permute-start | bytes 1966088 | tf_op jit(solution)/shard_map/ppermute | solution.py:641
  299.6 17.5 %collective-permute-start.43 = (bf16[4,10,32,128]{3,2,1,0:T(8,128)(2,1)}, bf16[4,10,32,128]{3,2,1,0:T(8,128)(2,1)}, u32[]{:S(2)}, u32[]{:S(2)}) collective-permute-start(bf16[4,10,32,128]{3,2,1,0:T(8,128)(2,1)} %add_convert_fusion.5), channel_id=1, source_target_pairs={{0,8},{4,12},{8,0},{12,4},{16,24},{20,28},{24,16},{28,20},{1,9},{5... | collective-permute-start | bytes 983048 | tf_op jit(solution)/shard_map/ppermute | solution.py:641
  308.2 70.4 %collective-permute-start.23 = (bf16[16,240,128]{2,1,0:T(8,128)(2,1)}, bf16[16,240,128]{2,1,0:T(8,128)(2,1)S(1)}, u32[]{:S(2)}, u32[]{:S(2)}) collective-permute-start(bf16[16,240,128]{2,1,0:T(8,128)(2,1)} %get-tuple-element.64), channel_id=1, source_target_pairs={{0,1},{1,0},{2,3},{3,2},{4,5},{5,4},{6,7},{7,6},{8,9},{9,8},{10,11... | collective-permute-start | bytes 2949128 | tf_op jit(solution)/shard_map/ppermute | solution.py:641
  318.4 50.7 %collective-permute-start.44 = (bf16[2,10,32,128]{3,2,1,0:T(8,128)(2,1)S(1)}, bf16[2,10,32,128]{3,2,1,0:T(8,128)(2,1)S(1)}, u32[]{:S(2)}, u32[]{:S(2)}) collective-permute-start(bf16[2,10,32,128]{3,2,1,0:T(8,128)(2,1)S(1)} %add_convert_fusion.10), channel_id=1, source_target_pairs={{0,2},{1,3},{2,0},{3,1},{4,6},{5,7},{6,4},{7,5},{8,10},{9,11},{10,... | collective-permute-start | bytes 491528 | tf_op jit(solution)/shard_map/ppermute | solution.py:641
  318.4 60.4 %collective-permute-start.28 = (bf16[16,240,128]{2,1,0:T(8,128)(2,1)}, bf16[16,240,128]{2,1,0:T(8,128)(2,1)S(1)}, u32[]{:S(2)}, u32[]{:S(2)}) collective-permute-start(bf16[16,240,128]{2,1,0:T(8,128)(2,1)} %get-tuple-element.66), channel_id=1, source_target_pairs={{0,1},{1,0},{2,3},{3,2},{4,5},{5,4},{6,7},{7,6},{8,9},{9,8},{10,11... | collective-permute-start | bytes 2949128 | tf_op jit(solution)/shard_map/ppermute | solution.py:641
  319.7 54.8 %collective-permute-start.34 = (bf16[8,160,128]{2,1,0:T(8,128)(2,1)S(1)}, bf16[8,160,128]{2,1,0:T(8,128)(2,1)S(1)}, u32[]{:S(2)}, u32[]{:S(2)}) collective-permute-start(bf16[8,160,128]{2,1,0:T(8,128)(2,1)S(1)} %add_convert_fusion.7), channel_id=1, source_target_pairs={{0,8},{4,12},{8,0},{12,4},{16,24},{20,28},{24,16},{28,20},{1,9},{5... | collective-permute-start | bytes 983048 | tf_op jit(solution)/shard_map/ppermute | solution.py:641
  324.0 124.5 %collective-permute-start.41 = (bf16[1,10,32,128]{3,2,1,0:T(8,128)(2,1)}, bf16[1,10,32,128]{3,2,1,0:T(8,128)(2,1)S(1)}, u32[]{:S(2)}, u32[]{:S(2)}) collective-permute-start(bf16[1,10,32,128]{3,2,1,0:T(8,128)(2,1)} %get-tuple-element.116), channel_id=1, source_target_pairs={{0,16},{4,20},{8,24},{12,28},{16,0},{20,4},{24,8},{28,12},{1,17},{... | collective-permute-start | bytes 245768 | tf_op jit(solution)/shard_map/ppermute | solution.py:641
  371.0 77.5 %collective-permute-start.45 = (bf16[1,10,32,128]{3,2,1,0:T(8,128)(2,1)}, bf16[1,10,32,128]{3,2,1,0:T(8,128)(2,1)}, u32[]{:S(2)}, u32[]{:S(2)}) collective-permute-start(bf16[1,10,32,128]{3,2,1,0:T(8,128)(2,1)} %get-tuple-element.114), channel_id=1, source_target_pairs={{0,16},{4,20},{8,24},{12,28},{16,0},{20,4},{24,8},{28,12},{1,17},{... | collective-permute-start | bytes 245768 | tf_op jit(solution)/shard_map/ppermute | solution.py:641
  375.5 32.0 %collective-permute-start.35 = (bf16[4,160,128]{2,1,0:T(8,128)(2,1)S(1)}, bf16[4,160,128]{2,1,0:T(8,128)(2,1)S(1)}, u32[]{:S(2)}, u32[]{:S(2)}) collective-permute-start(bf16[4,160,128]{2,1,0:T(8,128)(2,1)S(1)} %add_convert_fusion.12), channel_id=1, source_target_pairs={{0,2},{1,3},{2,0},{3,1},{4,6},{5,7},{6,4},{7,5},{8,10},{9,11},{10,... | collective-permute-start | bytes 491528 | tf_op jit(solution)/shard_map/ppermute | solution.py:641
  378.7 34.4 %collective-permute-start.24 = (bf16[8,240,128]{2,1,0:T(8,128)(2,1)S(1)}, bf16[8,240,128]{2,1,0:T(8,128)(2,1)S(1)}, u32[]{:S(2)}, u32[]{:S(2)}) collective-permute-start(bf16[8,240,128]{2,1,0:T(8,128)(2,1)S(1)} %add_convert_fusion.3), channel_id=1, source_target_pairs={{0,2},{1,3},{2,0},{3,1},{4,6},{5,7},{6,4},{7,5},{8,10},{9,11},{10,... | collective-permute-start | bytes 1474568 | tf_op jit(solution)/shard_map/ppermute | solution.py:641
  379.0 41.5 %collective-permute-start.29 = (bf16[8,240,128]{2,1,0:T(8,128)(2,1)S(1)}, bf16[8,240,128]{2,1,0:T(8,128)(2,1)S(1)}, u32[]{:S(2)}, u32[]{:S(2)}) collective-permute-start(bf16[8,240,128]{2,1,0:T(8,128)(2,1)S(1)} %add_convert_fusion.2), channel_id=1, source_target_pairs={{0,4},{4,0},{8,12},{12,8},{16,20},{20,16},{24,28},{28,24},{1,5},{5... | collective-permute-start | bytes 1474568 | tf_op jit(solution)/shard_map/ppermute | solution.py:641
  422.1 19.9 %collective-permute-start.37 = (bf16[1,160,128]{2,1,0:T(8,128)(2,1)}, bf16[1,160,128]{2,1,0:T(8,128)(2,1)}, u32[]{:S(2)}, u32[]{:S(2)}) collective-permute-start(bf16[1,160,128]{2,1,0:T(8,128)(2,1)} %get-tuple-element.126), channel_id=1, source_target_pairs={{0,16},{4,20},{8,24},{12,28},{16,0},{20,4},{24,8},{28,12},{1,17},{... | collective-permute-start | bytes 122888 | tf_op jit(solution)/shard_map/ppermute | solution.py:641
  (77 other events, 852.0 us)
Sparse Core Ops, SparseCore 0:
  11.5 135.4 all-gather.1
  191.2 209.5 reduce-scatter.1
